TPU v7x, 32 devices: a whole 2x2x4 slice. The times are simulated.
32 devices in a mesh: tm: 4 (over z), grid: 8 (over y, x, core).
Axes of the slice: x: 2, y: 2, z: 4, core: 2. Of those that a mesh axis runs over, the one named last changes fastest.
Arguments:
- starts: float32 [4, 3, 1024, 1024], P('tm', None, 'grid'), may hold values from -1.6 to 1.6
- coriolis: float32 [1024], P('grid'), may hold values from 100 to 800
Outputs:
- ends: float32 [4, 3, 1024, 1024], P('tm', None, 'grid')
All inputs are finite; a program needn't handle non-finite values.
Results may differ from a plain program's by a relative error of at most 0.0003.
Values sent between devices are 32-bit elements; how exact they have to be, the bound alone decides.
No kernel may reach another device: no remote copies, remote signals or barrier semaphores. Data moves between devices by JAX's collectives and lax.ppermute only.
A program may use at most 128 MiB of HBM per device.

v0:
```python
import math

import jax
import jax.numpy as jnp
from jax import lax
from jax.sharding import PartitionSpec as P

SWEEPS = 2


STEP_LENGTH = 0.001
GRAVITY = 1.0
WEIGHTS_FIRST = (5.0 / 24.0, 8.0 / 24.0, -1.0 / 24.0)
WEIGHTS_SECOND = (-1.0 / 24.0, 8.0 / 24.0, 5.0 / 24.0)
HIGHEST = lax.Precision.HIGHEST


def shifted(array, axis, by):
    size = lax.axis_size(axis)
    pairs = [(i, i + by) for i in range(size) if 0 <= i + by < size]
    return lax.ppermute(array, axis, pairs)


def split_factor(length):
    best = 1
    for divisor in range(1, math.isqrt(length) + 1):
        if length % divisor == 0:
            best = divisor
    return best


def angle_table(first_count, second_count, period):
    first = jnp.arange(first_count, dtype=jnp.int32)[:, None]
    second = jnp.arange(second_count, dtype=jnp.int32)[None, :]
    turns = first * second % period
    theta = turns.astype(jnp.float32) * (2.0 * math.pi / period)
    return (jnp.cos(theta), jnp.sin(theta))


def make_tables(length):
    outer = split_factor(length)
    inner = length // outer
    cos_outer, sin_outer = angle_table(outer, outer, outer)
    cos_inner, sin_inner = angle_table(inner, inner, inner)
    cos_twist, sin_twist = angle_table(inner, outer, length)
    k_inner = jnp.arange(inner, dtype=jnp.int32)[:, None]
    k_outer = jnp.arange(outer, dtype=jnp.int32)[None, :]
    index_full = k_outer + outer * k_inner
    signed = jnp.where(index_full < length // 2, index_full, index_full - length)
    signed = jnp.where(index_full == length // 2, 0, signed)
    waves = signed.astype(jnp.float32) / length
    return (outer, inner, cos_outer, sin_outer, cos_inner, sin_inner, cos_twist, sin_twist, waves)


def mat(left, right):
    return jnp.dot(left, right, precision=HIGHEST, preferred_element_type=jnp.float32)


def along_last(values, tables):
    outer, inner, cos_outer, sin_outer, cos_inner, sin_inner, cos_twist, sin_twist, waves = tables
    length = values.shape[-1]
    flat = values.reshape(-1, length)
    batch = flat.shape[0]
    blocks = jnp.transpose(flat.reshape(batch, outer, inner), (1, 2, 0)).reshape(
        outer, inner * batch
    )
    real_a = mat(cos_outer, blocks).reshape(outer, inner, batch)
    imag_a = -mat(sin_outer, blocks).reshape(outer, inner, batch)
    twist_c = jnp.transpose(cos_twist)[:, :, None]
    twist_s = jnp.transpose(sin_twist)[:, :, None]
    real_b = real_a * twist_c + imag_a * twist_s
    imag_b = imag_a * twist_c - real_a * twist_s
    real_b = jnp.transpose(real_b, (1, 0, 2)).reshape(inner, outer * batch)
    imag_b = jnp.transpose(imag_b, (1, 0, 2)).reshape(inner, outer * batch)
    real_c = mat(cos_inner, real_b) + mat(sin_inner, imag_b)
    imag_c = mat(cos_inner, imag_b) - mat(sin_inner, real_b)
    wave_cols = jnp.broadcast_to(waves[:, :, None], (inner, outer, batch)).reshape(
        inner, outer * batch
    )
    real_d = -wave_cols * imag_c
    imag_d = wave_cols * real_c
    real_e = (mat(cos_inner, real_d) - mat(sin_inner, imag_d)).reshape(inner, outer, batch)
    imag_e = (mat(cos_inner, imag_d) + mat(sin_inner, real_d)).reshape(inner, outer, batch)
    back_c = cos_twist[:, :, None]
    back_s = sin_twist[:, :, None]
    real_f = real_e * back_c - imag_e * back_s
    imag_f = imag_e * back_c + real_e * back_s
    real_f = jnp.transpose(real_f, (1, 0, 2)).reshape(outer, inner * batch)
    imag_f = jnp.transpose(imag_f, (1, 0, 2)).reshape(outer, inner * batch)
    result = (mat(cos_outer, real_f) - mat(sin_outer, imag_f)).reshape(outer, inner, batch)
    return jnp.transpose(result, (2, 0, 1)).reshape(values.shape)


def assemble(state_now, grad_x, grad_y, coriolis_rows):
    height, east_vel, north_vel = (state_now[0], state_now[1], state_now[2])
    height_x, east_x, north_x = (grad_x[0], grad_x[1], grad_x[2])
    height_y, east_y, north_y = (grad_y[0], grad_y[1], grad_y[2])
    turning = coriolis_rows[:, None]
    rate_height = -(east_vel * height_x + north_vel * height_y) - (1.0 + height) * (
        east_x + north_y
    )
    rate_east = -(east_vel * east_x + north_vel * east_y) + turning * north_vel - GRAVITY * height_x
    rate_north = (
        -(east_vel * north_x + north_vel * north_y) - turning * east_vel - GRAVITY * height_y
    )
    return jnp.stack([rate_height, rate_east, rate_north])


def tendency_from(state_now, coriolis_rows, tables):
    grad_x = along_last(state_now, tables)
    moved = lax.all_to_all(
        jnp.transpose(state_now, (0, 2, 1)), "grid", split_axis=1, concat_axis=2, tiled=True
    )
    along_col = along_last(moved, tables)
    returned = lax.all_to_all(along_col, "grid", split_axis=2, concat_axis=1, tiled=True)
    grad_y = jnp.transpose(returned, (0, 2, 1))
    return assemble(state_now, grad_x, grad_y, coriolis_rows)


def quadrature(weights, rates):
    return weights[0] * rates[0] + weights[1] * rates[1] + weights[2] * rates[2]


def per_device(starts, coriolis):
    time_index = lax.axis_index("tm")
    first_state = starts[0]
    tables = make_tables(first_state.shape[2])
    rate_first = tendency_from(first_state, coriolis, tables)
    old_nodes = (first_state, first_state, first_state)
    old_rates = (rate_first, rate_first, rate_first)
    for sweep_index in range(SWEEPS):
        got_state, got_rate = shifted((old_nodes[2], old_rates[2]), "tm", 1)
        node_zero = jnp.where(time_index == 0, first_state, got_state)
        rate_zero = jnp.where(time_index == 0, rate_first, got_rate)
        node_one = (
            node_zero
            + 0.5 * STEP_LENGTH * (rate_zero - old_rates[0])
            + STEP_LENGTH * quadrature(WEIGHTS_FIRST, old_rates)
        )
        rate_one = tendency_from(node_one, coriolis, tables)
        node_two = (
            node_one
            + 0.5 * STEP_LENGTH * (rate_one - old_rates[1])
            + STEP_LENGTH * quadrature(WEIGHTS_SECOND, old_rates)
        )
        if sweep_index + 1 < SWEEPS:
            rate_two = tendency_from(node_two, coriolis, tables)
        else:
            rate_two = old_rates[2]
        old_nodes = (node_zero, node_one, node_two)
        old_rates = (rate_zero, rate_one, rate_two)
    return old_nodes[2][None]


def solution(mesh):
    return jax.shard_map(
        per_device,
        mesh=mesh,
        in_specs=(P("tm", None, "grid", None), P("grid")),
        out_specs=P("tm", None, "grid", None),
        check_vma=False,
    )
```

profile of v0, /device:TPU:9, one launch (start us, length us, event | category | flops | bytes accessed | tf_op | source)
XLA Modules:
  0.0 553.2 jit_solution(3439289250706120958)
XLA Ops:
  2.8 5.0 all-to-all-start
  20.6 10.4 %all-to-all-done = f32[3,1024,128]{2,0,1:T(4,128)} async-done(((f32[3,1024,128]{2,0,1:T(4,128)}), f32[3,1024,128]{2,0,1:T(4,128)}, u32[]{:S(2)}, u32[]{:S(2)}) %all-to-all-start) | async-done | bytes 1572896 | tf_op jit(solution)/shard_map/all_to_all | solution.py:111
  31.0 3.9 copy.77
  82.0 7.9 %all-to-all-start.1 = ((f32[3,128,1024]{1,0,2:T(4,128)}), f32[3,128,1024]{1,0,2:T(4,128)}, u32[]{:S(2)}, u32[]{:S(2)}) async-start(f32[3,128,1024]{1,0,2:T(4,128)} %reshape.572), calls=%async_computation.1 | async-start | bytes 4194304 | tf_op jit(solution)/shard_map/all_to_all | solution.py:115
  101.5 11.5 %all-to-all-done.1 = f32[3,128,1024]{1,0,2:T(4,128)} async-done(((f32[3,128,1024]{1,0,2:T(4,128)}), f32[3,128,1024]{1,0,2:T(4,128)}, u32[]{:S(2)}, u32[]{:S(2)}) %all-to-all-start.1) | async-done | bytes 1572896 | tf_op jit(solution)/shard_map/all_to_all | solution.py:115
  129.6 32.5 %collective-permute-done.1 = f32[3,128,1024]{1,2,0:T(8,128)} collective-permute-done((f32[3,128,1024]{1,2,0:T(8,128)}, f32[3,128,1024]{1,2,0:T(8,128)}, u32[]{:S(2)}, u32[]{:S(2)}) %collective-permute-start.1) | collective-permute-done | bytes 1572896 | tf_op jit(solution)/shard_map/ppermute | solution.py:21
  167.9 6.4 %all-to-all-start.2 = ((f32[3,1024,128]{2,0,1:T(4,128)}), f32[3,1024,128]{2,0,1:T(4,128)}, u32[]{:S(2)}, u32[]{:S(2)}) async-start(f32[3,1024,128]{2,0,1:T(4,128)} %copy.90), calls=%async_computation.2 | async-start | bytes 4194304 | tf_op jit(solution)/shard_map/all_to_all | solution.py:111
  180.5 4.8 fusion.52
  185.3 12.1 %all-to-all-done.2 = f32[3,1024,128]{2,0,1:T(4,128)} async-done(((f32[3,1024,128]{2,0,1:T(4,128)}), f32[3,1024,128]{2,0,1:T(4,128)}, u32[]{:S(2)}, u32[]{:S(2)}) %all-to-all-start.2) | async-done | bytes 1572896 | tf_op jit(solution)/shard_map/all_to_all | solution.py:111
  197.4 3.9 copy.91
  201.3 3.9 reshape_reshape.23
  205.2 3.8 fusion.93
  228.8 4.4 fusion.25
  241.5 8.0 %all-to-all-start.3 = ((f32[3,128,1024]{1,0,2:T(4,128)}), f32[3,128,1024]{1,0,2:T(4,128)}, u32[]{:S(2)}, u32[]{:S(2)}) async-start(f32[3,128,1024]{1,0,2:T(4,128)} %reshape.589), calls=%async_computation.3 | async-start | bytes 4194304 | tf_op jit(solution)/shard_map/all_to_all | solution.py:115
  284.3 7.9 %all-to-all-start.4 = ((f32[3,1024,128]{2,0,1:T(4,128)}), f32[3,1024,128]{2,0,1:T(4,128)}, u32[]{:S(2)}, u32[]{:S(2)}) async-start(f32[3,1024,128]{2,0,1:T(4,128)} %copy.103), calls=%async_computation.4 | async-start | bytes 4194304 | tf_op jit(solution)/shard_map/all_to_all | solution.py:111
  295.6 3.8 copy.98
  308.9 6.4 %all-to-all-done.4 = f32[3,1024,128]{2,0,1:T(4,128)} async-done(((f32[3,1024,128]{2,0,1:T(4,128)}), f32[3,1024,128]{2,0,1:T(4,128)}, u32[]{:S(2)}, u32[]{:S(2)}) %all-to-all-start.4) | async-done | bytes 1572896 | tf_op jit(solution)/shard_map/all_to_all | solution.py:111
  315.3 3.9 copy.104
  319.1 3.9 reshape_reshape.25
  323.1 3.8 fusion.99
  346.2 4.4 fusion.21
  355.9 8.2 %all-to-all-start.5 = ((f32[3,128,1024]{1,0,2:T(4,128)}), f32[3,128,1024]{1,0,2:T(4,128)}, u32[]{:S(2)}, u32[]{:S(2)}) async-start(f32[3,128,1024]{1,0,2:T(4,128)} %reshape.606), calls=%async_computation.5 | async-start | bytes 4194304 | tf_op jit(solution)/shard_map/all_to_all | solution.py:115
  396.8 30.9 %collective-permute-done.3 = f32[3,128,1024]{1,2,0:T(8,128)S(1)} collective-permute-done((f32[3,128,1024]{1,2,0:T(8,128)S(1)}, f32[3,128,1024]{1,2,0:T(8,128)S(1)}, u32[]{:S(2)}, u32[]{:S(2)}) %collective-permute-start.3) | collective-permute-done | bytes 1572896 | tf_op jit(solution)/shard_map/ppermute | solution.py:21
  432.9 9.5 %all-to-all-start.6 = ((f32[3,1024,128]{2,0,1:T(4,128)}), f32[3,1024,128]{2,0,1:T(4,128)}, u32[]{:S(2)}, u32[]{:S(2)}) async-start(f32[3,1024,128]{2,0,1:T(4,128)} %copy.116), calls=%async_computation.6 | async-start | bytes 4194304 | tf_op jit(solution)/shard_map/all_to_all | solution.py:111
  444.9 3.8 reshape_reshape.26
  448.7 4.8 fusion.36
  453.5 12.1 %all-to-all-done.6 = f32[3,1024,128]{2,0,1:T(4,128)} async-done(((f32[3,1024,128]{2,0,1:T(4,128)}), f32[3,1024,128]{2,0,1:T(4,128)}, u32[]{:S(2)}, u32[]{:S(2)}) %all-to-all-start.6) | async-done | bytes 1572896 | tf_op jit(solution)/shard_map/all_to_all | solution.py:111
  465.6 3.9 copy.117
  469.5 3.9 reshape_reshape.27
  473.4 3.8 fusion.105
  497.0 4.4 fusion.17
  509.7 7.9 %all-to-all-start.7 = ((f32[3,128,1024]{1,0,2:T(4,128)}), f32[3,128,1024]{1,0,2:T(4,128)}, u32[]{:S(2)}, u32[]{:S(2)}) async-start(f32[3,128,1024]{1,0,2:T(4,128)} %reshape.623), calls=%async_computation.7 | async-start | bytes 4194304 | tf_op jit(solution)/shard_map/all_to_all | solution.py:115
  (294 shorter events, 305.5 us)
Async XLA Ops:
  2.8 5.0 copy-start.14
  2.8 28.2 %all-to-all-start = ((f32[3,1024,128]{2,0,1:T(4,128)}), f32[3,1024,128]{2,0,1:T(4,128)}, u32[]{:S(2)}, u32[]{:S(2)}) async-start(f32[3,1024,128]{2,0,1:T(4,128)} %copy.76), calls=%async_computation | async-start | bytes 4194304 | tf_op jit(solution)/shard_map/all_to_all | solution.py:111
  82.0 31.0 %all-to-all-start.1 = ((f32[3,128,1024]{1,0,2:T(4,128)}), f32[3,128,1024]{1,0,2:T(4,128)}, u32[]{:S(2)}, u32[]{:S(2)}) async-start(f32[3,128,1024]{1,0,2:T(4,128)} %reshape.572), calls=%async_computation.1 | async-start | bytes 4194304 | tf_op jit(solution)/shard_map/all_to_all | solution.py:115
  91.7 27.2 %copy-start.12 = (f32[1,3,128,1024]{2,3,1,0:T(8,128)}, f32[1,3,128,1024]{2,3,1,0:T(8,128)S(1)}, u32[]{:S(2)}) copy-start(f32[1,3,128,1024]{2,3,1,0:T(8,128)S(1)} %copy.68) | copy-start | bytes 4718596
  91.7 37.9 %collective-permute-start = (f32[3,128,1024]{1,2,0:T(8,128)S(1)}, f32[3,128,1024]{1,2,0:T(8,128)}, u32[]{:S(2)}, u32[]{:S(2)}) collective-permute-start(f32[3,128,1024]{1,2,0:T(8,128)S(1)} %bitcast.851), channel_id=1, source_target_pairs={{0,8},{8,16},{16,24},{1,9},{9,17},{17,25},{2,10},{10,18},{18,26},{... | collective-permute-start | bytes 4718600 | tf_op jit(solution)/shard_map/ppermute | solution.py:21
  115.8 3.1 copy-start.45
  122.8 39.3 %collective-permute-start.1 = (f32[3,128,1024]{1,2,0:T(8,128)}, f32[3,128,1024]{1,2,0:T(8,128)}, u32[]{:S(2)}, u32[]{:S(2)}) collective-permute-start(f32[3,128,1024]{1,2,0:T(8,128)} %pad_maximum_fusion), channel_id=1, source_target_pairs={{0,8},{8,16},{16,24},{1,9},{9,17},{17,25},{2,10},{10,18},{18,26},{... | collective-permute-start | bytes 4718600 | tf_op jit(solution)/shard_map/ppermute | solution.py:21
  167.9 29.5 %all-to-all-start.2 = ((f32[3,1024,128]{2,0,1:T(4,128)}), f32[3,1024,128]{2,0,1:T(4,128)}, u32[]{:S(2)}, u32[]{:S(2)}) async-start(f32[3,1024,128]{2,0,1:T(4,128)} %copy.90), calls=%async_computation.2 | async-start | bytes 4194304 | tf_op jit(solution)/shard_map/all_to_all | solution.py:111
  205.2 3.8 copy-start.17
  241.5 31.0 %all-to-all-start.3 = ((f32[3,128,1024]{1,0,2:T(4,128)}), f32[3,128,1024]{1,0,2:T(4,128)}, u32[]{:S(2)}, u32[]{:S(2)}) async-start(f32[3,128,1024]{1,0,2:T(4,128)} %reshape.589), calls=%async_computation.3 | async-start | bytes 4194304 | tf_op jit(solution)/shard_map/all_to_all | solution.py:115
  284.3 31.0 %all-to-all-start.4 = ((f32[3,1024,128]{2,0,1:T(4,128)}), f32[3,1024,128]{2,0,1:T(4,128)}, u32[]{:S(2)}, u32[]{:S(2)}) async-start(f32[3,1024,128]{2,0,1:T(4,128)} %copy.103), calls=%async_computation.4 | async-start | bytes 4194304 | tf_op jit(solution)/shard_map/all_to_all | solution.py:111
  299.5 97.3 %collective-permute-start.2 = (f32[3,128,1024]{1,2,0:T(8,128)}, f32[3,128,1024]{1,2,0:T(8,128)}, u32[]{:S(2)}, u32[]{:S(2)}) collective-permute-start(f32[3,128,1024]{1,2,0:T(8,128)} %multiply_add_fusion.1), channel_id=1, source_target_pairs={{0,8},{8,16},{16,24},{1,9},{9,17},{17,25},{2,10},{10,18},{18,26},{... | collective-permute-start | bytes 4718600 | tf_op jit(solution)/shard_map/ppermute | solution.py:21
  323.1 3.8 copy-start.18
  355.9 8.2 %copy-start.42 = (f32[32,32,384]{2,1,0:T(8,128)S(1)}, f32[32,32,384]{2,1,0:T(8,128)}, u32[]{:S(2)}) copy-start(f32[32,32,384]{2,1,0:T(8,128)} %get-tuple-element.64) | copy-start | bytes 4718596
  355.9 31.1 %all-to-all-start.5 = ((f32[3,128,1024]{1,0,2:T(4,128)}), f32[3,128,1024]{1,0,2:T(4,128)}, u32[]{:S(2)}, u32[]{:S(2)}) async-start(f32[3,128,1024]{1,0,2:T(4,128)} %reshape.606), calls=%async_computation.5 | async-start | bytes 4194304 | tf_op jit(solution)/shard_map/all_to_all | solution.py:115
  390.3 37.4 %copy-start.21 = (f32[1,128,1024]{1,2,0:T(8,128)S(1)}, f32[1,128,1024]{1,2,0:T(8,128)}, u32[]{:S(2)}) copy-start(f32[1,128,1024]{1,2,0:T(8,128)} %copy-done.20) | copy-start | bytes 1572868
  390.3 37.4 %copy-start.24 = (f32[1,128,1024]{1,2,0:T(8,128)S(1)}, f32[1,128,1024]{1,2,0:T(8,128)}, u32[]{:S(2)}) copy-start(f32[1,128,1024]{1,2,0:T(8,128)} %copy-done.23) | copy-start | bytes 1572868
  390.3 37.4 %copy-start.27 = (f32[1,128,1024]{1,2,0:T(8,128)S(1)}, f32[1,128,1024]{1,2,0:T(8,128)}, u32[]{:S(2)}) copy-start(f32[1,128,1024]{1,2,0:T(8,128)} %copy-done.26) | copy-start | bytes 1572868
  393.1 34.6 %copy-start.29 = (f32[1,128,1024]{1,2,0:T(8,128)}, f32[1,128,1024]{1,2,0:T(8,128)S(1)}, u32[]{:S(2)}) copy-start(f32[1,128,1024]{1,2,0:T(8,128)S(1)} %get-tuple-element.7) | copy-start | bytes 1572868
  393.1 34.6 %copy-start.31 = (f32[1,128,1024]{1,2,0:T(8,128)}, f32[1,128,1024]{1,2,0:T(8,128)S(1)}, u32[]{:S(2)}) copy-start(f32[1,128,1024]{1,2,0:T(8,128)S(1)} %get-tuple-element.8) | copy-start | bytes 1572868
  393.1 34.6 %copy-start.33 = (f32[1,128,1024]{1,2,0:T(8,128)}, f32[1,128,1024]{1,2,0:T(8,128)S(1)}, u32[]{:S(2)}) copy-start(f32[1,128,1024]{1,2,0:T(8,128)S(1)} %get-tuple-element.47) | copy-start | bytes 1572868
  393.1 34.6 %copy-start.2 = (f32[1,128,1024]{1,2,0:T(8,128)S(1)}, f32[1,128,1024]{1,2,0:T(8,128)}, u32[]{:S(2)}) copy-start(f32[1,128,1024]{1,2,0:T(8,128)} %copy-done) | copy-start | bytes 1572868
  393.1 34.6 %copy-start.6 = (f32[1,128,1024]{1,2,0:T(8,128)S(1)}, f32[1,128,1024]{1,2,0:T(8,128)}, u32[]{:S(2)}) copy-start(f32[1,128,1024]{1,2,0:T(8,128)} %copy-done.4) | copy-start | bytes 1572868
  393.2 34.6 %copy-start.10 = (f32[1,128,1024]{1,2,0:T(8,128)S(1)}, f32[1,128,1024]{1,2,0:T(8,128)}, u32[]{:S(2)}) copy-start(f32[1,128,1024]{1,2,0:T(8,128)} %copy-done.8) | copy-start | bytes 1572868
  393.2 34.6 %copy-start.13 = (f32[1,3,128,1024]{2,3,1,0:T(8,128)S(1)}, f32[1,3,128,1024]{2,3,1,0:T(8,128)}, u32[]{:S(2)}) copy-start(f32[1,3,128,1024]{2,3,1,0:T(8,128)} %copy-done.12) | copy-start | bytes 4718596
  393.3 34.4 %collective-permute-start.3 = (f32[3,128,1024]{1,2,0:T(8,128)S(1)}, f32[3,128,1024]{1,2,0:T(8,128)S(1)}, u32[]{:S(2)}, u32[]{:S(2)}) collective-permute-start(f32[3,128,1024]{1,2,0:T(8,128)S(1)} %pad_maximum_fusion.2), channel_id=1, source_target_pairs={{0,8},{8,16},{16,24},{1,9},{9,17},{17,25},{2,10},{10,18},{18,26},{... | collective-permute-start | bytes 4718600 | tf_op jit(solution)/shard_map/ppermute | solution.py:21
  432.9 32.7 %all-to-all-start.6 = ((f32[3,1024,128]{2,0,1:T(4,128)}), f32[3,1024,128]{2,0,1:T(4,128)}, u32[]{:S(2)}, u32[]{:S(2)}) async-start(f32[3,1024,128]{2,0,1:T(4,128)} %copy.116), calls=%async_computation.6 | async-start | bytes 4194304 | tf_op jit(solution)/shard_map/all_to_all | solution.py:111
  473.4 3.8 copy-start.19
  509.7 30.9 %all-to-all-start.7 = ((f32[3,128,1024]{1,0,2:T(4,128)}), f32[3,128,1024]{1,0,2:T(4,128)}, u32[]{:S(2)}, u32[]{:S(2)}) async-start(f32[3,128,1024]{1,0,2:T(4,128)} %reshape.623), calls=%async_computation.7 | async-start | bytes 4194304 | tf_op jit(solution)/shard_map/all_to_all | solution.py:115
  544.0 2.9 copy-start.30
  544.0 3.1 copy-start.32
  544.0 3.2 copy-start.34
  (26 other events, 48.8 us)
where the time goes:
time: 564 us; the launch traced here: 553 us
  matrix products  186 us (33%)
  local copies, waits for them, and re-layouts  140 us (25%)
  waiting for transfers between devices  123 us (22%)
  starting transfers between devices  73.8 us (13%)
  other arithmetic  28.3 us (5%)
    dot_general x96, matrix products, mat(): jnp.dot(left, right, precision=HIGHEST, preferred_element_type=jnp.float32)  186 us
    ppermute x4, waiting for transfers between devices, shifted(): return lax.ppermute(array, axis, pairs)  67 us
    all_to_all x4, waiting for transfers between devices, tendency_from(): lax.all_to_all(jnp.transpose(state_now, (0, 2, 1)), 'grid', split_axis=1,...  41 us
    unnamed x135, local copies, waits for them, and re-layouts  37.4 us
    all_to_all x4, starting transfers between devices, tendency_from(): lax.all_to_all(along_col, 'grid', split_axis=2, concat_axis=1, tiled=True)  32 us
    all_to_all x4, starting transfers between devices, tendency_from(): lax.all_to_all(jnp.transpose(state_now, (0, 2, 1)), 'grid', split_axis=1,...  28.8 us
    another operation x8, local copies, waits for them, and re-layouts, along_last(): flat.reshape(batch, outer, inner)  27.8 us
    all_to_all x8, local copies, waits for them, and re-layouts, tendency_from(): lax.all_to_all(along_col, 'grid', split_axis=2, concat_axis=1, tiled=True)  18.4 us
  transfers between devices with their start and end apart: 12, of which 11 were waited for; matrix products, arithmetic and copies ran while one was open for 32% of the time, Pallas kernels for 0%

commit v1 on v0

v1 whole, which is shorter than its diff:
```python
import functools
import math

import jax
import jax.numpy as jnp
import ml_dtypes
import numpy as np
from jax import lax
from jax.experimental import pallas as pl
from jax.experimental.pallas import tpu as pltpu
from jax.sharding import PartitionSpec as P

SWEEPS = 2
STEP_LENGTH = 0.001
HALF_STEP = 0.5 * STEP_LENGTH
GRAVITY = 1.0
CORRECT_FIRST = (5.0 / 24.0 - 0.5, 8.0 / 24.0, -1.0 / 24.0)
CORRECT_SECOND = (-1.0 / 24.0, 8.0 / 24.0 - 0.5, 5.0 / 24.0)
TOLERANCE = 1e-8
TILE = 256
ROWS = 16
F32 = jnp.float32
BF16 = jnp.bfloat16


def kernel_values(length):
    values = np.zeros(length)
    for j in range(1, length):
        values[j] = (0.5 if j % 2 == 0 else -0.5) / math.tan(math.pi * j / length)
    values[length // 2] = 0.0
    return values


def toeplitz(values, rows, cols, offset):
    index = np.arange(rows)[:, None] - np.arange(cols)[None, :] + offset
    return values[index % len(values)]


def cross_factors(block, tolerance):
    rest = block.copy()
    lefts, rights = [], []
    while True:
        at = int(np.argmax(np.abs(rest)))
        i, j = divmod(at, rest.shape[1])
        pivot = rest[i, j]
        small = abs(pivot) <= tolerance
        if (small and lefts and len(lefts) % 8 == 0) or len(lefts) == block.shape[0]:
            break
        if abs(pivot) == 0.0:
            left, right = np.zeros(rest.shape[0]), np.zeros(rest.shape[1])
        else:
            left, right = rest[:, j] / pivot, rest[i, :].copy()
        lefts.append(left)
        rights.append(right)
        rest = rest - left[:, None] * right[None, :]
    return np.stack(lefts, axis=1), np.stack(rights, axis=0)


def two_parts(table):
    high = table.astype(ml_dtypes.bfloat16)
    low = (table - high.astype(np.float64)).astype(ml_dtypes.bfloat16)
    return high, low


def pad_rows(table, multiple):
    extra = -table.shape[0] % multiple
    return np.pad(table, ((0, extra), (0, 0)))


def x_tables(length):
    values = kernel_values(length)
    half = length // 2
    near = toeplitz(values, half, half, 0).T
    far = toeplitz(values, half, half, half).T
    plus = two_parts(0.5 * (near + far))
    minus = two_parts(0.5 * (near - far))
    return np.stack([plus[0], plus[1], minus[0], minus[1]])


@functools.lru_cache(maxsize=None)
def y_tables(length, devices):
    rows = length // devices
    pair = 2 * rows
    pairs = devices // 2
    values = kernel_values(length)
    tolerance = TOLERANCE * float(np.max(np.abs(values)))
    factors = [cross_factors(toeplitz(values, pair, pair, d * pair), tolerance) for d in range(1, pairs)]
    ranks = tuple(f[0].shape[1] for f in factors)
    mates = [cross_factors(toeplitz(values, rows, rows, rows if k == 0 else -rows), tolerance) for k in range(2)]
    mate_rank = max(m[0].shape[1] for m in mates)
    send, apply = [], []
    for k in range(2):
        span = slice(k * rows, (k + 1) * rows)
        to_mate = np.pad(mates[k][1], ((0, mate_rank - mates[k][1].shape[0]), (0, 0)))
        from_mate = np.pad(mates[1 - k][0], ((0, 0), (0, mate_rank - mates[1 - k][0].shape[1])))
        down = pad_rows(np.concatenate([f[1][:, span] for f in factors] + [to_mate], axis=0), 16)
        send.append(np.concatenate(two_parts(down), axis=0))
        own = pad_rows(toeplitz(values, rows, rows, 0).T, 16).T
        up = np.concatenate([own] + [f[0][span] for f in factors] + [from_mate], axis=1)
        up = pad_rows(up.T, 16).T
        apply.append(np.concatenate(two_parts(up), axis=0))
    return ranks, mate_rank, np.stack(send), np.stack(apply)


def parts_of(value):
    high = value.astype(BF16)
    return high, (value - high.astype(F32)).astype(BF16)


def dot(left, right):
    return jnp.dot(left, right, preferred_element_type=F32)


def product(stacked, high, low):
    count = stacked.shape[0] // 2
    both = dot(stacked, high)
    return both[:count] + both[count:] + dot(stacked[:count], low)


def x_kernel(state_ref, table_ref, out_ref):
    value = state_ref[...]
    half = value.shape[1] // 2
    left, right = value[:, :half], value[:, half:]

    def folded(total, at):
        high, low = parts_of(total)
        return dot(high, table_ref[at]) + dot(low, table_ref[at]) + dot(high, table_ref[at + 1])

    even = folded(left + right, 0)
    odd = folded(left - right, 2)
    out_ref[:, :half] = even + odd
    out_ref[:, half:] = even - odd


def along_x(state, table):
    fields, rows, length = state.shape
    out = pl.pallas_call(
        x_kernel,
        grid=(fields,),
        in_specs=[
            pl.BlockSpec((rows, length), lambda f: (f, 0)),
            pl.BlockSpec(table.shape, lambda f: (0, 0, 0)),
        ],
        out_specs=pl.BlockSpec((rows, length), lambda f: (f, 0)),
        out_shape=jax.ShapeDtypeStruct((fields * rows, length), F32),
        name="along_x",
    )(state.reshape(fields * rows, length), table)
    return out.reshape(state.shape)


class Plan:
    def __init__(self, rows, length, ranks, mate_rank):
        self.rows, self.length = rows, length
        self.ranks, self.mate_rank = ranks, mate_rank
        self.total = sum(ranks)
        self.half = length // 2
        self.per_half = self.half // TILE
        self.tiles = length // TILE
        self.state = jax.ShapeDtypeStruct((3, rows, length), F32)
        self.state_spec = pl.BlockSpec((3, rows, TILE), lambda t, flags: (0, 0, t))
        self.row_blocks = [(r, min(ROWS, rows - r)) for r in range(0, rows, ROWS)]

    def whole(self, shape):
        return pl.BlockSpec(shape, lambda t, flags: (0,) * len(shape))

    def moment_outs(self):
        half = jax.ShapeDtypeStruct((3, self.total, self.half), F32)
        mate = jax.ShapeDtypeStruct((3, self.mate_rank, self.length), F32)
        return (half, half, mate), (
            self.whole(half.shape),
            self.whole(half.shape),
            pl.BlockSpec((3, self.mate_rank, TILE), lambda t, flags: (0, 0, t)),
        )

    def emit_moments(self, flags_ref, next_ref, send_ref, mine_ref, theirs_ref, mate_ref):
        tile = pl.program_id(0)
        is_mine = tile // self.per_half == flags_ref[0]
        start = pl.multiple_of((tile % self.per_half) * TILE, TILE)
        for f in range(3):
            found = product(send_ref[...], *parts_of(next_ref[f]))
            mate_ref[f] = found[self.total : self.total + self.mate_rank]

            @pl.when(is_mine)
            def _():
                mine_ref[f, :, pl.ds(start, TILE)] = found[: self.total]

            @pl.when(jnp.logical_not(is_mine))
            def _():
                theirs_ref[f, :, pl.ds(start, TILE)] = found[: self.total]

    def y_gradient(self, f, flags_ref, state_ref, mine_refs, other_refs, mate_ref, apply_ref):
        tile = pl.program_id(0)
        is_mine = tile // self.per_half == flags_ref[0]
        start = pl.multiple_of((tile % self.per_half) * TILE, TILE)
        pieces = [state_ref[f]]
        if self.rows % 16:
            pieces.append(jnp.zeros((-self.rows % 16, TILE), F32))
        for a, b in zip(mine_refs, other_refs):
            here = a[f, :, pl.ds(start, TILE)]
            there = b[f, :, pl.ds(start, TILE)]
            pieces.append(jnp.where(is_mine, here, there))
        pieces.append(mate_ref[f])
        width = apply_ref.shape[1] - sum(p.shape[0] for p in pieces)
        if width:
            pieces.append(jnp.zeros((width, TILE), F32))
        return product(apply_ref[...], *parts_of(jnp.concatenate(pieces, axis=0)))


def tendency_rows(h, u, v, gx, gy, turning):
    rate_h = -(u * gx[0] + v * gy[0]) - (1.0 + h) * (gx[1] + gy[2])
    rate_u = -(u * gx[1] + v * gy[1]) + turning * v - GRAVITY * gx[0]
    rate_v = -(u * gx[2] + v * gy[2]) - turning * u - GRAVITY * gy[0]
    return rate_h, rate_u, rate_v


def select_call(plan, flags, received, own, added, send):
    extra = [] if added is None else [added]

    def body(flags_ref, received_ref, own_ref, *rest):
        added_ref = rest[0] if extra else None
        send_ref, next_ref, mine_ref, theirs_ref, mate_ref = rest[len(extra) :]
        first = flags_ref[1] == 0
        for f in range(3):
            value = jnp.where(first, own_ref[f], received_ref[f])
            next_ref[f] = value if added_ref is None else value + added_ref[f]
        plan.emit_moments(flags_ref, next_ref, send_ref, mine_ref, theirs_ref, mate_ref)

    shapes, specs = plan.moment_outs()
    return pl.pallas_call(
        body,
        grid_spec=pltpu.PrefetchScalarGridSpec(
            num_scalar_prefetch=1,
            grid=(plan.tiles,),
            in_specs=[plan.state_spec] * (2 + len(extra)) + [plan.whole(send.shape)],
            out_specs=[plan.state_spec, *specs],
        ),
        out_shape=[plan.state, *shapes],
        name="select_state",
    )(flags, received, own, *extra, send)


def stage_call(plan, flags, stage, state, grad_x, received, turning, apply, send, others):
    mine, other, mate = received
    count = len(mine)
    with_moments = stage in (1, 2)

    def body(flags_ref, state_ref, grad_ref, turning_ref, *rest):
        mine_refs, rest = rest[:count], rest[count:]
        other_refs, rest = rest[:count], rest[count:]
        mate_ref, apply_ref, rest = rest[0], rest[1], rest[2:]
        other_ins, rest = rest[: len(others)], rest[len(others) :]
        if with_moments:
            send_ref, rest = rest[0], rest[1:]
        grad_y = rest[-1]
        for f in range(3):
            grad_y[f] = plan.y_gradient(f, flags_ref, state_ref, mine_refs, other_refs, mate_ref, apply_ref)
        for start, size in plan.row_blocks:
            at = slice(start, start + size)
            now = [state_ref[f, at, :] for f in range(3)]
            rates = tendency_rows(
                *now,
                [grad_ref[f, at, :] for f in range(3)],
                [grad_y[f, at, :] for f in range(3)],
                turning_ref[at, :],
            )
            for f in range(3):
                ahead = now[f] + HALF_STEP * rates[f]
                if stage in (1, 2):
                    rest[0][f, at, :] = ahead
                    rest[1][f, at, :] = rates[f]
                elif stage == 3:
                    rest[0][f, at, :] = ahead
                    olds = (other_ins[0][f, at, :], other_ins[1][f, at, :], rates[f])
                    for out, weights in ((rest[1], CORRECT_FIRST), (rest[2], CORRECT_SECOND)):
                        out[f, at, :] = sum((STEP_LENGTH * w) * r for w, r in zip(weights, olds))
                else:
                    rest[0][f, at, :] = ahead + other_ins[0][f, at, :]
        if with_moments:
            plan.emit_moments(flags_ref, rest[0], send_ref, *rest[2:5])

    state_outs = {1: 2, 2: 2, 3: 3, 4: 1}[stage]
    shapes, specs = plan.moment_outs() if with_moments else ((), ())
    mate_spec = pl.BlockSpec((3, plan.mate_rank, TILE), lambda t, flags: (0, 0, t))
    return pl.pallas_call(
        body,
        grid_spec=pltpu.PrefetchScalarGridSpec(
            num_scalar_prefetch=1,
            grid=(plan.tiles,),
            in_specs=[plan.state_spec] * 2
            + [plan.whole(turning.shape)]
            + [plan.whole(a.shape) for a in (*mine, *other)]
            + [mate_spec, plan.whole(apply.shape)]
            + [plan.state_spec] * len(others)
            + ([plan.whole(send.shape)] if with_moments else []),
            out_specs=[plan.state_spec] * state_outs + list(specs),
            scratch_shapes=[pltpu.VMEM((3, plan.rows, TILE), F32)],
        ),
        out_shape=[plan.state] * state_outs + list(shapes),
        name=f"stage_{stage}",
    )(flags, state, grad_x, turning, *mine, *other, mate, apply, *others, *([send] if with_moments else []))


def ahead_in_time(array):
    size = lax.axis_size("tm")
    return lax.ppermute(array, "tm", [(i, i + 1) for i in range(size - 1)])


def mate_swap(array):
    size = lax.axis_size("grid")
    return lax.ppermute(array, "grid", [(i, i ^ 1) for i in range(size)])


def exchange(plan, mine, theirs, to_mate):
    size = lax.axis_size("grid")
    from_mate = mate_swap(to_mate)
    merged = mine + mate_swap(theirs)
    mine_in, other_in, start = [], [], 0
    for d, rank in enumerate(plan.ranks, 1):
        part = merged[:, start : start + rank]
        start += rank
        mine_in.append(lax.ppermute(part, "grid", [(i, (i + 2 * d) % size) for i in range(size)]))
    for part in mine_in:
        other_in.append(mate_swap(part))
    return mine_in, other_in, from_mate


def per_device(starts, coriolis):
    first_state = starts[0]
    _, rows, length = first_state.shape
    ranks, mate_rank, send_tables, apply_tables = y_tables(length, lax.axis_size("grid"))
    plan = Plan(rows, length, ranks, mate_rank)
    member = lax.axis_index("grid") % 2
    flags = jnp.stack([member, lax.axis_index("tm")]).astype(jnp.int32)
    table = jnp.asarray(x_tables(length))
    send = lax.dynamic_index_in_dim(jnp.asarray(send_tables), member, 0, keepdims=False)
    apply = lax.dynamic_index_in_dim(jnp.asarray(apply_tables), member, 0, keepdims=False)
    turning = coriolis[:, None]

    def stage(number, state, moments, others=()):
        received = exchange(plan, *moments)
        grad_x = along_x(state, table)
        return stage_call(plan, flags, number, state, grad_x, received, turning, apply, send, others)

    before = ahead_in_time(first_state)
    node_zero, *moments = select_call(plan, flags, before, first_state, None, send)
    node_one, rate_zero, *moments = stage(1, node_zero, moments)
    node_two, rate_one, *moments = stage(2, node_one, moments)
    lead, add_first, add_second = stage(3, node_two, moments, (rate_zero, rate_one))
    came = ahead_in_time(lead)
    node, *moments = select_call(plan, flags, came, node_one, add_first, send)
    (ends,) = stage(4, node, moments, (add_second,))
    return ends[None]


def solution(mesh):
    return jax.shard_map(
        per_device,
        mesh=mesh,
        in_specs=(P("tm", None, "grid", None), P("grid")),
        out_specs=P("tm", None, "grid", None),
        check_vma=False,
    )
```

time: 564 us -> 191 us (0.34); the launches traced: 553 us -> 190 us
  matrix products: 186 us -> 0 us
  local copies, waits for them, and re-layouts: 140 us -> 8.11 us
  Pallas kernels: 0 us -> 60.7 us
  starting transfers between devices: 73.8 us -> 31.4 us
  waiting for transfers between devices: 123 us -> 84.7 us
  other arithmetic: 28.3 us -> 4.58 us
    dot_general x96 -> x0, matrix products: 186 us -> none  [mat(): jnp.dot(left, right, precision=HIGHEST, preferred_element_type=jnp.float32)]
    all_to_all x8 -> x0, starting transfers between devices: 60.7 us -> none  [the longest x4 32 us: tendency_from(): lax.all_to_all(along_col, 'grid', split_axis=2, concat_axis=1, tiled=True)]
    pallas_call x0 -> x10, Pallas kernels: none -> 60.7 us  [the longest x4 28.6 us: stage_call(): pl.pallas_call(body, grid_spec=pltpu.PrefetchScalarGridSpec(num_scalar_pr...]
    all_to_all x8 -> x0, waiting for transfers between devices: 56.4 us -> none  [the longest x4 41 us: tendency_from(): lax.all_to_all(jnp.transpose(state_now, (0, 2, 1)), 'grid', split_axis=1,...]
    all_to_all x12 -> x0, local copies, waits for them, and re-layouts: 33.8 us -> none  [the longest x8 18.4 us: tendency_from(): lax.all_to_all(along_col, 'grid', split_axis=2, concat_axis=1, tiled=True)]
    unnamed x135 -> x64, local copies, waits for them, and re-layouts: 37.4 us -> 5.24 us
    another operation x8 -> x0, local copies, waits for them, and re-layouts: 27.8 us -> none  [along_last(): flat.reshape(batch, outer, inner)]
    ppermute x4 -> x34, starting transfers between devices: 13.1 us -> 31.4 us  [the longest x20 15.2 us: mate_swap(): return lax.ppermute(array, 'grid', [(i, i ^ 1) for i in range(size)])]
  transfers between devices with their start and end apart: 12 -> 34, of which waited for: 11 -> 13; matrix products, arithmetic and copies ran while one was open for 32% -> 3% of each run, Pallas kernels for 0% -> 11%
where the time goes in v1:
time: 191 us; the launch traced here: 190 us
  waiting for transfers between devices  84.7 us (44%)
  Pallas kernels  60.7 us (32%)
  starting transfers between devices  31.4 us (16%)
  local copies, waits for them, and re-layouts  8.11 us (4%)
  other arithmetic  4.58 us (2%)
    ppermute x2, waiting for transfers between devices, ahead_in_time(): return lax.ppermute(array, 'tm', [(i, i + 1) for i in range(size - 1)])  66.6 us
    pallas_call x4, Pallas kernels, stage_call(): pl.pallas_call(body, grid_spec=pltpu.PrefetchScalarGridSpec(num_scalar_pr...  28.6 us
    pallas_call x4, Pallas kernels, along_x(): pl.pallas_call(x_kernel, grid=(fields,), in_specs=[pl.BlockSpec((rows, le...  19.9 us
    ppermute x20, starting transfers between devices, mate_swap(): return lax.ppermute(array, 'grid', [(i, i ^ 1) for i in range(size)])  15.2 us
    ppermute x12, waiting for transfers between devices, exchange(): lax.ppermute(part, 'grid', [(i, (i + 2 * d) % size) for i in range(size)])  13 us
    pallas_call x2, Pallas kernels, select_call(): pl.pallas_call(body, grid_spec=pltpu.PrefetchScalarGridSpec(num_scalar_pr...  12.2 us
    ppermute x12, starting transfers between devices, exchange(): lax.ppermute(part, 'grid', [(i, (i + 2 * d) % size) for i in range(size)])  9.74 us
    ppermute x2, starting transfers between devices, ahead_in_time(): return lax.ppermute(array, 'tm', [(i, i + 1) for i in range(size - 1)])  6.39 us
  transfers between devices with their start and end apart: 34, of which 13 were waited for; matrix products, arithmetic and copies ran while one was open for 3% of the time, Pallas kernels for 11%

profile of v1, /device:TPU:9, one launch (start us, length us, event | category | flops | bytes accessed | tf_op | source)
XLA Modules:
  0.0 189.8 jit_solution(9695809564941555544)
XLA Ops:
  0.0 3.2 %collective-permute-start = (f32[3,128,1024]{2,1,0:T(8,128)}, f32[3,128,1024]{2,1,0:T(8,128)S(1)}, u32[]{:S(2)}, u32[]{:S(2)}) collective-permute-start(f32[3,128,1024]{2,1,0:T(8,128)} %bitcast.25), channel_id=1, source_target_pairs={{0,8},{8,16},{16,24},{1,9},{9,17},{17,25},{2,10},{10,18},{18,26},{... | collective-permute-start | bytes 4718600 | tf_op jit(solution)/shard_map/ppermute | solution.py:305
  3.9 1.4 dynamic-slice_bitcast_fusion.1.rest_0_.rest_8_.rest_1_
  5.2 32.1 %collective-permute-done.received_ref = f32[3,128,1024]{2,1,0:T(8,128)S(1)} collective-permute-done((f32[3,128,1024]{2,1,0:T(8,128)}, f32[3,128,1024]{2,1,0:T(8,128)S(1)}, u32[]{:S(2)}, u32[]{:S(2)}) %collective-permute-start) | collective-permute-done | bytes 1572896 | tf_op jit(solution)/shard_map/ppermute | solution.py:305
  38.5 6.0 %select_state.2 = (f32[3,128,1024]{2,1,0:T(8,128)}, f32[3,40,512]{2,1,0:T(8,128)}, f32[3,40,512]{2,1,0:T(8,128)}, f32[3,16,1024]{2,1,0:T(8,128)}) custom-call(s32[2]{0:T(128)} %pad_add_fusion.flags_ref, f32[3,128,1024]{2,1,0:T(8,128)} %copy-done.1, f32[3,128,1024]{2,1,0:T(8,128)} %bitcast.26, bf16[128,128]{1,0:T(8,128)(2,1)} %dynamic-slice_bitcast_fusion.1.rest_0_.rest_8_.rest_1_), custom_call_target="tpu_custom_call" | custom-call | tf_op jit(solution)/shard_map/select_state/pallas_call | solution.py:229
  44.5 1.6 collective-permute-start.1
  46.1 1.3 collective-permute-done.1
  48.5 2.2 %collective-permute-start.4 = (f32[3,16,512]{2,1,0:T(8,128)S(1)}, f32[3,16,512]{2,1,0:T(8,128)S(1)}, u32[]{:S(2)}, u32[]{:S(2)}) collective-permute-start(f32[3,16,512]{2,1,0:T(8,128)S(1)} %get-tuple-element.53), channel_id=1, source_target_pairs={{0,6},{1,7},{2,0},{3,1},{4,2},{5,3},{6,4},{7,5},{8,14},{9,15},{10,... | collective-permute-start | bytes 294920 | tf_op jit(solution)/shard_map/ppermute | solution.py:321
  52.1 4.7 %collective-permute-done.3.rest_1_ = f32[3,8,512]{2,1,0:T(8,128)S(1)} collective-permute-done((f32[3,8,512]{2,1,0:T(8,128)S(1)}, f32[3,8,512]{2,1,0:T(8,128)S(1)}, u32[]{:S(2)}, u32[]{:S(2)}) %collective-permute-start.3) | collective-permute-done | bytes 49184 | tf_op jit(solution)/shard_map/ppermute | solution.py:321
  59.6 5.0 %along_x.4 = f32[384,1024]{1,0:T(8,128)} custom-call(f32[384,1024]{1,0:T(8,128)} %bitcast.22, bf16[4,512,512]{2,1,0:T(8,128)(2,1)} %constant.35.clone.table_ref), custom_call_target="tpu_custom_call" | custom-call | tf_op jit(solution)/shard_map/along_x/pallas_call | solution.py:137
  65.3 7.6 %stage_1.1 = (f32[3,128,1024]{2,1,0:T(8,128)}, f32[3,128,1024]{2,1,0:T(8,128)}, f32[3,40,512]{2,1,0:T(8,128)}, f32[3,40,512]{2,1,0:T(8,128)}, f32[3,16,1024]{2,1,0:T(8,128)}) custom-call(s32[2]{0:T(128)} %pad_add_fusion.flags_ref, f32[3,128,1024]{2,1,0:T(8,128)} %get-tuple-element.26.state_ref, f32[3,128,1024]{2,1,0:T(8,128)} %bitcast.23, ...), custom_call_target="tpu_custom_call" | custom-call | tf_op jit(solution)/shard_map/stage_1/pallas_call | solution.py:284
  73.5 1.2 collective-permute-done.9
  77.7 2.3 %collective-permute-done.12.rest_2_ = f32[3,16,512]{2,1,0:T(8,128)S(1)} collective-permute-done((f32[3,16,512]{2,1,0:T(8,128)S(1)}, f32[3,16,512]{2,1,0:T(8,128)S(1)}, u32[]{:S(2)}, u32[]{:S(2)}) %collective-permute-start.12) | collective-permute-done | bytes 98336 | tf_op jit(solution)/shard_map/ppermute | solution.py:321
  80.1 1.5 collective-permute-start.15
  83.7 5.0 %along_x.5 = f32[384,1024]{1,0:T(8,128)} custom-call(f32[384,1024]{1,0:T(8,128)} %bitcast.17, bf16[4,512,512]{2,1,0:T(8,128)(2,1)} %constant.35.clone.table_ref), custom_call_target="tpu_custom_call" | custom-call | tf_op jit(solution)/shard_map/along_x/pallas_call | solution.py:137
  89.5 7.6 %stage_2.1 = (f32[3,128,1024]{2,1,0:T(8,128)}, f32[3,128,1024]{2,1,0:T(8,128)}, f32[3,40,512]{2,1,0:T(8,128)}, f32[3,40,512]{2,1,0:T(8,128)}, f32[3,16,1024]{2,1,0:T(8,128)}) custom-call(s32[2]{0:T(128)} %pad_add_fusion.flags_ref, f32[3,128,1024]{2,1,0:T(8,128)} %get-tuple-element.30.state_ref.own_ref, f32[3,128,1024]{2,1,0:T(8,128)} %bitcast.24, ...), custom_call_target="tpu_custom_call" | custom-call | tf_op jit(solution)/shard_map/stage_2/pallas_call | solution.py:284
  97.8 1.2 collective-permute-done.17
  100.3 1.2 collective-permute-start.18
  102.3 1.9 %collective-permute-done.20.rest_2_ = f32[3,16,512]{2,1,0:T(8,128)S(1)} collective-permute-done((f32[3,16,512]{2,1,0:T(8,128)S(1)}, f32[3,16,512]{2,1,0:T(8,128)S(1)}, u32[]{:S(2)}, u32[]{:S(2)}) %collective-permute-start.20) | collective-permute-done | bytes 98336 | tf_op jit(solution)/shard_map/ppermute | solution.py:321
  104.3 1.6 collective-permute-start.23
  106.7 1.3 collective-permute-start.21
  108.1 5.0 %along_x.6 = f32[384,1024]{1,0:T(8,128)} custom-call(f32[384,1024]{1,0:T(8,128)} %bitcast.18, bf16[4,512,512]{2,1,0:T(8,128)(2,1)} %constant.35.clone.table_ref), custom_call_target="tpu_custom_call" | custom-call | tf_op jit(solution)/shard_map/along_x/pallas_call | solution.py:137
  113.9 7.4 %stage_3.1 = (f32[3,128,1024]{2,1,0:T(8,128)}, f32[3,128,1024]{2,1,0:T(8,128)}, f32[3,128,1024]{2,1,0:T(8,128)}) custom-call(s32[2]{0:T(128)} %pad_add_fusion.flags_ref, f32[3,128,1024]{2,1,0:T(8,128)} %get-tuple-element.34.state_ref, f32[3,128,1024]{2,1,0:T(8,128)} %bitcast.20, f32[128,1]{1,0:T(8,128)} %copy.6.turning_ref, f32[3,16,512]{2,1,0:T(8,128)} %copy-done.8, ...), custom_call_target="tpu_custom_call" | custom-call | tf_op jit(solution)/shard_map/stage_3/pallas_call | solution.py:284
  121.3 3.2 %collective-permute-start.25 = (f32[3,128,1024]{2,1,0:T(8,128)}, f32[3,128,1024]{2,1,0:T(8,128)S(1)}, u32[]{:S(2)}, u32[]{:S(2)}) collective-permute-start(f32[3,128,1024]{2,1,0:T(8,128)} %get-tuple-element.40), channel_id=1, source_target_pairs={{0,8},{8,16},{16,24},{1,9},{9,17},{17,25},{2,10},{10,18},{18,26},{... | collective-permute-start | bytes 4718600 | tf_op jit(solution)/shard_map/ppermute | solution.py:305
  124.5 34.4 %collective-permute-done.25.received_ref = f32[3,128,1024]{2,1,0:T(8,128)S(1)} collective-permute-done((f32[3,128,1024]{2,1,0:T(8,128)}, f32[3,128,1024]{2,1,0:T(8,128)S(1)}, u32[]{:S(2)}, u32[]{:S(2)}) %collective-permute-start.25) | collective-permute-done | bytes 1572896 | tf_op jit(solution)/shard_map/ppermute | solution.py:305
  160.1 6.2 %select_state.3 = (f32[3,128,1024]{2,1,0:T(8,128)}, f32[3,40,512]{2,1,0:T(8,128)}, f32[3,40,512]{2,1,0:T(8,128)}, f32[3,16,1024]{2,1,0:T(8,128)}) custom-call(s32[2]{0:T(128)} %pad_add_fusion.flags_ref, f32[3,128,1024]{2,1,0:T(8,128)} %copy-done, f32[3,128,1024]{2,1,0:T(8,128)} %get-tuple-element.30.state_ref.own_ref, ...), custom_call_target="tpu_custom_call" | custom-call | tf_op jit(solution)/shard_map/select_state/pallas_call | solution.py:229
  166.3 1.3 collective-permute-start.26
  167.6 1.3 collective-permute-done.26
  172.3 1.7 collective-permute-done.29.rest_2_
  174.0 2.0 %collective-permute-start.32 = (f32[3,16,512]{2,1,0:T(8,128)S(1)}, f32[3,16,512]{2,1,0:T(8,128)S(1)}, u32[]{:S(2)}, u32[]{:S(2)}) collective-permute-start(f32[3,16,512]{2,1,0:T(8,128)S(1)} %collective-permute-done.29.rest_2_), channel_id=1, source_target_pairs={{0,1},{1,0},{2,3},{3,2},{4,5},{5,4},{6,7},{7,6},{8,9},{9,8},{10,11... | collective-permute-start | bytes 294920 | tf_op jit(solution)/shard_map/ppermute | solution.py:310
  176.7 1.3 collective-permute-start.30
  178.1 5.0 %along_x.7 = f32[384,1024]{1,0:T(8,128)} custom-call(f32[384,1024]{1,0:T(8,128)} %bitcast.19, bf16[4,512,512]{2,1,0:T(8,128)(2,1)} %constant.35.clone.table_ref), custom_call_target="tpu_custom_call" | custom-call | tf_op jit(solution)/shard_map/along_x/pallas_call | solution.py:137
  183.9 5.9 %stage_4.1 = f32[3,128,1024]{2,1,0:T(8,128)} custom-call(s32[2]{0:T(128)} %pad_add_fusion.flags_ref, f32[3,128,1024]{2,1,0:T(8,128)} %get-tuple-element.42.state_ref, f32[3,128,1024]{2,1,0:T(8,128)} %bitcast.21, f32[128,1]{1,0:T(8,128)} %copy.6.turning_ref, f32[3,16,512]{2,1,0:T(8,128)} %copy-done.9, f32[3,8,512]{2,1,0:T(8,128)} %copy-done.25, ...), custom_call_target="tpu_custom_call" | custom-call | tf_op jit(solution)/shard_map/stage_4/pallas_call | solution.py:284
  (126 shorter events, 24.7 us)
Async XLA Ops:
  0.0 37.4 %collective-permute-start = (f32[3,128,1024]{2,1,0:T(8,128)}, f32[3,128,1024]{2,1,0:T(8,128)S(1)}, u32[]{:S(2)}, u32[]{:S(2)}) collective-permute-start(f32[3,128,1024]{2,1,0:T(8,128)} %bitcast.25), channel_id=1, source_target_pairs={{0,8},{8,16},{16,24},{1,9},{9,17},{17,25},{2,10},{10,18},{18,26},{... | collective-permute-start | bytes 4718600 | tf_op jit(solution)/shard_map/ppermute | solution.py:305
  44.5 3.0 %collective-permute-start.1 = (f32[3,40,512]{2,1,0:T(8,128)}, f32[3,40,512]{2,1,0:T(8,128)S(1)}, u32[]{:S(2)}, u32[]{:S(2)}) collective-permute-start(f32[3,40,512]{2,1,0:T(8,128)} %get-tuple-element.28), channel_id=1, source_target_pairs={{0,1},{1,0},{2,3},{3,2},{4,5},{5,4},{6,7},{7,6},{8,9},{9,8},{10,11... | collective-permute-start | bytes 737288 | tf_op jit(solution)/shard_map/ppermute | solution.py:310
  48.5 9.2 %collective-permute-start.4 = (f32[3,16,512]{2,1,0:T(8,128)S(1)}, f32[3,16,512]{2,1,0:T(8,128)S(1)}, u32[]{:S(2)}, u32[]{:S(2)}) collective-permute-start(f32[3,16,512]{2,1,0:T(8,128)S(1)} %get-tuple-element.53), channel_id=1, source_target_pairs={{0,6},{1,7},{2,0},{3,1},{4,2},{5,3},{6,4},{7,5},{8,14},{9,15},{10,... | collective-permute-start | bytes 294920 | tf_op jit(solution)/shard_map/ppermute | solution.py:321
  50.7 7.0 %collective-permute-start.2 = (f32[3,16,512]{2,1,0:T(8,128)S(1)}, f32[3,16,512]{2,1,0:T(8,128)S(1)}, u32[]{:S(2)}, u32[]{:S(2)}) collective-permute-start(f32[3,16,512]{2,1,0:T(8,128)S(1)} %get-tuple-element.54), channel_id=1, source_target_pairs={{0,2},{1,3},{2,4},{3,5},{4,6},{5,7},{6,0},{7,1},{8,10},{9,11},{10,... | collective-permute-start | bytes 294920 | tf_op jit(solution)/shard_map/ppermute | solution.py:321
  50.7 13.9 %collective-permute-start.8 = (f32[3,16,1024]{2,1,0:T(8,128)}, f32[3,16,1024]{2,1,0:T(8,128)S(1)}, u32[]{:S(2)}, u32[]{:S(2)}) collective-permute-start(f32[3,16,1024]{2,1,0:T(8,128)} %get-tuple-element.29), channel_id=1, source_target_pairs={{0,1},{1,0},{2,3},{3,2},{4,5},{5,4},{6,7},{7,6},{8,9},{9,8},{10,11... | collective-permute-start | bytes 589832 | tf_op jit(solution)/shard_map/ppermute | solution.py:310
  51.3 5.5 %collective-permute-start.3 = (f32[3,8,512]{2,1,0:T(8,128)S(1)}, f32[3,8,512]{2,1,0:T(8,128)S(1)}, u32[]{:S(2)}, u32[]{:S(2)}) collective-permute-start(f32[3,8,512]{2,1,0:T(8,128)S(1)} %slice.49), channel_id=1, source_target_pairs={{0,4},{1,5},{2,6},{3,7},{4,0},{5,1},{6,2},{7,3},{8,12},{9,13},{10,... | collective-permute-start | bytes 147464 | tf_op jit(solution)/shard_map/ppermute | solution.py:321
  56.9 7.7 %collective-permute-start.6 = (f32[3,8,512]{2,1,0:T(8,128)S(1)}, f32[3,8,512]{2,1,0:T(8,128)S(1)}, u32[]{:S(2)}, u32[]{:S(2)}) collective-permute-start(f32[3,8,512]{2,1,0:T(8,128)S(1)} %collective-permute-done.3.rest_1_), channel_id=1, source_target_pairs={{0,1},{1,0},{2,3},{3,2},{4,5},{5,4},{6,7},{7,6},{8,9},{9,8},{10,11... | collective-permute-start | bytes 147464 | tf_op jit(solution)/shard_map/ppermute | solution.py:310
  57.6 7.0 %collective-permute-start.7 = (f32[3,16,512]{2,1,0:T(8,128)S(1)}, f32[3,16,512]{2,1,0:T(8,128)S(1)}, u32[]{:S(2)}, u32[]{:S(2)}) collective-permute-start(f32[3,16,512]{2,1,0:T(8,128)S(1)} %collective-permute-done.4.rest_2_), channel_id=1, source_target_pairs={{0,1},{1,0},{2,3},{3,2},{4,5},{5,4},{6,7},{7,6},{8,9},{9,8},{10,11... | collective-permute-start | bytes 294920 | tf_op jit(solution)/shard_map/ppermute | solution.py:310
  57.7 6.9 %collective-permute-start.5 = (f32[3,16,512]{2,1,0:T(8,128)S(1)}, f32[3,16,512]{2,1,0:T(8,128)S(1)}, u32[]{:S(2)}, u32[]{:S(2)}) collective-permute-start(f32[3,16,512]{2,1,0:T(8,128)S(1)} %collective-permute-done.2.rest_0_), channel_id=1, source_target_pairs={{0,1},{1,0},{2,3},{3,2},{4,5},{5,4},{6,7},{7,6},{8,9},{9,8},{10,11... | collective-permute-start | bytes 294920 | tf_op jit(solution)/shard_map/ppermute | solution.py:310
  73.1 15.6 %collective-permute-start.16 = (f32[3,16,1024]{2,1,0:T(8,128)}, f32[3,16,1024]{2,1,0:T(8,128)S(1)}, u32[]{:S(2)}, u32[]{:S(2)}) collective-permute-start(f32[3,16,1024]{2,1,0:T(8,128)} %get-tuple-element.33), channel_id=1, source_target_pairs={{0,1},{1,0},{2,3},{3,2},{4,5},{5,4},{6,7},{7,6},{8,9},{9,8},{10,11... | collective-permute-start | bytes 589832 | tf_op jit(solution)/shard_map/ppermute | solution.py:310
  75.7 4.3 %collective-permute-start.12 = (f32[3,16,512]{2,1,0:T(8,128)S(1)}, f32[3,16,512]{2,1,0:T(8,128)S(1)}, u32[]{:S(2)}, u32[]{:S(2)}) collective-permute-start(f32[3,16,512]{2,1,0:T(8,128)S(1)} %get-tuple-element.51), channel_id=1, source_target_pairs={{0,6},{1,7},{2,0},{3,1},{4,2},{5,3},{6,4},{7,5},{8,14},{9,15},{10,... | collective-permute-start | bytes 294920 | tf_op jit(solution)/shard_map/ppermute | solution.py:321
  76.6 5.8 %collective-permute-start.10 = (f32[3,16,512]{2,1,0:T(8,128)S(1)}, f32[3,16,512]{2,1,0:T(8,128)S(1)}, u32[]{:S(2)}, u32[]{:S(2)}) collective-permute-start(f32[3,16,512]{2,1,0:T(8,128)S(1)} %get-tuple-element.52), channel_id=1, source_target_pairs={{0,2},{1,3},{2,4},{3,5},{4,6},{5,7},{6,0},{7,1},{8,10},{9,11},{10,... | collective-permute-start | bytes 294920 | tf_op jit(solution)/shard_map/ppermute | solution.py:321
  77.3 6.1 %collective-permute-start.11 = (f32[3,8,512]{2,1,0:T(8,128)S(1)}, f32[3,8,512]{2,1,0:T(8,128)S(1)}, u32[]{:S(2)}, u32[]{:S(2)}) collective-permute-start(f32[3,8,512]{2,1,0:T(8,128)S(1)} %slice.52), channel_id=1, source_target_pairs={{0,4},{1,5},{2,6},{3,7},{4,0},{5,1},{6,2},{7,3},{8,12},{9,13},{10,... | collective-permute-start | bytes 147464 | tf_op jit(solution)/shard_map/ppermute | solution.py:321
  80.1 8.7 %collective-permute-start.15 = (f32[3,16,512]{2,1,0:T(8,128)S(1)}, f32[3,16,512]{2,1,0:T(8,128)S(1)}, u32[]{:S(2)}, u32[]{:S(2)}) collective-permute-start(f32[3,16,512]{2,1,0:T(8,128)S(1)} %collective-permute-done.12.rest_2_), channel_id=1, source_target_pairs={{0,1},{1,0},{2,3},{3,2},{4,5},{5,4},{6,7},{7,6},{8,9},{9,8},{10,11... | collective-permute-start | bytes 294920 | tf_op jit(solution)/shard_map/ppermute | solution.py:310
  82.4 6.4 %collective-permute-start.13 = (f32[3,16,512]{2,1,0:T(8,128)S(1)}, f32[3,16,512]{2,1,0:T(8,128)S(1)}, u32[]{:S(2)}, u32[]{:S(2)}) collective-permute-start(f32[3,16,512]{2,1,0:T(8,128)S(1)} %collective-permute-done.10.rest_0_), channel_id=1, source_target_pairs={{0,1},{1,0},{2,3},{3,2},{4,5},{5,4},{6,7},{7,6},{8,9},{9,8},{10,11... | collective-permute-start | bytes 294920 | tf_op jit(solution)/shard_map/ppermute | solution.py:310
  83.4 5.3 %collective-permute-start.14 = (f32[3,8,512]{2,1,0:T(8,128)S(1)}, f32[3,8,512]{2,1,0:T(8,128)S(1)}, u32[]{:S(2)}, u32[]{:S(2)}) collective-permute-start(f32[3,8,512]{2,1,0:T(8,128)S(1)} %collective-permute-done.11.rest_1_), channel_id=1, source_target_pairs={{0,1},{1,0},{2,3},{3,2},{4,5},{5,4},{6,7},{7,6},{8,9},{9,8},{10,11... | collective-permute-start | bytes 147464 | tf_op jit(solution)/shard_map/ppermute | solution.py:310
  97.4 15.6 %collective-permute-start.24 = (f32[3,16,1024]{2,1,0:T(8,128)}, f32[3,16,1024]{2,1,0:T(8,128)S(1)}, u32[]{:S(2)}, u32[]{:S(2)}) collective-permute-start(f32[3,16,1024]{2,1,0:T(8,128)} %get-tuple-element.37), channel_id=1, source_target_pairs={{0,1},{1,0},{2,3},{3,2},{4,5},{5,4},{6,7},{7,6},{8,9},{9,8},{10,11... | collective-permute-start | bytes 589832 | tf_op jit(solution)/shard_map/ppermute | solution.py:310
  100.0 4.3 %collective-permute-start.20 = (f32[3,16,512]{2,1,0:T(8,128)S(1)}, f32[3,16,512]{2,1,0:T(8,128)S(1)}, u32[]{:S(2)}, u32[]{:S(2)}) collective-permute-start(f32[3,16,512]{2,1,0:T(8,128)S(1)} %get-tuple-element.49), channel_id=1, source_target_pairs={{0,6},{1,7},{2,0},{3,1},{4,2},{5,3},{6,4},{7,5},{8,14},{9,15},{10,... | collective-permute-start | bytes 294920 | tf_op jit(solution)/shard_map/ppermute | solution.py:321
  100.3 6.4 %collective-permute-start.18 = (f32[3,16,512]{2,1,0:T(8,128)S(1)}, f32[3,16,512]{2,1,0:T(8,128)S(1)}, u32[]{:S(2)}, u32[]{:S(2)}) collective-permute-start(f32[3,16,512]{2,1,0:T(8,128)S(1)} %get-tuple-element.50), channel_id=1, source_target_pairs={{0,2},{1,3},{2,4},{3,5},{4,6},{5,7},{6,0},{7,1},{8,10},{9,11},{10,... | collective-permute-start | bytes 294920 | tf_op jit(solution)/shard_map/ppermute | solution.py:321
  101.5 6.5 %collective-permute-start.19 = (f32[3,8,512]{2,1,0:T(8,128)S(1)}, f32[3,8,512]{2,1,0:T(8,128)S(1)}, u32[]{:S(2)}, u32[]{:S(2)}) collective-permute-start(f32[3,8,512]{2,1,0:T(8,128)S(1)} %slice.55), channel_id=1, source_target_pairs={{0,4},{1,5},{2,6},{3,7},{4,0},{5,1},{6,2},{7,3},{8,12},{9,13},{10,... | collective-permute-start | bytes 147464 | tf_op jit(solution)/shard_map/ppermute | solution.py:321
  104.3 8.8 %collective-permute-start.23 = (f32[3,16,512]{2,1,0:T(8,128)S(1)}, f32[3,16,512]{2,1,0:T(8,128)S(1)}, u32[]{:S(2)}, u32[]{:S(2)}) collective-permute-start(f32[3,16,512]{2,1,0:T(8,128)S(1)} %collective-permute-done.20.rest_2_), channel_id=1, source_target_pairs={{0,1},{1,0},{2,3},{3,2},{4,5},{5,4},{6,7},{7,6},{8,9},{9,8},{10,11... | collective-permute-start | bytes 294920 | tf_op jit(solution)/shard_map/ppermute | solution.py:310
  106.7 6.4 %collective-permute-start.21 = (f32[3,16,512]{2,1,0:T(8,128)S(1)}, f32[3,16,512]{2,1,0:T(8,128)S(1)}, u32[]{:S(2)}, u32[]{:S(2)}) collective-permute-start(f32[3,16,512]{2,1,0:T(8,128)S(1)} %collective-permute-done.18.rest_0_), channel_id=1, source_target_pairs={{0,1},{1,0},{2,3},{3,2},{4,5},{5,4},{6,7},{7,6},{8,9},{9,8},{10,11... | collective-permute-start | bytes 294920 | tf_op jit(solution)/shard_map/ppermute | solution.py:310
  108.0 5.1 %collective-permute-start.22 = (f32[3,8,512]{2,1,0:T(8,128)S(1)}, f32[3,8,512]{2,1,0:T(8,128)S(1)}, u32[]{:S(2)}, u32[]{:S(2)}) collective-permute-start(f32[3,8,512]{2,1,0:T(8,128)S(1)} %collective-permute-done.19.rest_1_), channel_id=1, source_target_pairs={{0,1},{1,0},{2,3},{3,2},{4,5},{5,4},{6,7},{7,6},{8,9},{9,8},{10,11... | collective-permute-start | bytes 147464 | tf_op jit(solution)/shard_map/ppermute | solution.py:310
  121.3 37.6 %collective-permute-start.25 = (f32[3,128,1024]{2,1,0:T(8,128)}, f32[3,128,1024]{2,1,0:T(8,128)S(1)}, u32[]{:S(2)}, u32[]{:S(2)}) collective-permute-start(f32[3,128,1024]{2,1,0:T(8,128)} %get-tuple-element.40), channel_id=1, source_target_pairs={{0,8},{8,16},{16,24},{1,9},{9,17},{17,25},{2,10},{10,18},{18,26},{... | collective-permute-start | bytes 4718600 | tf_op jit(solution)/shard_map/ppermute | solution.py:305
  166.3 2.6 %collective-permute-start.26 = (f32[3,40,512]{2,1,0:T(8,128)}, f32[3,40,512]{2,1,0:T(8,128)S(1)}, u32[]{:S(2)}, u32[]{:S(2)}) collective-permute-start(f32[3,40,512]{2,1,0:T(8,128)} %get-tuple-element.44), channel_id=1, source_target_pairs={{0,1},{1,0},{2,3},{3,2},{4,5},{5,4},{6,7},{7,6},{8,9},{9,8},{10,11... | collective-permute-start | bytes 737288 | tf_op jit(solution)/shard_map/ppermute | solution.py:310
  167.6 15.5 %collective-permute-start.33 = (f32[3,16,1024]{2,1,0:T(8,128)}, f32[3,16,1024]{2,1,0:T(8,128)S(1)}, u32[]{:S(2)}, u32[]{:S(2)}) collective-permute-start(f32[3,16,1024]{2,1,0:T(8,128)} %get-tuple-element.45), channel_id=1, source_target_pairs={{0,1},{1,0},{2,3},{3,2},{4,5},{5,4},{6,7},{7,6},{8,9},{9,8},{10,11... | collective-permute-start | bytes 589832 | tf_op jit(solution)/shard_map/ppermute | solution.py:310
  169.9 4.1 %collective-permute-start.29 = (f32[3,16,512]{2,1,0:T(8,128)S(1)}, f32[3,16,512]{2,1,0:T(8,128)S(1)}, u32[]{:S(2)}, u32[]{:S(2)}) collective-permute-start(f32[3,16,512]{2,1,0:T(8,128)S(1)} %get-tuple-element.47), channel_id=1, source_target_pairs={{0,6},{1,7},{2,0},{3,1},{4,2},{5,3},{6,4},{7,5},{8,14},{9,15},{10,... | collective-permute-start | bytes 294920 | tf_op jit(solution)/shard_map/ppermute | solution.py:321
  170.5 6.2 %collective-permute-start.27 = (f32[3,16,512]{2,1,0:T(8,128)S(1)}, f32[3,16,512]{2,1,0:T(8,128)S(1)}, u32[]{:S(2)}, u32[]{:S(2)}) collective-permute-start(f32[3,16,512]{2,1,0:T(8,128)S(1)} %get-tuple-element.48), channel_id=1, source_target_pairs={{0,2},{1,3},{2,4},{3,5},{4,6},{5,7},{6,0},{7,1},{8,10},{9,11},{10,... | collective-permute-start | bytes 294920 | tf_op jit(solution)/shard_map/ppermute | solution.py:321
  171.4 6.5 %collective-permute-start.28 = (f32[3,8,512]{2,1,0:T(8,128)S(1)}, f32[3,8,512]{2,1,0:T(8,128)S(1)}, u32[]{:S(2)}, u32[]{:S(2)}) collective-permute-start(f32[3,8,512]{2,1,0:T(8,128)S(1)} %slice.58), channel_id=1, source_target_pairs={{0,4},{1,5},{2,6},{3,7},{4,0},{5,1},{6,2},{7,3},{8,12},{9,13},{10,... | collective-permute-start | bytes 147464 | tf_op jit(solution)/shard_map/ppermute | solution.py:321
  174.0 9.2 %collective-permute-start.32 = (f32[3,16,512]{2,1,0:T(8,128)S(1)}, f32[3,16,512]{2,1,0:T(8,128)S(1)}, u32[]{:S(2)}, u32[]{:S(2)}) collective-permute-start(f32[3,16,512]{2,1,0:T(8,128)S(1)} %collective-permute-done.29.rest_2_), channel_id=1, source_target_pairs={{0,1},{1,0},{2,3},{3,2},{4,5},{5,4},{6,7},{7,6},{8,9},{9,8},{10,11... | collective-permute-start | bytes 294920 | tf_op jit(solution)/shard_map/ppermute | solution.py:310
  176.7 6.5 %collective-permute-start.30 = (f32[3,16,512]{2,1,0:T(8,128)S(1)}, f32[3,16,512]{2,1,0:T(8,128)S(1)}, u32[]{:S(2)}, u32[]{:S(2)}) collective-permute-start(f32[3,16,512]{2,1,0:T(8,128)S(1)} %collective-permute-done.27.rest_0_), channel_id=1, source_target_pairs={{0,1},{1,0},{2,3},{3,2},{4,5},{5,4},{6,7},{7,6},{8,9},{9,8},{10,11... | collective-permute-start | bytes 294920 | tf_op jit(solution)/shard_map/ppermute | solution.py:310
  178.0 5.1 %collective-permute-start.31 = (f32[3,8,512]{2,1,0:T(8,128)S(1)}, f32[3,8,512]{2,1,0:T(8,128)S(1)}, u32[]{:S(2)}, u32[]{:S(2)}) collective-permute-start(f32[3,8,512]{2,1,0:T(8,128)S(1)} %collective-permute-done.28.rest_1_), channel_id=1, source_target_pairs={{0,1},{1,0},{2,3},{3,2},{4,5},{5,4},{6,7},{7,6},{8,9},{9,8},{10,11... | collective-permute-start | bytes 147464 | tf_op jit(solution)/shard_map/ppermute | solution.py:310
  (34 other events, 206.2 us)

commit v2 on v1

--- a/solution.py
+++ b/solution.py
@@ -17,8 +17,8 @@
 CORRECT_FIRST = (5.0 / 24.0 - 0.5, 8.0 / 24.0, -1.0 / 24.0)
 CORRECT_SECOND = (-1.0 / 24.0, 8.0 / 24.0 - 0.5, 5.0 / 24.0)
 TOLERANCE = 1e-8
-TILE = 256
-ROWS = 16
+ROWS = 8
+KERNEL_BYTES = 20 * 2**20
 F32 = jnp.float32
 BF16 = jnp.bfloat16
 
@@ -117,10 +117,26 @@
     return both[:count] + both[count:] + dot(stacked[:count], low)
 
 
+VMEM = pl.BlockSpec(memory_space=pltpu.VMEM)
+SMEM = pl.BlockSpec(memory_space=pltpu.SMEM)
+
+
+def on_chip_call(body, operands, shapes, scalars=1, keep=True, **options):
+    held = [pltpu.with_memory_space_constraint(a, pltpu.VMEM) for a in operands[scalars:]]
+    outs = [pltpu.VMEM(s.shape, s.dtype) for s in shapes] if keep else shapes
+    return pl.pallas_call(
+        body,
+        in_specs=[SMEM] * scalars + [VMEM] * len(held),
+        out_specs=[VMEM] * len(outs),
+        out_shape=outs,
+        compiler_params=pltpu.CompilerParams(vmem_limit_bytes=KERNEL_BYTES),
+        **options,
+    )(*operands[:scalars], *held)
+
+
 def x_kernel(state_ref, table_ref, out_ref):
-    value = state_ref[...]
-    half = value.shape[1] // 2
-    left, right = value[:, :half], value[:, half:]
+    half = state_ref.shape[1] // 2
+    left, right = state_ref[:, :half], state_ref[:, half:]
 
     def folded(total, at):
         high, low = parts_of(total)
@@ -134,17 +150,14 @@
 
 def along_x(state, table):
     fields, rows, length = state.shape
-    out = pl.pallas_call(
-        x_kernel,
-        grid=(fields,),
-        in_specs=[
-            pl.BlockSpec((rows, length), lambda f: (f, 0)),
-            pl.BlockSpec(table.shape, lambda f: (0, 0, 0)),
-        ],
-        out_specs=pl.BlockSpec((rows, length), lambda f: (f, 0)),
-        out_shape=jax.ShapeDtypeStruct((fields * rows, length), F32),
-        name="along_x",
-    )(state.reshape(fields * rows, length), table)
+    flat = state.reshape(fields * rows, length)
+    cost = pl.CostEstimate(
+        flops=6 * flat.shape[0] * length * length // 2,
+        transcendentals=0,
+        bytes_accessed=8 * flat.size + 2 * table.size,
+    )
+    shape = jax.ShapeDtypeStruct(flat.shape, F32)
+    (out,) = on_chip_call(x_kernel, [flat, table], [shape], scalars=0, cost_estimate=cost, name="along_x")
     return out.reshape(state.shape)
 
 
@@ -154,55 +167,30 @@
         self.ranks, self.mate_rank = ranks, mate_rank
         self.total = sum(ranks)
         self.half = length // 2
-        self.per_half = self.half // TILE
-        self.tiles = length // TILE
         self.state = jax.ShapeDtypeStruct((3, rows, length), F32)
-        self.state_spec = pl.BlockSpec((3, rows, TILE), lambda t, flags: (0, 0, t))
-        self.row_blocks = [(r, min(ROWS, rows - r)) for r in range(0, rows, ROWS)]
-
-    def whole(self, shape):
-        return pl.BlockSpec(shape, lambda t, flags: (0,) * len(shape))
-
-    def moment_outs(self):
         half = jax.ShapeDtypeStruct((3, self.total, self.half), F32)
-        mate = jax.ShapeDtypeStruct((3, self.mate_rank, self.length), F32)
-        return (half, half, mate), (
-            self.whole(half.shape),
-            self.whole(half.shape),
-            pl.BlockSpec((3, self.mate_rank, TILE), lambda t, flags: (0, 0, t)),
-        )
-
-    def emit_moments(self, flags_ref, next_ref, send_ref, mine_ref, theirs_ref, mate_ref):
-        tile = pl.program_id(0)
-        is_mine = tile // self.per_half == flags_ref[0]
-        start = pl.multiple_of((tile % self.per_half) * TILE, TILE)
+        self.moments = (half, half, jax.ShapeDtypeStruct((3, mate_rank, length), F32))
+
+    def halves(self, flags_ref):
+        member = flags_ref[0]
+        for slot, at in ((0, member), (1, 1 - member)):
+            yield slot, pl.ds(pl.multiple_of(at * self.half, 128), self.half)
+
+    def emit_moments(self, slot, cols, next_ref, send_ref, moment_refs):
         for f in range(3):
-            found = product(send_ref[...], *parts_of(next_ref[f]))
-            mate_ref[f] = found[self.total : self.total + self.mate_rank]
-
-            @pl.when(is_mine)
-            def _():
-                mine_ref[f, :, pl.ds(start, TILE)] = found[: self.total]
-
-            @pl.when(jnp.logical_not(is_mine))
-            def _():
-                theirs_ref[f, :, pl.ds(start, TILE)] = found[: self.total]
-
-    def y_gradient(self, f, flags_ref, state_ref, mine_refs, other_refs, mate_ref, apply_ref):
-        tile = pl.program_id(0)
-        is_mine = tile // self.per_half == flags_ref[0]
-        start = pl.multiple_of((tile % self.per_half) * TILE, TILE)
-        pieces = [state_ref[f]]
+            found = product(send_ref[...], *parts_of(next_ref[f, :, cols]))
+            moment_refs[slot][f] = found[: self.total]
+            moment_refs[2][f, :, cols] = found[self.total : self.total + self.mate_rank]
+
+    def y_gradient(self, f, cols, state_ref, pair_refs, mate_ref, apply_ref):
+        pieces = [state_ref[f, :, cols]]
         if self.rows % 16:
-            pieces.append(jnp.zeros((-self.rows % 16, TILE), F32))
-        for a, b in zip(mine_refs, other_refs):
-            here = a[f, :, pl.ds(start, TILE)]
-            there = b[f, :, pl.ds(start, TILE)]
-            pieces.append(jnp.where(is_mine, here, there))
-        pieces.append(mate_ref[f])
+            pieces.append(jnp.zeros((-self.rows % 16, self.half), F32))
+        pieces += [ref[f] for ref in pair_refs]
+        pieces.append(mate_ref[f, :, cols])
         width = apply_ref.shape[1] - sum(p.shape[0] for p in pieces)
         if width:
-            pieces.append(jnp.zeros((width, TILE), F32))
+            pieces.append(jnp.zeros((width, self.half), F32))
         return product(apply_ref[...], *parts_of(jnp.concatenate(pieces, axis=0)))
 
 
@@ -218,25 +206,16 @@
 
     def body(flags_ref, received_ref, own_ref, *rest):
         added_ref = rest[0] if extra else None
-        send_ref, next_ref, mine_ref, theirs_ref, mate_ref = rest[len(extra) :]
+        send_ref, next_ref, *moment_refs = rest[len(extra) :]
         first = flags_ref[1] == 0
-        for f in range(3):
-            value = jnp.where(first, own_ref[f], received_ref[f])
-            next_ref[f] = value if added_ref is None else value + added_ref[f]
-        plan.emit_moments(flags_ref, next_ref, send_ref, mine_ref, theirs_ref, mate_ref)
-
-    shapes, specs = plan.moment_outs()
-    return pl.pallas_call(
-        body,
-        grid_spec=pltpu.PrefetchScalarGridSpec(
-            num_scalar_prefetch=1,
-            grid=(plan.tiles,),
-            in_specs=[plan.state_spec] * (2 + len(extra)) + [plan.whole(send.shape)],
-            out_specs=[plan.state_spec, *specs],
-        ),
-        out_shape=[plan.state, *shapes],
-        name="select_state",
-    )(flags, received, own, *extra, send)
+        for slot, cols in plan.halves(flags_ref):
+            for f in range(3):
+                value = jnp.where(first, own_ref[f, :, cols], received_ref[f, :, cols])
+                next_ref[f, :, cols] = value if added_ref is None else value + added_ref[f, :, cols]
+            plan.emit_moments(slot, cols, next_ref, send_ref, moment_refs)
+
+    operands = [flags, received, own, *extra, send]
+    return on_chip_call(body, operands, [plan.state, *plan.moments], name="select_state")
 
 
 def stage_call(plan, flags, stage, state, grad_x, received, turning, apply, send, others):
@@ -245,59 +224,52 @@
     with_moments = stage in (1, 2)
 
     def body(flags_ref, state_ref, grad_ref, turning_ref, *rest):
-        mine_refs, rest = rest[:count], rest[count:]
-        other_refs, rest = rest[:count], rest[count:]
+        pair_refs, rest = (rest[:count], rest[count : 2 * count]), rest[2 * count :]
         mate_ref, apply_ref, rest = rest[0], rest[1], rest[2:]
         other_ins, rest = rest[: len(others)], rest[len(others) :]
         if with_moments:
             send_ref, rest = rest[0], rest[1:]
         grad_y = rest[-1]
-        for f in range(3):
-            grad_y[f] = plan.y_gradient(f, flags_ref, state_ref, mine_refs, other_refs, mate_ref, apply_ref)
-        for start, size in plan.row_blocks:
-            at = slice(start, start + size)
-            now = [state_ref[f, at, :] for f in range(3)]
-            rates = tendency_rows(
-                *now,
-                [grad_ref[f, at, :] for f in range(3)],
-                [grad_y[f, at, :] for f in range(3)],
-                turning_ref[at, :],
-            )
+        for slot, cols in plan.halves(flags_ref):
             for f in range(3):
-                ahead = now[f] + HALF_STEP * rates[f]
-                if stage in (1, 2):
-                    rest[0][f, at, :] = ahead
-                    rest[1][f, at, :] = rates[f]
-                elif stage == 3:
-                    rest[0][f, at, :] = ahead
-                    olds = (other_ins[0][f, at, :], other_ins[1][f, at, :], rates[f])
-                    for out, weights in ((rest[1], CORRECT_FIRST), (rest[2], CORRECT_SECOND)):
-                        out[f, at, :] = sum((STEP_LENGTH * w) * r for w, r in zip(weights, olds))
-                else:
-                    rest[0][f, at, :] = ahead + other_ins[0][f, at, :]
-        if with_moments:
-            plan.emit_moments(flags_ref, rest[0], send_ref, *rest[2:5])
-
+                grad_y[f] = plan.y_gradient(f, cols, state_ref, pair_refs[slot], mate_ref, apply_ref)
+            for start in range(0, plan.rows, ROWS):
+                at = slice(start, start + ROWS)
+                now = [state_ref[f, at, cols] for f in range(3)]
+                rates = tendency_rows(
+                    *now,
+                    [grad_ref[f, at, cols] for f in range(3)],
+                    [grad_y[f, at, :] for f in range(3)],
+                    turning_ref[at, :],
+                )
+                for f in range(3):
+                    ahead = now[f] + HALF_STEP * rates[f]
+                    if stage in (1, 2):
+                        rest[0][f, at, cols] = ahead
+                        rest[1][f, at, cols] = rates[f]
+                    elif stage == 3:
+                        rest[0][f, at, cols] = ahead
+                        olds = (other_ins[0][f, at, cols], other_ins[1][f, at, cols], rates[f])
+                        for out, weights in ((rest[1], CORRECT_FIRST), (rest[2], CORRECT_SECOND)):
+                            out[f, at, cols] = sum((STEP_LENGTH * w) * r for w, r in zip(weights, olds))
+                    else:
+                        rest[0][f, at, cols] = ahead + other_ins[0][f, at, cols]
+            if with_moments:
+                plan.emit_moments(slot, cols, rest[0], send_ref, rest[2:5])
+
+    operands = [flags, state, grad_x, turning, *mine, *other, mate, apply, *others]
+    if with_moments:
+        operands.append(send)
     state_outs = {1: 2, 2: 2, 3: 3, 4: 1}[stage]
-    shapes, specs = plan.moment_outs() if with_moments else ((), ())
-    mate_spec = pl.BlockSpec((3, plan.mate_rank, TILE), lambda t, flags: (0, 0, t))
-    return pl.pallas_call(
+    shapes = [plan.state] * state_outs + (list(plan.moments) if with_moments else [])
+    return on_chip_call(
         body,
-        grid_spec=pltpu.PrefetchScalarGridSpec(
-            num_scalar_prefetch=1,
-            grid=(plan.tiles,),
-            in_specs=[plan.state_spec] * 2
-            + [plan.whole(turning.shape)]
-            + [plan.whole(a.shape) for a in (*mine, *other)]
-            + [mate_spec, plan.whole(apply.shape)]
-            + [plan.state_spec] * len(others)
-            + ([plan.whole(send.shape)] if with_moments else []),
-            out_specs=[plan.state_spec] * state_outs + list(specs),
-            scratch_shapes=[pltpu.VMEM((3, plan.rows, TILE), F32)],
-        ),
-        out_shape=[plan.state] * state_outs + list(shapes),
+        operands,
+        shapes,
+        keep=stage != 4,
+        scratch_shapes=[pltpu.VMEM((3, plan.rows, plan.half), F32)],
         name=f"stage_{stage}",
-    )(flags, state, grad_x, turning, *mine, *other, mate, apply, *others, *([send] if with_moments else []))
+    )
 
 
 def ahead_in_time(array):

time: 191 us -> 145 us (0.76)
  Pallas kernels: 60.7 us -> 18.5 us
  other arithmetic: 4.58 us -> 0.22 us
    pallas_call x10, Pallas kernels: 60.7 us -> 18.5 us  [on_chip_call(): pl.pallas_call(body, in_specs=[SMEM] * scalars + [VMEM] * len(held), out_...]
    add x4, other arithmetic: 3.94 us -> 0.14 us  [exchange(): merged = mine + mate_swap(theirs)]
    unnamed x64 -> x18, local copies, waits for them, and re-layouts: 5.24 us -> 6.52 us
  transfers between devices with their start and end apart: 34 -> 34, of which waited for: 13 -> 12; matrix products, arithmetic and copies ran while one was open for 3% -> 1% of each run, Pallas kernels for 11% -> 4%
where the time goes in v2:
time: 145 us
  waiting for transfers between devices  86.2 us (59%)
  starting transfers between devices  31.9 us (22%)
  Pallas kernels  18.5 us (13%)
  local copies, waits for them, and re-layouts  7.48 us (5%)
    ppermute x2, waiting for transfers between devices, ahead_in_time(): return lax.ppermute(array, 'tm', [(i, i + 1) for i in range(size - 1)])  67.9 us
    pallas_call x10, Pallas kernels, on_chip_call(): pl.pallas_call(body, in_specs=[SMEM] * scalars + [VMEM] * len(held), out_...  18.5 us
    ppermute x20, starting transfers between devices, mate_swap(): return lax.ppermute(array, 'grid', [(i, i ^ 1) for i in range(size)])  15 us
    ppermute x12, waiting for transfers between devices, exchange(): lax.ppermute(part, 'grid', [(i, (i + 2 * d) % size) for i in range(size)])  13 us
    ppermute x12, starting transfers between devices, exchange(): lax.ppermute(part, 'grid', [(i, (i + 2 * d) % size) for i in range(size)])  10.5 us
    unnamed x18, local copies, waits for them, and re-layouts  6.52 us
    ppermute x2, starting transfers between devices, ahead_in_time(): return lax.ppermute(array, 'tm', [(i, i + 1) for i in range(size - 1)])  6.4 us
    ppermute x20, waiting for transfers between devices, mate_swap(): return lax.ppermute(array, 'grid', [(i, i ^ 1) for i in range(size)])  5.26 us
  transfers between devices with their start and end apart: 34, of which 12 were waited for; matrix products, arithmetic and copies ran while one was open for 1% of the time, Pallas kernels for 4%

profile of v2, /device:TPU:9, one launch (start us, length us, event | category | flops | bytes accessed | tf_op | source)
XLA Modules:
  0.0 144.6 jit_solution(2530785493527939060)
XLA Ops:
  0.0 3.2 %collective-permute-start = (f32[3,128,1024]{2,1,0:T(8,128)}, f32[3,128,1024]{2,1,0:T(8,128)S(1)}, u32[]{:S(2)}, u32[]{:S(2)}) collective-permute-start(f32[3,128,1024]{2,1,0:T(8,128)} %bitcast.25), channel_id=1, source_target_pairs={{0,8},{8,16},{16,24},{1,9},{9,17},{17,25},{2,10},{10,18},{18,26},{... | collective-permute-start | bytes 4718600 | tf_op jit(solution)/shard_map/ppermute | solution.py:277
  4.1 33.3 %collective-permute-done.received_ref = f32[3,128,1024]{2,1,0:T(8,128)S(1)} collective-permute-done((f32[3,128,1024]{2,1,0:T(8,128)}, f32[3,128,1024]{2,1,0:T(8,128)S(1)}, u32[]{:S(2)}, u32[]{:S(2)}) %collective-permute-start) | collective-permute-done | bytes 1572896 | tf_op jit(solution)/shard_map/ppermute | solution.py:277
  38.5 1.4 copy-done.4
  39.9 1.4 copy-done.6
  41.3 1.2 select_state.2
  43.7 1.5 %collective-permute-start.1 = (f32[3,40,512]{2,1,0:T(8,128)S(1)}, f32[3,40,512]{2,1,0:T(8,128)S(1)}, u32[]{:S(2)}, u32[]{:S(2)}) collective-permute-start(f32[3,40,512]{2,1,0:T(8,128)S(1)} %get-tuple-element.28), channel_id=1, source_target_pairs={{0,1},{1,0},{2,3},{3,2},{4,5},{5,4},{6,7},{7,6},{8,9},{9,8},{10,11... | collective-permute-start | bytes 737288 | tf_op jit(solution)/shard_map/ppermute | solution.py:282
  46.4 1.3 collective-permute-start.3
  47.7 1.2 collective-permute-start.4
  49.4 1.5 %collective-permute-start.6 = (f32[3,8,512]{2,1,0:T(8,128)S(1)}, f32[3,8,512]{2,1,0:T(8,128)S(1)}, u32[]{:S(2)}, u32[]{:S(2)}) collective-permute-start(f32[3,8,512]{2,1,0:T(8,128)S(1)} %collective-permute-done.3.rest_1_), channel_id=1, source_target_pairs={{0,1},{1,0},{2,3},{3,2},{4,5},{5,4},{6,7},{7,6},{8,9},{9,8},{10,11... | collective-permute-start | bytes 147464 | tf_op jit(solution)/shard_map/ppermute | solution.py:282
  51.2 1.9 %collective-permute-start.7 = (f32[3,16,512]{2,1,0:T(8,128)S(1)}, f32[3,16,512]{2,1,0:T(8,128)S(1)}, u32[]{:S(2)}, u32[]{:S(2)}) collective-permute-start(f32[3,16,512]{2,1,0:T(8,128)S(1)} %collective-permute-done.4.rest_2_), channel_id=1, source_target_pairs={{0,1},{1,0},{2,3},{3,2},{4,5},{5,4},{6,7},{7,6},{8,9},{9,8},{10,11... | collective-permute-start | bytes 294920 | tf_op jit(solution)/shard_map/ppermute | solution.py:282
  53.3 2.0 %collective-permute-start.5 = (f32[3,16,512]{2,1,0:T(8,128)S(1)}, f32[3,16,512]{2,1,0:T(8,128)S(1)}, u32[]{:S(2)}, u32[]{:S(2)}) collective-permute-start(f32[3,16,512]{2,1,0:T(8,128)S(1)} %collective-permute-done.2.rest_0_), channel_id=1, source_target_pairs={{0,1},{1,0},{2,3},{3,2},{4,5},{5,4},{6,7},{7,6},{8,9},{9,8},{10,11... | collective-permute-start | bytes 294920 | tf_op jit(solution)/shard_map/ppermute | solution.py:282
  55.3 1.4 copy-done.2
  56.7 1.4 along_x.4
  58.2 2.4 %stage_1.1 = (f32[3,128,1024]{2,1,0:T(8,128)S(1)}, f32[3,128,1024]{2,1,0:T(8,128)S(1)}, f32[3,40,512]{2,1,0:T(8,128)S(1)}, f32[3,40,512]{2,1,0:T(8,128)S(1)}, f32[3,16,1024]{2,1,0:T(8,128)S(1)}) custom-call(s32[2]{0:T(128)S(1)} %pad_add_fusion.flags_ref, f32[3,128,1024]{2,1,0:T(8,128)S(1)} %copy-done.3, f32[3,128,1024]{2,1,0:T(8,128)S(1)} %bitcast.23, ...), custom_call_target="tpu_custom_call" | custom-call | tf_op jit(solution)/shard_map/stage_1/pallas_call | solution.py:127
  60.7 1.5 %collective-permute-done.9 = f32[3,40,512]{2,1,0:T(8,128)S(1)} collective-permute-done((f32[3,40,512]{2,1,0:T(8,128)S(1)}, f32[3,40,512]{2,1,0:T(8,128)S(1)}, u32[]{:S(2)}, u32[]{:S(2)}) %collective-permute-start.9) | collective-permute-done | bytes 245792 | tf_op jit(solution)/shard_map/ppermute | solution.py:282
  62.3 1.9 %collective-permute-start.12 = (f32[3,16,512]{2,1,0:T(8,128)S(1)}, f32[3,16,512]{2,1,0:T(8,128)S(1)}, u32[]{:S(2)}, u32[]{:S(2)}) collective-permute-start(f32[3,16,512]{2,1,0:T(8,128)S(1)} %get-tuple-element.51), channel_id=1, source_target_pairs={{0,6},{1,7},{2,0},{3,1},{4,2},{5,3},{6,4},{7,5},{8,14},{9,15},{10,... | collective-permute-start | bytes 294920 | tf_op jit(solution)/shard_map/ppermute | solution.py:293
  64.6 1.2 collective-permute-start.11
  65.8 3.2 %collective-permute-done.11.rest_1_ = f32[3,8,512]{2,1,0:T(8,128)S(1)} collective-permute-done((f32[3,8,512]{2,1,0:T(8,128)S(1)}, f32[3,8,512]{2,1,0:T(8,128)S(1)}, u32[]{:S(2)}, u32[]{:S(2)}) %collective-permute-start.11) | collective-permute-done | bytes 49184 | tf_op jit(solution)/shard_map/ppermute | solution.py:293
  68.9 2.0 %collective-permute-start.14 = (f32[3,8,512]{2,1,0:T(8,128)S(1)}, f32[3,8,512]{2,1,0:T(8,128)S(1)}, u32[]{:S(2)}, u32[]{:S(2)}) collective-permute-start(f32[3,8,512]{2,1,0:T(8,128)S(1)} %collective-permute-done.11.rest_1_), channel_id=1, source_target_pairs={{0,1},{1,0},{2,3},{3,2},{4,5},{5,4},{6,7},{7,6},{8,9},{9,8},{10,11... | collective-permute-start | bytes 147464 | tf_op jit(solution)/shard_map/ppermute | solution.py:282
  71.4 1.5 %along_x.5 = f32[384,1024]{1,0:T(8,128)S(1)} custom-call(f32[384,1024]{1,0:T(8,128)S(1)} %bitcast.17, bf16[4,512,512]{2,1,0:T(8,128)(2,1)S(1)} %copy-done), custom_call_target="tpu_custom_call" | custom-call | flops 1207959552 | bytes 5242880 | tf_op jit(solution)/shard_map/along_x/pallas_call | solution.py:127
  72.9 2.4 %stage_2.1 = (f32[3,128,1024]{2,1,0:T(8,128)S(1)}, f32[3,128,1024]{2,1,0:T(8,128)S(1)}, f32[3,40,512]{2,1,0:T(8,128)S(1)}, f32[3,40,512]{2,1,0:T(8,128)S(1)}, f32[3,16,1024]{2,1,0:T(8,128)S(1)}) custom-call(s32[2]{0:T(128)S(1)} %pad_add_fusion.flags_ref, f32[3,128,1024]{2,1,0:T(8,128)S(1)} %get-tuple-element.30.state_ref.own_ref, ...), custom_call_target="tpu_custom_call" | custom-call | tf_op jit(solution)/shard_map/stage_2/pallas_call | solution.py:127
  75.5 1.4 collective-permute-done.17
  80.1 4.7 %collective-permute-done.19.rest_1_ = f32[3,8,512]{2,1,0:T(8,128)S(1)} collective-permute-done((f32[3,8,512]{2,1,0:T(8,128)S(1)}, f32[3,8,512]{2,1,0:T(8,128)S(1)}, u32[]{:S(2)}, u32[]{:S(2)}) %collective-permute-start.19) | collective-permute-done | bytes 49184 | tf_op jit(solution)/shard_map/ppermute | solution.py:293
  86.0 1.4 %along_x.6 = f32[384,1024]{1,0:T(8,128)S(1)} custom-call(f32[384,1024]{1,0:T(8,128)S(1)} %bitcast.18, bf16[4,512,512]{2,1,0:T(8,128)(2,1)S(1)} %copy-done), custom_call_target="tpu_custom_call" | custom-call | flops 1207959552 | bytes 5242880 | tf_op jit(solution)/shard_map/along_x/pallas_call | solution.py:127
  87.5 2.4 %stage_3.1 = (f32[3,128,1024]{2,1,0:T(8,128)S(1)}, f32[3,128,1024]{2,1,0:T(8,128)S(1)}, f32[3,128,1024]{2,1,0:T(8,128)S(1)}) custom-call(s32[2]{0:T(128)S(1)} %pad_add_fusion.flags_ref, f32[3,128,1024]{2,1,0:T(8,128)S(1)} %get-tuple-element.34.state_ref, f32[3,128,1024]{2,1,0:T(8,128)S(1)} %bitcast.20, f32[128,1]{1,0:T(8,128)S(1)} %copy.6.turning_ref, ...), custom_call_target="tpu_custom_call" | custom-call | tf_op jit(solution)/shard_map/stage_3/pallas_call | solution.py:127
  89.9 3.2 %collective-permute-start.25 = (f32[3,128,1024]{2,1,0:T(8,128)S(1)}, f32[3,128,1024]{2,1,0:T(8,128)S(1)}, u32[]{:S(2)}, u32[]{:S(2)}) collective-permute-start(f32[3,128,1024]{2,1,0:T(8,128)S(1)} %get-tuple-element.40), channel_id=1, source_target_pairs={{0,8},{8,16},{16,24},{1,9},{9,17},{17,25},{2,10},{10,18},{18,26},{... | collective-permute-start | bytes 4718600 | tf_op jit(solution)/shard_map/ppermute | solution.py:277
  93.1 34.6 %collective-permute-done.25.received_ref = f32[3,128,1024]{2,1,0:T(8,128)S(1)} collective-permute-done((f32[3,128,1024]{2,1,0:T(8,128)S(1)}, f32[3,128,1024]{2,1,0:T(8,128)S(1)}, u32[]{:S(2)}, u32[]{:S(2)}) %collective-permute-start.25) | collective-permute-done | bytes 1572896 | tf_op jit(solution)/shard_map/ppermute | solution.py:277
  127.7 1.2 select_state.3
  131.1 1.5 %collective-permute-start.27 = (f32[3,16,512]{2,1,0:T(8,128)S(1)}, f32[3,16,512]{2,1,0:T(8,128)S(1)}, u32[]{:S(2)}, u32[]{:S(2)}) collective-permute-start(f32[3,16,512]{2,1,0:T(8,128)S(1)} %get-tuple-element.48), channel_id=1, source_target_pairs={{0,2},{1,3},{2,4},{3,5},{4,6},{5,7},{6,0},{7,1},{8,10},{9,11},{10,... | collective-permute-start | bytes 294920 | tf_op jit(solution)/shard_map/ppermute | solution.py:293
  134.3 4.5 %collective-permute-done.28.rest_1_ = f32[3,8,512]{2,1,0:T(8,128)S(1)} collective-permute-done((f32[3,8,512]{2,1,0:T(8,128)S(1)}, f32[3,8,512]{2,1,0:T(8,128)S(1)}, u32[]{:S(2)}, u32[]{:S(2)}) %collective-permute-start.28) | collective-permute-done | bytes 49184 | tf_op jit(solution)/shard_map/ppermute | solution.py:293
  140.0 1.4 along_x.7
  141.5 3.1 %stage_4.1 = f32[3,128,1024]{2,1,0:T(8,128)} custom-call(s32[2]{0:T(128)S(1)} %pad_add_fusion.flags_ref, f32[3,128,1024]{2,1,0:T(8,128)S(1)} %get-tuple-element.42.state_ref, f32[3,128,1024]{2,1,0:T(8,128)S(1)} %bitcast.21, f32[128,1]{1,0:T(8,128)S(1)} %copy.6.turning_ref, f32[3,16,512]{2,1,0:T(8,128)S(1)} %collective-permute-done.27.rest_0_, ...), custom_call_target="tpu_custom_call" | custom-call | tf_op jit(solution)/shard_map/stage_4/pallas_call | solution.py:127
  (80 shorter events, 16.0 us)
Async XLA Ops:
  0.0 37.4 %collective-permute-start = (f32[3,128,1024]{2,1,0:T(8,128)}, f32[3,128,1024]{2,1,0:T(8,128)S(1)}, u32[]{:S(2)}, u32[]{:S(2)}) collective-permute-start(f32[3,128,1024]{2,1,0:T(8,128)} %bitcast.25), channel_id=1, source_target_pairs={{0,8},{8,16},{16,24},{1,9},{9,17},{17,25},{2,10},{10,18},{18,26},{... | collective-permute-start | bytes 4718600 | tf_op jit(solution)/shard_map/ppermute | solution.py:277
  43.7 2.7 %collective-permute-start.1 = (f32[3,40,512]{2,1,0:T(8,128)S(1)}, f32[3,40,512]{2,1,0:T(8,128)S(1)}, u32[]{:S(2)}, u32[]{:S(2)}) collective-permute-start(f32[3,40,512]{2,1,0:T(8,128)S(1)} %get-tuple-element.28), channel_id=1, source_target_pairs={{0,1},{1,0},{2,3},{3,2},{4,5},{5,4},{6,7},{7,6},{8,9},{9,8},{10,11... | collective-permute-start | bytes 737288 | tf_op jit(solution)/shard_map/ppermute | solution.py:282
  45.2 12.9 %collective-permute-start.8 = (f32[3,16,1024]{2,1,0:T(8,128)S(1)}, f32[3,16,1024]{2,1,0:T(8,128)S(1)}, u32[]{:S(2)}, u32[]{:S(2)}) collective-permute-start(f32[3,16,1024]{2,1,0:T(8,128)S(1)} %get-tuple-element.29), channel_id=1, source_target_pairs={{0,1},{1,0},{2,3},{3,2},{4,5},{5,4},{6,7},{7,6},{8,9},{9,8},{10,11... | collective-permute-start | bytes 589832 | tf_op jit(solution)/shard_map/ppermute | solution.py:282
  46.4 3.0 %collective-permute-start.3 = (f32[3,8,512]{2,1,0:T(8,128)S(1)}, f32[3,8,512]{2,1,0:T(8,128)S(1)}, u32[]{:S(2)}, u32[]{:S(2)}) collective-permute-start(f32[3,8,512]{2,1,0:T(8,128)S(1)} %slice.49), channel_id=1, source_target_pairs={{0,4},{1,5},{2,6},{3,7},{4,0},{5,1},{6,2},{7,3},{8,12},{9,13},{10,... | collective-permute-start | bytes 147464 | tf_op jit(solution)/shard_map/ppermute | solution.py:293
  47.7 3.5 %collective-permute-start.4 = (f32[3,16,512]{2,1,0:T(8,128)S(1)}, f32[3,16,512]{2,1,0:T(8,128)S(1)}, u32[]{:S(2)}, u32[]{:S(2)}) collective-permute-start(f32[3,16,512]{2,1,0:T(8,128)S(1)} %get-tuple-element.53), channel_id=1, source_target_pairs={{0,6},{1,7},{2,0},{3,1},{4,2},{5,3},{6,4},{7,5},{8,14},{9,15},{10,... | collective-permute-start | bytes 294920 | tf_op jit(solution)/shard_map/ppermute | solution.py:293
  48.9 4.4 %collective-permute-start.2 = (f32[3,16,512]{2,1,0:T(8,128)S(1)}, f32[3,16,512]{2,1,0:T(8,128)S(1)}, u32[]{:S(2)}, u32[]{:S(2)}) collective-permute-start(f32[3,16,512]{2,1,0:T(8,128)S(1)} %get-tuple-element.54), channel_id=1, source_target_pairs={{0,2},{1,3},{2,4},{3,5},{4,6},{5,7},{6,0},{7,1},{8,10},{9,11},{10,... | collective-permute-start | bytes 294920 | tf_op jit(solution)/shard_map/ppermute | solution.py:293
  49.4 8.7 %collective-permute-start.6 = (f32[3,8,512]{2,1,0:T(8,128)S(1)}, f32[3,8,512]{2,1,0:T(8,128)S(1)}, u32[]{:S(2)}, u32[]{:S(2)}) collective-permute-start(f32[3,8,512]{2,1,0:T(8,128)S(1)} %collective-permute-done.3.rest_1_), channel_id=1, source_target_pairs={{0,1},{1,0},{2,3},{3,2},{4,5},{5,4},{6,7},{7,6},{8,9},{9,8},{10,11... | collective-permute-start | bytes 147464 | tf_op jit(solution)/shard_map/ppermute | solution.py:282
  51.2 7.0 %collective-permute-start.7 = (f32[3,16,512]{2,1,0:T(8,128)S(1)}, f32[3,16,512]{2,1,0:T(8,128)S(1)}, u32[]{:S(2)}, u32[]{:S(2)}) collective-permute-start(f32[3,16,512]{2,1,0:T(8,128)S(1)} %collective-permute-done.4.rest_2_), channel_id=1, source_target_pairs={{0,1},{1,0},{2,3},{3,2},{4,5},{5,4},{6,7},{7,6},{8,9},{9,8},{10,11... | collective-permute-start | bytes 294920 | tf_op jit(solution)/shard_map/ppermute | solution.py:282
  53.3 4.9 %collective-permute-start.5 = (f32[3,16,512]{2,1,0:T(8,128)S(1)}, f32[3,16,512]{2,1,0:T(8,128)S(1)}, u32[]{:S(2)}, u32[]{:S(2)}) collective-permute-start(f32[3,16,512]{2,1,0:T(8,128)S(1)} %collective-permute-done.2.rest_0_), channel_id=1, source_target_pairs={{0,1},{1,0},{2,3},{3,2},{4,5},{5,4},{6,7},{7,6},{8,9},{9,8},{10,11... | collective-permute-start | bytes 294920 | tf_op jit(solution)/shard_map/ppermute | solution.py:282
  62.3 8.6 %collective-permute-start.12 = (f32[3,16,512]{2,1,0:T(8,128)S(1)}, f32[3,16,512]{2,1,0:T(8,128)S(1)}, u32[]{:S(2)}, u32[]{:S(2)}) collective-permute-start(f32[3,16,512]{2,1,0:T(8,128)S(1)} %get-tuple-element.51), channel_id=1, source_target_pairs={{0,6},{1,7},{2,0},{3,1},{4,2},{5,3},{6,4},{7,5},{8,14},{9,15},{10,... | collective-permute-start | bytes 294920 | tf_op jit(solution)/shard_map/ppermute | solution.py:293
  64.2 6.7 %collective-permute-start.10 = (f32[3,16,512]{2,1,0:T(8,128)S(1)}, f32[3,16,512]{2,1,0:T(8,128)S(1)}, u32[]{:S(2)}, u32[]{:S(2)}) collective-permute-start(f32[3,16,512]{2,1,0:T(8,128)S(1)} %get-tuple-element.52), channel_id=1, source_target_pairs={{0,2},{1,3},{2,4},{3,5},{4,6},{5,7},{6,0},{7,1},{8,10},{9,11},{10,... | collective-permute-start | bytes 294920 | tf_op jit(solution)/shard_map/ppermute | solution.py:293
  64.2 8.7 %collective-permute-start.16 = (f32[3,16,1024]{2,1,0:T(8,128)S(1)}, f32[3,16,1024]{2,1,0:T(8,128)S(1)}, u32[]{:S(2)}, u32[]{:S(2)}) collective-permute-start(f32[3,16,1024]{2,1,0:T(8,128)S(1)} %get-tuple-element.33), channel_id=1, source_target_pairs={{0,1},{1,0},{2,3},{3,2},{4,5},{5,4},{6,7},{7,6},{8,9},{9,8},{10,11... | collective-permute-start | bytes 589832 | tf_op jit(solution)/shard_map/ppermute | solution.py:282
  64.6 4.3 %collective-permute-start.11 = (f32[3,8,512]{2,1,0:T(8,128)S(1)}, f32[3,8,512]{2,1,0:T(8,128)S(1)}, u32[]{:S(2)}, u32[]{:S(2)}) collective-permute-start(f32[3,8,512]{2,1,0:T(8,128)S(1)} %slice.52), channel_id=1, source_target_pairs={{0,4},{1,5},{2,6},{3,7},{4,0},{5,1},{6,2},{7,3},{8,12},{9,13},{10,... | collective-permute-start | bytes 147464 | tf_op jit(solution)/shard_map/ppermute | solution.py:293
  68.9 4.0 %collective-permute-start.14 = (f32[3,8,512]{2,1,0:T(8,128)S(1)}, f32[3,8,512]{2,1,0:T(8,128)S(1)}, u32[]{:S(2)}, u32[]{:S(2)}) collective-permute-start(f32[3,8,512]{2,1,0:T(8,128)S(1)} %collective-permute-done.11.rest_1_), channel_id=1, source_target_pairs={{0,1},{1,0},{2,3},{3,2},{4,5},{5,4},{6,7},{7,6},{8,9},{9,8},{10,11... | collective-permute-start | bytes 147464 | tf_op jit(solution)/shard_map/ppermute | solution.py:282
  70.9 2.0 %collective-permute-start.15 = (f32[3,16,512]{2,1,0:T(8,128)S(1)}, f32[3,16,512]{2,1,0:T(8,128)S(1)}, u32[]{:S(2)}, u32[]{:S(2)}) collective-permute-start(f32[3,16,512]{2,1,0:T(8,128)S(1)} %collective-permute-done.12.rest_2_), channel_id=1, source_target_pairs={{0,1},{1,0},{2,3},{3,2},{4,5},{5,4},{6,7},{7,6},{8,9},{9,8},{10,11... | collective-permute-start | bytes 294920 | tf_op jit(solution)/shard_map/ppermute | solution.py:282
  70.9 2.0 %collective-permute-start.13 = (f32[3,16,512]{2,1,0:T(8,128)S(1)}, f32[3,16,512]{2,1,0:T(8,128)S(1)}, u32[]{:S(2)}, u32[]{:S(2)}) collective-permute-start(f32[3,16,512]{2,1,0:T(8,128)S(1)} %collective-permute-done.10.rest_0_), channel_id=1, source_target_pairs={{0,1},{1,0},{2,3},{3,2},{4,5},{5,4},{6,7},{7,6},{8,9},{9,8},{10,11... | collective-permute-start | bytes 294920 | tf_op jit(solution)/shard_map/ppermute | solution.py:282
  77.0 8.5 %collective-permute-start.20 = (f32[3,16,512]{2,1,0:T(8,128)S(1)}, f32[3,16,512]{2,1,0:T(8,128)S(1)}, u32[]{:S(2)}, u32[]{:S(2)}) collective-permute-start(f32[3,16,512]{2,1,0:T(8,128)S(1)} %get-tuple-element.49), channel_id=1, source_target_pairs={{0,6},{1,7},{2,0},{3,1},{4,2},{5,3},{6,4},{7,5},{8,14},{9,15},{10,... | collective-permute-start | bytes 294920 | tf_op jit(solution)/shard_map/ppermute | solution.py:293
  77.8 7.7 %collective-permute-start.18 = (f32[3,16,512]{2,1,0:T(8,128)S(1)}, f32[3,16,512]{2,1,0:T(8,128)S(1)}, u32[]{:S(2)}, u32[]{:S(2)}) collective-permute-start(f32[3,16,512]{2,1,0:T(8,128)S(1)} %get-tuple-element.50), channel_id=1, source_target_pairs={{0,2},{1,3},{2,4},{3,5},{4,6},{5,7},{6,0},{7,1},{8,10},{9,11},{10,... | collective-permute-start | bytes 294920 | tf_op jit(solution)/shard_map/ppermute | solution.py:293
  78.5 9.0 %collective-permute-start.24 = (f32[3,16,1024]{2,1,0:T(8,128)S(1)}, f32[3,16,1024]{2,1,0:T(8,128)S(1)}, u32[]{:S(2)}, u32[]{:S(2)}) collective-permute-start(f32[3,16,1024]{2,1,0:T(8,128)S(1)} %get-tuple-element.37), channel_id=1, source_target_pairs={{0,1},{1,0},{2,3},{3,2},{4,5},{5,4},{6,7},{7,6},{8,9},{9,8},{10,11... | collective-permute-start | bytes 589832 | tf_op jit(solution)/shard_map/ppermute | solution.py:282
  79.2 5.6 %collective-permute-start.19 = (f32[3,8,512]{2,1,0:T(8,128)S(1)}, f32[3,8,512]{2,1,0:T(8,128)S(1)}, u32[]{:S(2)}, u32[]{:S(2)}) collective-permute-start(f32[3,8,512]{2,1,0:T(8,128)S(1)} %slice.55), channel_id=1, source_target_pairs={{0,4},{1,5},{2,6},{3,7},{4,0},{5,1},{6,2},{7,3},{8,12},{9,13},{10,... | collective-permute-start | bytes 147464 | tf_op jit(solution)/shard_map/ppermute | solution.py:293
  84.8 2.6 %collective-permute-start.22 = (f32[3,8,512]{2,1,0:T(8,128)S(1)}, f32[3,8,512]{2,1,0:T(8,128)S(1)}, u32[]{:S(2)}, u32[]{:S(2)}) collective-permute-start(f32[3,8,512]{2,1,0:T(8,128)S(1)} %collective-permute-done.19.rest_1_), channel_id=1, source_target_pairs={{0,1},{1,0},{2,3},{3,2},{4,5},{5,4},{6,7},{7,6},{8,9},{9,8},{10,11... | collective-permute-start | bytes 147464 | tf_op jit(solution)/shard_map/ppermute | solution.py:282
  85.5 2.0 %collective-permute-start.23 = (f32[3,16,512]{2,1,0:T(8,128)S(1)}, f32[3,16,512]{2,1,0:T(8,128)S(1)}, u32[]{:S(2)}, u32[]{:S(2)}) collective-permute-start(f32[3,16,512]{2,1,0:T(8,128)S(1)} %collective-permute-done.20.rest_2_), channel_id=1, source_target_pairs={{0,1},{1,0},{2,3},{3,2},{4,5},{5,4},{6,7},{7,6},{8,9},{9,8},{10,11... | collective-permute-start | bytes 294920 | tf_op jit(solution)/shard_map/ppermute | solution.py:282
  85.5 2.0 %collective-permute-start.21 = (f32[3,16,512]{2,1,0:T(8,128)S(1)}, f32[3,16,512]{2,1,0:T(8,128)S(1)}, u32[]{:S(2)}, u32[]{:S(2)}) collective-permute-start(f32[3,16,512]{2,1,0:T(8,128)S(1)} %collective-permute-done.18.rest_0_), channel_id=1, source_target_pairs={{0,1},{1,0},{2,3},{3,2},{4,5},{5,4},{6,7},{7,6},{8,9},{9,8},{10,11... | collective-permute-start | bytes 294920 | tf_op jit(solution)/shard_map/ppermute | solution.py:282
  89.9 37.9 %collective-permute-start.25 = (f32[3,128,1024]{2,1,0:T(8,128)S(1)}, f32[3,128,1024]{2,1,0:T(8,128)S(1)}, u32[]{:S(2)}, u32[]{:S(2)}) collective-permute-start(f32[3,128,1024]{2,1,0:T(8,128)S(1)} %get-tuple-element.40), channel_id=1, source_target_pairs={{0,8},{8,16},{16,24},{1,9},{9,17},{17,25},{2,10},{10,18},{18,26},{... | collective-permute-start | bytes 4718600 | tf_op jit(solution)/shard_map/ppermute | solution.py:277
  128.9 2.1 %collective-permute-start.26 = (f32[3,40,512]{2,1,0:T(8,128)S(1)}, f32[3,40,512]{2,1,0:T(8,128)S(1)}, u32[]{:S(2)}, u32[]{:S(2)}) collective-permute-start(f32[3,40,512]{2,1,0:T(8,128)S(1)} %get-tuple-element.44), channel_id=1, source_target_pairs={{0,1},{1,0},{2,3},{3,2},{4,5},{5,4},{6,7},{7,6},{8,9},{9,8},{10,11... | collective-permute-start | bytes 737288 | tf_op jit(solution)/shard_map/ppermute | solution.py:282
  131.0 8.4 %collective-permute-start.29 = (f32[3,16,512]{2,1,0:T(8,128)S(1)}, f32[3,16,512]{2,1,0:T(8,128)S(1)}, u32[]{:S(2)}, u32[]{:S(2)}) collective-permute-start(f32[3,16,512]{2,1,0:T(8,128)S(1)} %get-tuple-element.47), channel_id=1, source_target_pairs={{0,6},{1,7},{2,0},{3,1},{4,2},{5,3},{6,4},{7,5},{8,14},{9,15},{10,... | collective-permute-start | bytes 294920 | tf_op jit(solution)/shard_map/ppermute | solution.py:293
  131.1 8.3 %collective-permute-start.27 = (f32[3,16,512]{2,1,0:T(8,128)S(1)}, f32[3,16,512]{2,1,0:T(8,128)S(1)}, u32[]{:S(2)}, u32[]{:S(2)}) collective-permute-start(f32[3,16,512]{2,1,0:T(8,128)S(1)} %get-tuple-element.48), channel_id=1, source_target_pairs={{0,2},{1,3},{2,4},{3,5},{4,6},{5,7},{6,0},{7,1},{8,10},{9,11},{10,... | collective-permute-start | bytes 294920 | tf_op jit(solution)/shard_map/ppermute | solution.py:293
  132.6 8.9 %collective-permute-start.33 = (f32[3,16,1024]{2,1,0:T(8,128)S(1)}, f32[3,16,1024]{2,1,0:T(8,128)S(1)}, u32[]{:S(2)}, u32[]{:S(2)}) collective-permute-start(f32[3,16,1024]{2,1,0:T(8,128)S(1)} %get-tuple-element.45), channel_id=1, source_target_pairs={{0,1},{1,0},{2,3},{3,2},{4,5},{5,4},{6,7},{7,6},{8,9},{9,8},{10,11... | collective-permute-start | bytes 589832 | tf_op jit(solution)/shard_map/ppermute | solution.py:282
  133.5 5.3 %collective-permute-start.28 = (f32[3,8,512]{2,1,0:T(8,128)S(1)}, f32[3,8,512]{2,1,0:T(8,128)S(1)}, u32[]{:S(2)}, u32[]{:S(2)}) collective-permute-start(f32[3,8,512]{2,1,0:T(8,128)S(1)} %slice.58), channel_id=1, source_target_pairs={{0,4},{1,5},{2,6},{3,7},{4,0},{5,1},{6,2},{7,3},{8,12},{9,13},{10,... | collective-permute-start | bytes 147464 | tf_op jit(solution)/shard_map/ppermute | solution.py:293
  138.8 2.6 %collective-permute-start.31 = (f32[3,8,512]{2,1,0:T(8,128)S(1)}, f32[3,8,512]{2,1,0:T(8,128)S(1)}, u32[]{:S(2)}, u32[]{:S(2)}) collective-permute-start(f32[3,8,512]{2,1,0:T(8,128)S(1)} %collective-permute-done.28.rest_1_), channel_id=1, source_target_pairs={{0,1},{1,0},{2,3},{3,2},{4,5},{5,4},{6,7},{7,6},{8,9},{9,8},{10,11... | collective-permute-start | bytes 147464 | tf_op jit(solution)/shard_map/ppermute | solution.py:282
  139.5 2.0 %collective-permute-start.32 = (f32[3,16,512]{2,1,0:T(8,128)S(1)}, f32[3,16,512]{2,1,0:T(8,128)S(1)}, u32[]{:S(2)}, u32[]{:S(2)}) collective-permute-start(f32[3,16,512]{2,1,0:T(8,128)S(1)} %collective-permute-done.29.rest_2_), channel_id=1, source_target_pairs={{0,1},{1,0},{2,3},{3,2},{4,5},{5,4},{6,7},{7,6},{8,9},{9,8},{10,11... | collective-permute-start | bytes 294920 | tf_op jit(solution)/shard_map/ppermute | solution.py:282
  139.5 2.0 %collective-permute-start.30 = (f32[3,16,512]{2,1,0:T(8,128)S(1)}, f32[3,16,512]{2,1,0:T(8,128)S(1)}, u32[]{:S(2)}, u32[]{:S(2)}) collective-permute-start(f32[3,16,512]{2,1,0:T(8,128)S(1)} %collective-permute-done.27.rest_0_), channel_id=1, source_target_pairs={{0,1},{1,0},{2,3},{3,2},{4,5},{5,4},{6,7},{7,6},{8,9},{9,8},{10,11... | collective-permute-start | bytes 294920 | tf_op jit(solution)/shard_map/ppermute | solution.py:282
  (11 other events, 40.9 us)

commit v3 on v2

v3 whole, which is shorter than its diff:
```python
import functools
import math

import jax
import jax.numpy as jnp
import ml_dtypes
import numpy as np
from jax import lax
from jax.experimental import pallas as pl
from jax.experimental.pallas import tpu as pltpu
from jax.sharding import PartitionSpec as P

SWEEPS = 2
STEP_LENGTH = 0.001
HALF_STEP = 0.5 * STEP_LENGTH
GRAVITY = 1.0
CORRECT_FIRST = (5.0 / 24.0 - 0.5, 8.0 / 24.0, -1.0 / 24.0)
CORRECT_SECOND = (-1.0 / 24.0, 8.0 / 24.0 - 0.5, 5.0 / 24.0)
TOLERANCE = 1e-8
ROWS = 8
KERNEL_BYTES = 8 * 2**20
KERNEL_FLOPS = 10**10
F32 = jnp.float32
BF16 = jnp.bfloat16


def kernel_values(length):
    values = np.zeros(length)
    for j in range(1, length):
        values[j] = (0.5 if j % 2 == 0 else -0.5) / math.tan(math.pi * j / length)
    values[length // 2] = 0.0
    return values


def toeplitz(values, rows, cols, offset):
    index = np.arange(rows)[:, None] - np.arange(cols)[None, :] + offset
    return values[index % len(values)]


def cross_factors(block, tolerance):
    rest = block.copy()
    lefts, rights = [], []
    while True:
        at = int(np.argmax(np.abs(rest)))
        i, j = divmod(at, rest.shape[1])
        pivot = rest[i, j]
        small = abs(pivot) <= tolerance
        if (small and lefts and len(lefts) % 8 == 0) or len(lefts) == block.shape[0]:
            break
        if abs(pivot) == 0.0:
            left, right = np.zeros(rest.shape[0]), np.zeros(rest.shape[1])
        else:
            left, right = rest[:, j] / pivot, rest[i, :].copy()
        lefts.append(left)
        rights.append(right)
        rest = rest - left[:, None] * right[None, :]
    return np.stack(lefts, axis=1), np.stack(rights, axis=0)


def two_parts(table):
    high = table.astype(ml_dtypes.bfloat16)
    low = (table - high.astype(np.float64)).astype(ml_dtypes.bfloat16)
    return high, low


def pad_rows(table, multiple):
    extra = -table.shape[0] % multiple
    return np.pad(table, ((0, extra), (0, 0)))


def x_tables(length):
    values = kernel_values(length)
    half = length // 2
    near = toeplitz(values, half, half, 0).T
    far = toeplitz(values, half, half, half).T
    plus = two_parts(0.5 * (near + far))
    minus = two_parts(0.5 * (near - far))
    return np.stack([plus[0], plus[1], minus[0], minus[1]])


@functools.lru_cache(maxsize=None)
def y_tables(length, devices):
    rows = length // devices
    pair = 2 * rows
    pairs = devices // 2
    values = kernel_values(length)
    tolerance = TOLERANCE * float(np.max(np.abs(values)))
    factors = [cross_factors(toeplitz(values, pair, pair, d * pair), tolerance) for d in range(1, pairs)]
    ranks = tuple(f[0].shape[1] for f in factors)
    mates = [cross_factors(toeplitz(values, rows, rows, rows if k == 0 else -rows), tolerance) for k in range(2)]
    mate_rank = max(m[0].shape[1] for m in mates)
    send, apply = [], []
    for k in range(2):
        span = slice(k * rows, (k + 1) * rows)
        to_mate = np.pad(mates[k][1], ((0, mate_rank - mates[k][1].shape[0]), (0, 0)))
        from_mate = np.pad(mates[1 - k][0], ((0, 0), (0, mate_rank - mates[1 - k][0].shape[1])))
        down = pad_rows(np.concatenate([f[1][:, span] for f in factors] + [to_mate], axis=0), 16)
        send.append(np.concatenate(two_parts(down), axis=0))
        own = pad_rows(toeplitz(values, rows, rows, 0).T, 16).T
        up = np.concatenate([own] + [f[0][span] for f in factors] + [from_mate], axis=1)
        up = pad_rows(up.T, 16).T
        apply.append(np.concatenate(two_parts(up), axis=0))
    return ranks, mate_rank, np.stack(send), np.stack(apply)


COST = pl.CostEstimate(flops=KERNEL_FLOPS, transcendentals=0, bytes_accessed=2**20)


def parts_of(value):
    high = value.astype(BF16)
    return high, (value - high.astype(F32)).astype(BF16)


def dot(left, right):
    return jnp.dot(left, right, preferred_element_type=F32)


def product(stacked, high, low):
    count = stacked.shape[0] // 2
    both = dot(stacked, high)
    return both[:count] + both[count:] + dot(stacked[:count], low)


VMEM = pl.BlockSpec(memory_space=pltpu.VMEM)
SMEM = pl.BlockSpec(memory_space=pltpu.SMEM)
ANY = pl.BlockSpec(memory_space=pl.ANY)


def on_chip_call(body, operands, shapes, scalars=1, keep=True, **options):
    held = [pltpu.with_memory_space_constraint(a, pltpu.VMEM) for a in operands[scalars:]]
    outs = [pltpu.VMEM(s.shape, s.dtype) for s in shapes] if keep else shapes
    return pl.pallas_call(
        body,
        in_specs=[SMEM] * scalars + [VMEM] * len(held),
        out_specs=[VMEM] * len(outs),
        out_shape=outs,
        compiler_params=pltpu.CompilerParams(vmem_limit_bytes=KERNEL_BYTES),
        cost_estimate=COST,
        **options,
    )(*operands[:scalars], *held)


def x_kernel(theirs_ref, mine_ref, table_ref, grad_theirs_ref, grad_mine_ref):
    theirs, mine = theirs_ref[...], mine_ref[...]

    def folded(total, at):
        high, low = parts_of(total)
        return dot(high, table_ref[at]) + dot(low, table_ref[at]) + dot(high, table_ref[at + 1])

    even = folded(mine + theirs, 0)
    odd = folded(mine - theirs, 2)
    grad_mine_ref[...] = even + odd
    grad_theirs_ref[...] = even - odd


def along_x(theirs, mine, table):
    fields, rows, half = mine.shape
    flat = [a.reshape(fields * rows, half) for a in (theirs, mine)]
    shape = jax.ShapeDtypeStruct(flat[0].shape, F32)
    grads = on_chip_call(x_kernel, [*flat, table], [shape, shape], scalars=0, name="along_x")
    return [g.reshape(mine.shape) for g in grads]


class Plan:
    def __init__(self, rows, length, ranks, mate_rank):
        self.rows, self.length, self.half = rows, length, length // 2
        self.ranks, self.mate_rank, self.total = ranks, mate_rank, sum(ranks)
        self.state = jax.ShapeDtypeStruct((3, rows, self.half), F32)
        self.whole = jax.ShapeDtypeStruct((3, rows, length), F32)
        self.moments = [jax.ShapeDtypeStruct((3, self.total + mate_rank, self.half), F32)]

    def columns(self, flags_ref, mine):
        member = flags_ref[0]
        at = member if mine else 1 - member
        return pl.ds(pl.multiple_of(at * self.half, 128), self.half)

    def emit_moments(self, next_ref, send_ref, moments_ref):
        for f in range(3):
            found = product(send_ref[...], *parts_of(next_ref[f]))
            moments_ref[f] = found[: self.total + self.mate_rank]

    def y_gradient(self, f, state_ref, pair_refs, mate_ref, apply_ref):
        pieces = [state_ref[f]]
        if self.rows % 16:
            pieces.append(jnp.zeros((-self.rows % 16, self.half), F32))
        pieces += [ref[f] for ref in pair_refs]
        pieces.append(mate_ref[f, mate_ref.shape[1] - self.mate_rank :])
        width = apply_ref.shape[1] - sum(p.shape[0] for p in pieces)
        if width:
            pieces.append(jnp.zeros((width, self.half), F32))
        return product(apply_ref[...], *parts_of(jnp.concatenate(pieces, axis=0)))


def tendency_rows(h, u, v, gx, gy, turning):
    rate_h = -(u * gx[0] + v * gy[0]) - (1.0 + h) * (gx[1] + gy[2])
    rate_u = -(u * gx[1] + v * gy[1]) + turning * v - GRAVITY * gx[0]
    rate_v = -(u * gx[2] + v * gy[2]) - turning * u - GRAVITY * gy[0]
    return rate_h, rate_u, rate_v


def enter_call(plan, flags, state, received, send):
    sources = [state, *received]

    def body(flags_ref, own_ref, *refs):
        received_refs, (send_ref, *outs) = refs[: len(received)], refs[len(received) :]
        nexts, moments, arrived = outs[0:4:2], outs[1:4:2], outs[-1]

        def copy(source_ref, at):
            cols = plan.columns(flags_ref, at == 1)
            return pltpu.make_async_copy(source_ref.at[:, :, cols], nexts[at], arrived.at[at])

        def start(source_ref):
            for at in range(2):
                copy(source_ref, at).start()

        if received:
            pl.when(flags_ref[1] == 0)(lambda: start(own_ref))
            pl.when(flags_ref[1] != 0)(lambda: start(received_refs[0]))
        else:
            start(own_ref)
        for at in range(2):
            copy(own_ref, at).wait()
            plan.emit_moments(nexts[at], send_ref, moments[at])

    shapes = [plan.state, *plan.moments] * 2
    return pl.pallas_call(
        body,
        in_specs=[SMEM] + [ANY] * len(sources) + [VMEM],
        out_specs=[VMEM] * 4,
        out_shape=[pltpu.VMEM(s.shape, s.dtype) for s in shapes],
        scratch_shapes=[pltpu.SemaphoreType.DMA((2,))],
        compiler_params=pltpu.CompilerParams(vmem_limit_bytes=KERNEL_BYTES),
        cost_estimate=COST,
        name="enter",
    )(flags, *sources, pltpu.with_memory_space_constraint(send, pltpu.VMEM))


def restart_call(plan, flags, received, second, node_one, added, send):
    extra = list(second)
    fields = len(received)

    def body(flags_ref, *refs):
        received_refs, (node_ref, added_ref, *rest) = refs[:fields], refs[fields:]
        send_ref, next_ref, moments_ref = rest[len(extra) :]
        for f in range(3):
            value = received_refs[f][...]
            if extra:
                value = jnp.where(flags_ref[1] == 1, rest[f][...], value)
            next_ref[f] = jnp.where(flags_ref[1] == 0, node_ref[f], value) + added_ref[f]
        plan.emit_moments(next_ref, send_ref, moments_ref)

    operands = [flags, *received, node_one, added, *extra, send]
    return on_chip_call(body, operands, [plan.state, *plan.moments], name="restart")


def stage_call(plan, kind, state, grad_x, pair_in, mate_in, turning, apply, send=None, others=()):
    count = len(pair_in)
    split = kind in ("lead", "correct")

    def body(state_ref, grad_ref, turning_ref, *rest):
        pair_refs, (mate_ref, apply_ref), rest = rest[:count], rest[count : count + 2], rest[count + 2 :]
        other_refs, rest = rest[: len(others)], rest[len(others) :]
        if send is not None:
            send_ref, rest = rest[0], rest[1:]
        grad_y = rest[-1]
        for f in range(3):
            grad_y[f] = plan.y_gradient(f, state_ref, pair_refs, mate_ref, apply_ref)
        for start in range(0, plan.rows, ROWS):
            at = slice(start, start + ROWS)
            now = [state_ref[f, at] for f in range(3)]
            rates = tendency_rows(
                *now, [grad_ref[f, at] for f in range(3)], [grad_y[f, at] for f in range(3)], turning_ref[at]
            )
            for f in range(3):
                ahead = now[f] + HALF_STEP * rates[f]
                if kind == "end":
                    ahead = ahead + other_refs[0][f, at]
                if split:
                    rest[f][at] = ahead
                else:
                    rest[0][f, at] = ahead
                if kind == "keep":
                    rest[1][f, at] = rates[f]
                if kind == "correct":
                    olds = (other_refs[0][f, at], other_refs[1][f, at], rates[f])
                    for out, weights in ((rest[-3], CORRECT_FIRST), (rest[-2], CORRECT_SECOND)):
                        out[f, at] = sum((STEP_LENGTH * w) * r for w, r in zip(weights, olds))
        if send is not None:
            plan.emit_moments(rest[0], send_ref, rest[-2])

    operands = [state, grad_x, turning, *pair_in, mate_in, apply, *others]
    shapes = [plan.state] * {"move": 1, "keep": 2, "lead": 0, "correct": 2, "end": 1}[kind]
    if split:
        shapes = [jax.ShapeDtypeStruct(plan.state.shape[1:], F32)] * 3 + shapes
    if send is not None:
        operands.append(send)
        shapes += plan.moments
    return on_chip_call(
        body,
        operands,
        shapes,
        scalars=0,
        scratch_shapes=[pltpu.VMEM((3, plan.rows, plan.half), F32)],
        name=f"stage_{kind}",
    )


def join_call(plan, flags, theirs, mine):
    def body(flags_ref, theirs_ref, mine_ref, out_ref, done):
        copies = [
            pltpu.make_async_copy(ref, out_ref.at[:, :, plan.columns(flags_ref, at == 1)], done.at[at])
            for at, ref in enumerate((theirs_ref, mine_ref))
        ]
        for copy in copies:
            copy.start()
        for copy in copies:
            copy.wait()

    held = [pltpu.with_memory_space_constraint(a, pltpu.VMEM) for a in (theirs, mine)]
    return pl.pallas_call(
        body,
        in_specs=[SMEM, VMEM, VMEM],
        out_specs=ANY,
        out_shape=plan.whole,
        scratch_shapes=[pltpu.SemaphoreType.DMA((2,))],
        compiler_params=pltpu.CompilerParams(vmem_limit_bytes=KERNEL_BYTES),
        name="join",
    )(flags, *held)


def ahead_in_time(array, by):
    size = lax.axis_size("tm")
    return lax.ppermute(array, "tm", [(i, i + by) for i in range(size - by)])


def mate_swap(array):
    size = lax.axis_size("grid")
    return lax.ppermute(array, "grid", [(i, i ^ 1) for i in range(size)])


def exchange(plan, theirs, mine):
    size = lax.axis_size("grid")
    from_mate = mate_swap(theirs)
    mate_first = mate_swap(mine[:, plan.total :])
    merged = mine[:, : plan.total] + from_mate[:, : plan.total]
    first, start = [], 0
    for d, rank in enumerate(plan.ranks, 1):
        part = merged[:, start : start + rank]
        start += rank
        first.append(lax.ppermute(part, "grid", [(i, ((i + 2 * d) % size) ^ 1) for i in range(size)]))
    return (first, mate_first), ([mate_swap(part) for part in first], from_mate)


def per_device(starts, coriolis):
    own = starts[0]
    _, rows, length = own.shape
    ranks, mate_rank, send_tables, apply_tables = y_tables(length, lax.axis_size("grid"))
    plan = Plan(rows, length, ranks, mate_rank)
    member = lax.axis_index("grid") % 2
    flags = jnp.stack([member, lax.axis_index("tm")]).astype(jnp.int32)
    table = jnp.asarray(x_tables(length))
    send = lax.dynamic_index_in_dim(jnp.asarray(send_tables), member, 0, keepdims=False)
    apply = lax.dynamic_index_in_dim(jnp.asarray(apply_tables), member, 0, keepdims=False)
    turning = coriolis[:, None]

    def stage(kind, states, moments, others=((), ()), sends=True, only_first=False):
        received = exchange(plan, *moments)
        grads = along_x(*states, table)
        results = []
        for at in range(1 if only_first else 2):
            pair_in, mate_in = received[at]
            results.append(
                stage_call(
                    plan, kind, states[at], grads[at], pair_in, mate_in, turning, apply, send if sends else None, others[at]
                )
            )
        if not sends:
            return results
        return *zip(*[r[:-1] for r in results]), [r[-1] for r in results]

    def enter(received):
        theirs, theirs_moments, mine, mine_moments = enter_call(plan, flags, own, received, send)
        return [theirs, mine], [theirs_moments, mine_moments]

    before = [ahead_in_time(own, 1)]
    states, moments = enter([])
    states, moments = stage("move", states, moments)
    states, moments = stage("move", states, moments)
    (lead,) = stage("lead", states, moments, sends=False, only_first=True)
    far = [ahead_in_time(field, 2) for field in lead]

    *before, _ = lax.optimization_barrier((*before, lead[0]))
    states, moments = enter(before)
    nodes_one, rates_zero, moments = stage("keep", states, moments)
    states, rates_one, moments = stage("keep", nodes_one, moments)
    moments[0], far[0] = lax.optimization_barrier((moments[0], far[0]))
    theirs, mine = stage("correct", states, moments, list(zip(rates_zero, rates_one)), sends=False)
    near = [ahead_in_time(field, 1) for field in mine[:3]]

    results = [
        restart_call(plan, flags, far, theirs[:3], nodes_one[0], theirs[3], send),
        restart_call(plan, flags, near, (), nodes_one[1], mine[3], send),
    ]
    ends = stage("end", [r[0] for r in results], [r[1] for r in results], ((theirs[4],), (mine[4],)), sends=False)
    return join_call(plan, flags, ends[0][0], ends[1][0])[None]


def solution(mesh):
    return jax.shard_map(
        per_device,
        mesh=mesh,
        in_specs=(P("tm", None, "grid", None), P("grid")),
        out_specs=P("tm", None, "grid", None),
        check_vma=False,
    )
```

time: 145 us -> 119 us (0.82)
  waiting for transfers between devices: 86.2 us -> 28.8 us
  starting transfers between devices: 31.9 us -> 51.5 us
  Pallas kernels: 18.5 us -> 28.8 us
    ppermute x14 -> x28, waiting for transfers between devices: 80.9 us -> 28.3 us  [the longest x7 16.5 us: ahead_in_time(): return lax.ppermute(array, 'tm', [(i, i + by) for i in range(size - by)])]
    ppermute x14 -> x28, starting transfers between devices: 16.9 us -> 40 us  [the longest x21 25.5 us: exchange(): lax.ppermute(part, 'grid', [(i, (i + 2 * d) % size ^ 1) for i in range(si...]
    pallas_call x10 -> x22, Pallas kernels: 18.5 us -> 24.4 us  [on_chip_call(): pl.pallas_call(body, in_specs=[SMEM] * scalars + [VMEM] * len(held), out_...]
    ppermute x20 -> x32, waiting for transfers between devices: 5.26 us -> 0.55 us  [mate_swap(): return lax.ppermute(array, 'grid', [(i, i ^ 1) for i in range(size)])]
    pallas_call x0 -> x3, Pallas kernels: none -> 4.38 us  [the longest x2 2.68 us: enter_call(): pl.pallas_call(body, in_specs=[SMEM] + [ANY] * len(sources) + [VMEM], out...]
    ppermute x20 -> x32, starting transfers between devices: 15 us -> 11.5 us  [mate_swap(): return lax.ppermute(array, 'grid', [(i, i ^ 1) for i in range(size)])]
    unnamed x18 -> x24, local copies, waits for them, and re-layouts: 6.52 us -> 5.3 us
  transfers between devices with their start and end apart: 34 -> 60, of which waited for: 12 -> 16; matrix products, arithmetic and copies ran while one was open for 1% -> 2% of each run, Pallas kernels for 4% -> 21%
where the time goes in v3:
time: 119 us; the launch traced here: 117 us
  starting transfers between devices  51.5 us (43%)
  Pallas kernels  28.8 us (24%)
  waiting for transfers between devices  28.8 us (24%)
  local copies, waits for them, and re-layouts  7.1 us (6%)
    ppermute x21, starting transfers between devices, exchange(): lax.ppermute(part, 'grid', [(i, (i + 2 * d) % size ^ 1) for i in range(si...  25.5 us
    pallas_call x22, Pallas kernels, on_chip_call(): pl.pallas_call(body, in_specs=[SMEM] * scalars + [VMEM] * len(held), out_...  24.4 us
    ppermute x7, waiting for transfers between devices, ahead_in_time(): return lax.ppermute(array, 'tm', [(i, i + by) for i in range(size - by)])  16.5 us
    ppermute x7, starting transfers between devices, ahead_in_time(): return lax.ppermute(array, 'tm', [(i, i + by) for i in range(size - by)])  14.5 us
    ppermute x21, waiting for transfers between devices, exchange(): lax.ppermute(part, 'grid', [(i, (i + 2 * d) % size ^ 1) for i in range(si...  11.8 us
    ppermute x32, starting transfers between devices, mate_swap(): return lax.ppermute(array, 'grid', [(i, i ^ 1) for i in range(size)])  11.5 us
    unnamed x24, local copies, waits for them, and re-layouts  5.3 us
    pallas_call x2, Pallas kernels, enter_call(): pl.pallas_call(body, in_specs=[SMEM] + [ANY] * len(sources) + [VMEM], out...  2.68 us
  transfers between devices with their start and end apart: 60, of which 16 were waited for; matrix products, arithmetic and copies ran while one was open for 2% of the time, Pallas kernels for 21%

profile of v3, /device:TPU:9, one launch (start us, length us, event | category | flops | bytes accessed | tf_op | source)
XLA Modules:
  0.0 117.4 jit_solution(10472791179887823790)
XLA Ops:
  0.0 3.2 %collective-permute-start = (f32[3,128,1024]{2,1,0:T(8,128)}, f32[3,128,1024]{2,1,0:T(8,128)S(1)}, u32[]{:S(2)}, u32[]{:S(2)}) collective-permute-start(f32[3,128,1024]{2,1,0:T(8,128)} %bitcast.36), channel_id=1, source_target_pairs={{0,8},{8,16},{16,24},{1,9},{9,17},{17,25},{2,10},{10,18},{18,26},{... | collective-permute-start | bytes 4718600 | tf_op jit(solution)/shard_map/ppermute | solution.py:333
  4.1 1.4 %copy-done = f32[1,3,128,1024]{3,2,1,0:T(8,128)S(1)} copy-done((f32[1,3,128,1024]{3,2,1,0:T(8,128)S(1)}, f32[1,3,128,1024]{3,2,1,0:T(8,128)}, u32[]{:S(2)}) %copy-start) | copy-done | bytes 1572888
  8.0 1.5 %along_x.7 = (f32[384,512]{1,0:T(8,128)S(1)}, f32[384,512]{1,0:T(8,128)S(1)}) custom-call(f32[384,512]{1,0:T(8,128)S(1)} %bitcast.52, f32[384,512]{1,0:T(8,128)S(1)} %bitcast.45, bf16[4,512,512]{2,1,0:T(8,128)(2,1)S(1)} %copy-done.2), custom_call_target="tpu_custom_call" | custom-call | flops 10000000000 | bytes 1048576 | tf_op jit(solution)/shard_map/along_x/pallas_call | solution.py:132
  11.1 1.6 %collective-permute-start.2 = (f32[3,16,512]{2,1,0:T(8,128)}, f32[3,16,512]{2,1,0:T(8,128)S(1)}, u32[]{:S(2)}, u32[]{:S(2)}) collective-permute-start(f32[3,16,512]{2,1,0:T(8,128)} %get-tuple-element.140), channel_id=1, source_target_pairs={{0,3},{1,2},{2,5},{3,4},{4,7},{5,6},{6,1},{7,0},{8,11},{9,10},{10,... | collective-permute-start | bytes 294920 | tf_op jit(solution)/shard_map/ppermute | solution.py:350
  13.8 1.5 %collective-permute-start.4 = (f32[3,16,512]{2,1,0:T(8,128)S(1)}, f32[3,16,512]{2,1,0:T(8,128)S(1)}, u32[]{:S(2)}, u32[]{:S(2)}) collective-permute-start(f32[3,16,512]{2,1,0:T(8,128)S(1)} %get-tuple-element.139), channel_id=1, source_target_pairs={{0,7},{1,6},{2,1},{3,0},{4,3},{5,2},{6,5},{7,4},{8,15},{9,14},{10,... | collective-permute-start | bytes 294920 | tf_op jit(solution)/shard_map/ppermute | solution.py:350
  15.5 2.9 %collective-permute-done.3.rest_1_ = f32[3,8,512]{2,1,0:T(8,128)S(1)} collective-permute-done((f32[3,8,512]{2,1,0:T(8,128)S(1)}, f32[3,8,512]{2,1,0:T(8,128)S(1)}, u32[]{:S(2)}, u32[]{:S(2)}) %collective-permute-start.3) | collective-permute-done | bytes 49184 | tf_op jit(solution)/shard_map/ppermute | solution.py:350
  26.8 1.4 %collective-permute-start.12 = (f32[3,16,512]{2,1,0:T(8,128)S(1)}, f32[3,16,512]{2,1,0:T(8,128)S(1)}, u32[]{:S(2)}, u32[]{:S(2)}) collective-permute-start(f32[3,16,512]{2,1,0:T(8,128)S(1)} %get-tuple-element.137), channel_id=1, source_target_pairs={{0,7},{1,6},{2,1},{3,0},{4,3},{5,2},{6,5},{7,4},{8,15},{9,14},{10,... | collective-permute-start | bytes 294920 | tf_op jit(solution)/shard_map/ppermute | solution.py:350
  28.3 1.5 %along_x.8 = (f32[384,512]{1,0:T(8,128)S(1)}, f32[384,512]{1,0:T(8,128)S(1)}) custom-call(f32[384,512]{1,0:T(8,128)S(1)} %bitcast.47, f32[384,512]{1,0:T(8,128)S(1)} %bitcast.46, bf16[4,512,512]{2,1,0:T(8,128)(2,1)S(1)} %copy-done.3), custom_call_target="tpu_custom_call" | custom-call | flops 10000000000 | bytes 1048576 | tf_op jit(solution)/shard_map/along_x/pallas_call | solution.py:132
  29.7 2.0 %collective-permute-done.11.rest_1_ = f32[3,8,512]{2,1,0:T(8,128)S(1)} collective-permute-done((f32[3,8,512]{2,1,0:T(8,128)S(1)}, f32[3,8,512]{2,1,0:T(8,128)S(1)}, u32[]{:S(2)}, u32[]{:S(2)}) %collective-permute-start.11) | collective-permute-done | bytes 49184 | tf_op jit(solution)/shard_map/ppermute | solution.py:350
  37.3 1.7 %collective-permute-start.20 = (f32[3,16,512]{2,1,0:T(8,128)S(1)}, f32[3,16,512]{2,1,0:T(8,128)S(1)}, u32[]{:S(2)}, u32[]{:S(2)}) collective-permute-start(f32[3,16,512]{2,1,0:T(8,128)S(1)} %get-tuple-element.135), channel_id=1, source_target_pairs={{0,7},{1,6},{2,1},{3,0},{4,3},{5,2},{6,5},{7,4},{8,15},{9,14},{10,... | collective-permute-start | bytes 294920 | tf_op jit(solution)/shard_map/ppermute | solution.py:350
  38.9 2.3 %along_x.9 = (f32[384,512]{1,0:T(8,128)S(1)}, f32[384,512]{1,0:T(8,128)}) custom-call(f32[384,512]{1,0:T(8,128)S(1)} %bitcast.49, f32[384,512]{1,0:T(8,128)S(1)} %bitcast.60, bf16[4,512,512]{2,1,0:T(8,128)(2,1)S(1)} %copy-done.3), custom_call_target="tpu_custom_call" | custom-call | flops 10000000000 | bytes 1048576 | tf_op jit(solution)/shard_map/along_x/pallas_call | solution.py:132
  44.1 1.3 %enter.3 = (f32[3,128,512]{2,1,0:T(8,128)S(1)}, f32[3,56,512]{2,1,0:T(8,128)S(1)}, f32[3,128,512]{2,1,0:T(8,128)S(1)}, f32[3,56,512]{2,1,0:T(8,128)S(1)}) custom-call(s32[2]{0:T(128)S(1)} %pad_add_fusion.flags_ref, f32[3,128,1024]{2,1,0:T(8,128)S(1)} %bitcast.38, f32[3,128,1024]{2,1,0:T(8,128)S(1)} %collective-permute-done.refs_0_, ...), custom_call_target="tpu_custom_call" | custom-call | flops 10000000000 | bytes 1048576 | tf_op jit(solution)/shard_map/enter/pallas_call | solution.py:226
  45.8 2.0 %collective-permute-start.35 = (f32[128,512]{1,0:T(8,128)S(1)}, f32[128,512]{1,0:T(8,128)S(1)}, u32[]{:S(2)}, u32[]{:S(2)}) collective-permute-start(f32[128,512]{1,0:T(8,128)S(1)} %get-tuple-element.83), channel_id=1, source_target_pairs={{0,16},{8,24},{1,17},{9,25},{2,18},{10,26},{3,19},{11,27},{4,20},{... | collective-permute-start | bytes 786440 | tf_op jit(solution)/shard_map/ppermute | solution.py:333
  51.7 1.4 %along_x.10 = (f32[384,512]{1,0:T(8,128)S(1)}, f32[384,512]{1,0:T(8,128)S(1)}) custom-call(f32[384,512]{1,0:T(8,128)S(1)} %bitcast.51, f32[384,512]{1,0:T(8,128)S(1)} %bitcast.44, bf16[4,512,512]{2,1,0:T(8,128)(2,1)S(1)} %copy-done.3), custom_call_target="tpu_custom_call" | custom-call | flops 10000000000 | bytes 1048576 | tf_op jit(solution)/shard_map/along_x/pallas_call | solution.py:132
  53.1 2.1 %collective-permute-done.24.rest_1_ = f32[3,8,512]{2,1,0:T(8,128)S(1)} collective-permute-done((f32[3,8,512]{2,1,0:T(8,128)S(1)}, f32[3,8,512]{2,1,0:T(8,128)S(1)}, u32[]{:S(2)}, u32[]{:S(2)}) %collective-permute-start.24) | collective-permute-done | bytes 49184 | tf_op jit(solution)/shard_map/ppermute | solution.py:350
  60.7 1.6 %collective-permute-start.33 = (f32[3,16,512]{2,1,0:T(8,128)S(1)}, f32[3,16,512]{2,1,0:T(8,128)S(1)}, u32[]{:S(2)}, u32[]{:S(2)}) collective-permute-start(f32[3,16,512]{2,1,0:T(8,128)S(1)} %get-tuple-element.131), channel_id=1, source_target_pairs={{0,7},{1,6},{2,1},{3,0},{4,3},{5,2},{6,5},{7,4},{8,15},{9,14},{10,... | collective-permute-start | bytes 294920 | tf_op jit(solution)/shard_map/ppermute | solution.py:350
  62.3 1.4 %along_x.11 = (f32[384,512]{1,0:T(8,128)S(1)}, f32[384,512]{1,0:T(8,128)S(1)}) custom-call(f32[384,512]{1,0:T(8,128)S(1)} %bitcast.40, f32[384,512]{1,0:T(8,128)S(1)} %bitcast.39, bf16[4,512,512]{2,1,0:T(8,128)(2,1)S(1)} %copy-done.3), custom_call_target="tpu_custom_call" | custom-call | flops 10000000000 | bytes 1048576 | tf_op jit(solution)/shard_map/along_x/pallas_call | solution.py:132
  63.7 1.5 %collective-permute-start.36 = (f32[128,512]{1,0:T(8,128)S(1)}, f32[128,512]{1,0:T(8,128)S(1)}, u32[]{:S(2)}, u32[]{:S(2)}) collective-permute-start(f32[128,512]{1,0:T(8,128)S(1)} %get-tuple-element.98), channel_id=1, source_target_pairs={{0,16},{8,24},{1,17},{9,25},{2,18},{10,26},{3,19},{11,27},{4,20},{... | collective-permute-start | bytes 786440 | tf_op jit(solution)/shard_map/ppermute | solution.py:333
  71.3 1.4 %collective-permute-start.44 = (f32[3,16,512]{2,1,0:T(8,128)S(1)}, f32[3,16,512]{2,1,0:T(8,128)S(1)}, u32[]{:S(2)}, u32[]{:S(2)}) collective-permute-start(f32[3,16,512]{2,1,0:T(8,128)S(1)} %get-tuple-element.129), channel_id=1, source_target_pairs={{0,7},{1,6},{2,1},{3,0},{4,3},{5,2},{6,5},{7,4},{8,15},{9,14},{10,... | collective-permute-start | bytes 294920 | tf_op jit(solution)/shard_map/ppermute | solution.py:350
  72.8 1.4 %along_x.12 = (f32[384,512]{1,0:T(8,128)S(1)}, f32[384,512]{1,0:T(8,128)S(1)}) custom-call(f32[384,512]{1,0:T(8,128)S(1)} %bitcast.41, f32[384,512]{1,0:T(8,128)S(1)} %bitcast.42, bf16[4,512,512]{2,1,0:T(8,128)(2,1)S(1)} %copy-done.3), custom_call_target="tpu_custom_call" | custom-call | flops 10000000000 | bytes 1048576 | tf_op jit(solution)/shard_map/along_x/pallas_call | solution.py:132
  74.2 1.5 %collective-permute-start.37 = (f32[128,512]{1,0:T(8,128)S(1)}, f32[128,512]{1,0:T(8,128)S(1)}, u32[]{:S(2)}, u32[]{:S(2)}) collective-permute-start(f32[128,512]{1,0:T(8,128)S(1)} %get-tuple-element.99), channel_id=1, source_target_pairs={{0,16},{8,24},{1,17},{9,25},{2,18},{10,26},{3,19},{11,27},{4,20},{... | collective-permute-start | bytes 786440 | tf_op jit(solution)/shard_map/ppermute | solution.py:333
  79.1 2.5 %collective-permute-start.49 = (f32[128,512]{1,0:T(8,128)S(1)}, f32[128,512]{1,0:T(8,128)S(1)}, u32[]{:S(2)}, u32[]{:S(2)}) collective-permute-start(f32[128,512]{1,0:T(8,128)S(1)} %get-tuple-element.116), channel_id=1, source_target_pairs={{0,8},{8,16},{16,24},{1,9},{9,17},{17,25},{2,10},{10,18},{18,26},{... | collective-permute-start | bytes 786440 | tf_op jit(solution)/shard_map/ppermute | solution.py:333
  81.6 1.9 %collective-permute-start.50 = (f32[128,512]{1,0:T(8,128)S(1)}, f32[128,512]{1,0:T(8,128)S(1)}, u32[]{:S(2)}, u32[]{:S(2)}) collective-permute-start(f32[128,512]{1,0:T(8,128)S(1)} %get-tuple-element.117), channel_id=1, source_target_pairs={{0,8},{8,16},{16,24},{1,9},{9,17},{17,25},{2,10},{10,18},{18,26},{... | collective-permute-start | bytes 786440 | tf_op jit(solution)/shard_map/ppermute | solution.py:333
  83.5 1.9 %collective-permute-start.51 = (f32[128,512]{1,0:T(8,128)S(1)}, f32[128,512]{1,0:T(8,128)S(1)}, u32[]{:S(2)}, u32[]{:S(2)}) collective-permute-start(f32[128,512]{1,0:T(8,128)S(1)} %get-tuple-element.118), channel_id=1, source_target_pairs={{0,8},{8,16},{16,24},{1,9},{9,17},{17,25},{2,10},{10,18},{18,26},{... | collective-permute-start | bytes 786440 | tf_op jit(solution)/shard_map/ppermute | solution.py:333
  85.5 2.2 %collective-permute-done.37.refs_2_ = f32[128,512]{1,0:T(8,128)S(1)} collective-permute-done((f32[128,512]{1,0:T(8,128)S(1)}, f32[128,512]{1,0:T(8,128)S(1)}, u32[]{:S(2)}, u32[]{:S(2)}) %collective-permute-start.37) | collective-permute-done | bytes 262176 | tf_op jit(solution)/shard_map/ppermute | solution.py:333
  88.6 1.6 %collective-permute-start.52 = (f32[3,56,512]{2,1,0:T(8,128)S(1)}, f32[3,56,512]{2,1,0:T(8,128)S(1)}, u32[]{:S(2)}, u32[]{:S(2)}) collective-permute-start(f32[3,56,512]{2,1,0:T(8,128)S(1)} %get-tuple-element.123), channel_id=1, source_target_pairs={{0,1},{1,0},{2,3},{3,2},{4,5},{5,4},{6,7},{7,6},{8,9},{9,8},{10,11... | collective-permute-start | bytes 1032200 | tf_op jit(solution)/shard_map/ppermute | solution.py:338
  90.2 3.1 %collective-permute-done.49.refs_0_ = f32[128,512]{1,0:T(8,128)S(1)} collective-permute-done((f32[128,512]{1,0:T(8,128)S(1)}, f32[128,512]{1,0:T(8,128)S(1)}, u32[]{:S(2)}, u32[]{:S(2)}) %collective-permute-start.49) | collective-permute-done | bytes 262176 | tf_op jit(solution)/shard_map/ppermute | solution.py:333
  93.2 5.6 %collective-permute-done.50.refs_1_ = f32[128,512]{1,0:T(8,128)S(1)} collective-permute-done((f32[128,512]{1,0:T(8,128)S(1)}, f32[128,512]{1,0:T(8,128)S(1)}, u32[]{:S(2)}, u32[]{:S(2)}) %collective-permute-start.50) | collective-permute-done | bytes 262176 | tf_op jit(solution)/shard_map/ppermute | solution.py:333
  98.8 5.6 %collective-permute-done.51.refs_2_ = f32[128,512]{1,0:T(8,128)S(1)} collective-permute-done((f32[128,512]{1,0:T(8,128)S(1)}, f32[128,512]{1,0:T(8,128)S(1)}, u32[]{:S(2)}, u32[]{:S(2)}) %collective-permute-start.51) | collective-permute-done | bytes 262176 | tf_op jit(solution)/shard_map/ppermute | solution.py:333
  107.2 2.6 %collective-permute-start.55 = (f32[3,16,512]{2,1,0:T(8,128)S(1)}, f32[3,16,512]{2,1,0:T(8,128)S(1)}, u32[]{:S(2)}, u32[]{:S(2)}) collective-permute-start(f32[3,16,512]{2,1,0:T(8,128)S(1)} %get-tuple-element.127), channel_id=1, source_target_pairs={{0,7},{1,6},{2,1},{3,0},{4,3},{5,2},{6,5},{7,4},{8,15},{9,14},{10,... | collective-permute-start | bytes 294920 | tf_op jit(solution)/shard_map/ppermute | solution.py:350
  109.8 1.4 %along_x.13 = (f32[384,512]{1,0:T(8,128)S(1)}, f32[384,512]{1,0:T(8,128)S(1)}) custom-call(f32[384,512]{1,0:T(8,128)S(1)} %bitcast.43, f32[384,512]{1,0:T(8,128)S(1)} %bitcast.48, bf16[4,512,512]{2,1,0:T(8,128)(2,1)S(1)} %copy-done.3), custom_call_target="tpu_custom_call" | custom-call | flops 10000000000 | bytes 1048576 | tf_op jit(solution)/shard_map/along_x/pallas_call | solution.py:132
  115.5 1.7 %join.1 = f32[3,128,1024]{2,1,0:T(8,128)} custom-call(s32[2]{0:T(128)S(1)} %pad_add_fusion.flags_ref, f32[3,128,512]{2,1,0:T(8,128)S(1)} %stage_end.2.theirs_ref, f32[3,128,512]{2,1,0:T(8,128)S(1)} %stage_end.3.mine_ref), custom_call_target="tpu_custom_call" | custom-call | tf_op jit(solution)/shard_map/join/pallas_call | solution.py:320
  (169 shorter events, 49.8 us)
Async XLA Ops:
  0.0 43.4 %collective-permute-start = (f32[3,128,1024]{2,1,0:T(8,128)}, f32[3,128,1024]{2,1,0:T(8,128)S(1)}, u32[]{:S(2)}, u32[]{:S(2)}) collective-permute-start(f32[3,128,1024]{2,1,0:T(8,128)} %bitcast.36), channel_id=1, source_target_pairs={{0,8},{8,16},{16,24},{1,9},{9,17},{17,25},{2,10},{10,18},{18,26},{... | collective-permute-start | bytes 4718600 | tf_op jit(solution)/shard_map/ppermute | solution.py:333
  7.8 11.9 %collective-permute-start.5 = (f32[3,16,512]{2,1,0:T(8,128)S(1)}, f32[3,16,512]{2,1,0:T(8,128)S(1)}, u32[]{:S(2)}, u32[]{:S(2)}) collective-permute-start(f32[3,16,512]{2,1,0:T(8,128)S(1)} %slice.131), channel_id=1, source_target_pairs={{0,1},{1,0},{2,3},{3,2},{4,5},{5,4},{6,7},{7,6},{8,9},{9,8},{10,11... | collective-permute-start | bytes 294920 | tf_op jit(solution)/shard_map/ppermute | solution.py:338
  11.1 7.7 %collective-permute-start.2 = (f32[3,16,512]{2,1,0:T(8,128)}, f32[3,16,512]{2,1,0:T(8,128)S(1)}, u32[]{:S(2)}, u32[]{:S(2)}) collective-permute-start(f32[3,16,512]{2,1,0:T(8,128)} %get-tuple-element.140), channel_id=1, source_target_pairs={{0,3},{1,2},{2,5},{3,4},{4,7},{5,6},{6,1},{7,0},{8,11},{9,10},{10,... | collective-permute-start | bytes 294920 | tf_op jit(solution)/shard_map/ppermute | solution.py:350
  12.7 5.8 %collective-permute-start.3 = (f32[3,8,512]{2,1,0:T(8,128)S(1)}, f32[3,8,512]{2,1,0:T(8,128)S(1)}, u32[]{:S(2)}, u32[]{:S(2)}) collective-permute-start(f32[3,8,512]{2,1,0:T(8,128)S(1)} %slice.170), channel_id=1, source_target_pairs={{0,5},{1,4},{2,7},{3,6},{4,1},{5,0},{6,3},{7,2},{8,13},{9,12},{10,... | collective-permute-start | bytes 147464 | tf_op jit(solution)/shard_map/ppermute | solution.py:350
  13.8 5.7 %collective-permute-start.4 = (f32[3,16,512]{2,1,0:T(8,128)S(1)}, f32[3,16,512]{2,1,0:T(8,128)S(1)}, u32[]{:S(2)}, u32[]{:S(2)}) collective-permute-start(f32[3,16,512]{2,1,0:T(8,128)S(1)} %get-tuple-element.139), channel_id=1, source_target_pairs={{0,7},{1,6},{2,1},{3,0},{4,3},{5,2},{6,5},{7,4},{8,15},{9,14},{10,... | collective-permute-start | bytes 294920 | tf_op jit(solution)/shard_map/ppermute | solution.py:350
  24.4 8.3 %collective-permute-start.13 = (f32[3,16,512]{2,1,0:T(8,128)S(1)}, f32[3,16,512]{2,1,0:T(8,128)S(1)}, u32[]{:S(2)}, u32[]{:S(2)}) collective-permute-start(f32[3,16,512]{2,1,0:T(8,128)S(1)} %slice.137), channel_id=1, source_target_pairs={{0,1},{1,0},{2,3},{3,2},{4,5},{5,4},{6,7},{7,6},{8,9},{9,8},{10,11... | collective-permute-start | bytes 294920 | tf_op jit(solution)/shard_map/ppermute | solution.py:338
  24.7 7.4 %collective-permute-start.10 = (f32[3,16,512]{2,1,0:T(8,128)S(1)}, f32[3,16,512]{2,1,0:T(8,128)S(1)}, u32[]{:S(2)}, u32[]{:S(2)}) collective-permute-start(f32[3,16,512]{2,1,0:T(8,128)S(1)} %get-tuple-element.138), channel_id=1, source_target_pairs={{0,3},{1,2},{2,5},{3,4},{4,7},{5,6},{6,1},{7,0},{8,11},{9,10},{10,... | collective-permute-start | bytes 294920 | tf_op jit(solution)/shard_map/ppermute | solution.py:350
  26.0 5.8 %collective-permute-start.11 = (f32[3,8,512]{2,1,0:T(8,128)S(1)}, f32[3,8,512]{2,1,0:T(8,128)S(1)}, u32[]{:S(2)}, u32[]{:S(2)}) collective-permute-start(f32[3,8,512]{2,1,0:T(8,128)S(1)} %slice.174), channel_id=1, source_target_pairs={{0,5},{1,4},{2,7},{3,6},{4,1},{5,0},{6,3},{7,2},{8,13},{9,12},{10,... | collective-permute-start | bytes 147464 | tf_op jit(solution)/shard_map/ppermute | solution.py:350
  26.8 5.5 %collective-permute-start.12 = (f32[3,16,512]{2,1,0:T(8,128)S(1)}, f32[3,16,512]{2,1,0:T(8,128)S(1)}, u32[]{:S(2)}, u32[]{:S(2)}) collective-permute-start(f32[3,16,512]{2,1,0:T(8,128)S(1)} %get-tuple-element.137), channel_id=1, source_target_pairs={{0,7},{1,6},{2,1},{3,0},{4,3},{5,2},{6,5},{7,4},{8,15},{9,14},{10,... | collective-permute-start | bytes 294920 | tf_op jit(solution)/shard_map/ppermute | solution.py:350
  34.8 6.5 %collective-permute-start.21 = (f32[3,16,512]{2,1,0:T(8,128)S(1)}, f32[3,16,512]{2,1,0:T(8,128)S(1)}, u32[]{:S(2)}, u32[]{:S(2)}) collective-permute-start(f32[3,16,512]{2,1,0:T(8,128)S(1)} %slice.143), channel_id=1, source_target_pairs={{0,1},{1,0},{2,3},{3,2},{4,5},{5,4},{6,7},{7,6},{8,9},{9,8},{10,11... | collective-permute-start | bytes 294920 | tf_op jit(solution)/shard_map/ppermute | solution.py:338
  35.4 6.9 %collective-permute-start.18 = (f32[3,16,512]{2,1,0:T(8,128)S(1)}, f32[3,16,512]{2,1,0:T(8,128)S(1)}, u32[]{:S(2)}, u32[]{:S(2)}) collective-permute-start(f32[3,16,512]{2,1,0:T(8,128)S(1)} %get-tuple-element.136), channel_id=1, source_target_pairs={{0,3},{1,2},{2,5},{3,4},{4,7},{5,6},{6,1},{7,0},{8,11},{9,10},{10,... | collective-permute-start | bytes 294920 | tf_op jit(solution)/shard_map/ppermute | solution.py:350
  36.6 5.6 %collective-permute-start.19 = (f32[3,8,512]{2,1,0:T(8,128)S(1)}, f32[3,8,512]{2,1,0:T(8,128)S(1)}, u32[]{:S(2)}, u32[]{:S(2)}) collective-permute-start(f32[3,8,512]{2,1,0:T(8,128)S(1)} %slice.178), channel_id=1, source_target_pairs={{0,5},{1,4},{2,7},{3,6},{4,1},{5,0},{6,3},{7,2},{8,13},{9,12},{10,... | collective-permute-start | bytes 147464 | tf_op jit(solution)/shard_map/ppermute | solution.py:350
  37.3 5.4 %collective-permute-start.20 = (f32[3,16,512]{2,1,0:T(8,128)S(1)}, f32[3,16,512]{2,1,0:T(8,128)S(1)}, u32[]{:S(2)}, u32[]{:S(2)}) collective-permute-start(f32[3,16,512]{2,1,0:T(8,128)S(1)} %get-tuple-element.135), channel_id=1, source_target_pairs={{0,7},{1,6},{2,1},{3,0},{4,3},{5,2},{6,5},{7,4},{8,15},{9,14},{10,... | collective-permute-start | bytes 294920 | tf_op jit(solution)/shard_map/ppermute | solution.py:350
  45.8 21.8 %collective-permute-start.35 = (f32[128,512]{1,0:T(8,128)S(1)}, f32[128,512]{1,0:T(8,128)S(1)}, u32[]{:S(2)}, u32[]{:S(2)}) collective-permute-start(f32[128,512]{1,0:T(8,128)S(1)} %get-tuple-element.83), channel_id=1, source_target_pairs={{0,16},{8,24},{1,17},{9,25},{2,18},{10,26},{3,19},{11,27},{4,20},{... | collective-permute-start | bytes 786440 | tf_op jit(solution)/shard_map/ppermute | solution.py:333
  47.9 8.3 %collective-permute-start.26 = (f32[3,16,512]{2,1,0:T(8,128)S(1)}, f32[3,16,512]{2,1,0:T(8,128)S(1)}, u32[]{:S(2)}, u32[]{:S(2)}) collective-permute-start(f32[3,16,512]{2,1,0:T(8,128)S(1)} %slice.149), channel_id=1, source_target_pairs={{0,1},{1,0},{2,3},{3,2},{4,5},{5,4},{6,7},{7,6},{8,9},{9,8},{10,11... | collective-permute-start | bytes 294920 | tf_op jit(solution)/shard_map/ppermute | solution.py:338
  48.5 7.1 %collective-permute-start.23 = (f32[3,16,512]{2,1,0:T(8,128)S(1)}, f32[3,16,512]{2,1,0:T(8,128)S(1)}, u32[]{:S(2)}, u32[]{:S(2)}) collective-permute-start(f32[3,16,512]{2,1,0:T(8,128)S(1)} %get-tuple-element.134), channel_id=1, source_target_pairs={{0,3},{1,2},{2,5},{3,4},{4,7},{5,6},{6,1},{7,0},{8,11},{9,10},{10,... | collective-permute-start | bytes 294920 | tf_op jit(solution)/shard_map/ppermute | solution.py:350
  49.6 5.6 %collective-permute-start.24 = (f32[3,8,512]{2,1,0:T(8,128)S(1)}, f32[3,8,512]{2,1,0:T(8,128)S(1)}, u32[]{:S(2)}, u32[]{:S(2)}) collective-permute-start(f32[3,8,512]{2,1,0:T(8,128)S(1)} %slice.182), channel_id=1, source_target_pairs={{0,5},{1,4},{2,7},{3,6},{4,1},{5,0},{6,3},{7,2},{8,13},{9,12},{10,... | collective-permute-start | bytes 147464 | tf_op jit(solution)/shard_map/ppermute | solution.py:350
  58.9 7.2 %collective-permute-start.31 = (f32[3,16,512]{2,1,0:T(8,128)S(1)}, f32[3,16,512]{2,1,0:T(8,128)S(1)}, u32[]{:S(2)}, u32[]{:S(2)}) collective-permute-start(f32[3,16,512]{2,1,0:T(8,128)S(1)} %get-tuple-element.132), channel_id=1, source_target_pairs={{0,3},{1,2},{2,5},{3,4},{4,7},{5,6},{6,1},{7,0},{8,11},{9,10},{10,... | collective-permute-start | bytes 294920 | tf_op jit(solution)/shard_map/ppermute | solution.py:350
  60.1 5.7 %collective-permute-start.32 = (f32[3,8,512]{2,1,0:T(8,128)S(1)}, f32[3,8,512]{2,1,0:T(8,128)S(1)}, u32[]{:S(2)}, u32[]{:S(2)}) collective-permute-start(f32[3,8,512]{2,1,0:T(8,128)S(1)} %slice.186), channel_id=1, source_target_pairs={{0,5},{1,4},{2,7},{3,6},{4,1},{5,0},{6,3},{7,2},{8,13},{9,12},{10,... | collective-permute-start | bytes 147464 | tf_op jit(solution)/shard_map/ppermute | solution.py:350
  60.7 5.6 %collective-permute-start.33 = (f32[3,16,512]{2,1,0:T(8,128)S(1)}, f32[3,16,512]{2,1,0:T(8,128)S(1)}, u32[]{:S(2)}, u32[]{:S(2)}) collective-permute-start(f32[3,16,512]{2,1,0:T(8,128)S(1)} %get-tuple-element.131), channel_id=1, source_target_pairs={{0,7},{1,6},{2,1},{3,0},{4,3},{5,2},{6,5},{7,4},{8,15},{9,14},{10,... | collective-permute-start | bytes 294920 | tf_op jit(solution)/shard_map/ppermute | solution.py:350
  63.7 21.8 %collective-permute-start.36 = (f32[128,512]{1,0:T(8,128)S(1)}, f32[128,512]{1,0:T(8,128)S(1)}, u32[]{:S(2)}, u32[]{:S(2)}) collective-permute-start(f32[128,512]{1,0:T(8,128)S(1)} %get-tuple-element.98), channel_id=1, source_target_pairs={{0,16},{8,24},{1,17},{9,25},{2,18},{10,26},{3,19},{11,27},{4,20},{... | collective-permute-start | bytes 786440 | tf_op jit(solution)/shard_map/ppermute | solution.py:333
  69.4 7.2 %collective-permute-start.42 = (f32[3,16,512]{2,1,0:T(8,128)S(1)}, f32[3,16,512]{2,1,0:T(8,128)S(1)}, u32[]{:S(2)}, u32[]{:S(2)}) collective-permute-start(f32[3,16,512]{2,1,0:T(8,128)S(1)} %get-tuple-element.130), channel_id=1, source_target_pairs={{0,3},{1,2},{2,5},{3,4},{4,7},{5,6},{6,1},{7,0},{8,11},{9,10},{10,... | collective-permute-start | bytes 294920 | tf_op jit(solution)/shard_map/ppermute | solution.py:350
  70.6 5.7 %collective-permute-start.43 = (f32[3,8,512]{2,1,0:T(8,128)S(1)}, f32[3,8,512]{2,1,0:T(8,128)S(1)}, u32[]{:S(2)}, u32[]{:S(2)}) collective-permute-start(f32[3,8,512]{2,1,0:T(8,128)S(1)} %slice.190), channel_id=1, source_target_pairs={{0,5},{1,4},{2,7},{3,6},{4,1},{5,0},{6,3},{7,2},{8,13},{9,12},{10,... | collective-permute-start | bytes 147464 | tf_op jit(solution)/shard_map/ppermute | solution.py:350
  71.3 5.5 %collective-permute-start.44 = (f32[3,16,512]{2,1,0:T(8,128)S(1)}, f32[3,16,512]{2,1,0:T(8,128)S(1)}, u32[]{:S(2)}, u32[]{:S(2)}) collective-permute-start(f32[3,16,512]{2,1,0:T(8,128)S(1)} %get-tuple-element.129), channel_id=1, source_target_pairs={{0,7},{1,6},{2,1},{3,0},{4,3},{5,2},{6,5},{7,4},{8,15},{9,14},{10,... | collective-permute-start | bytes 294920 | tf_op jit(solution)/shard_map/ppermute | solution.py:350
  74.2 13.4 %collective-permute-start.37 = (f32[128,512]{1,0:T(8,128)S(1)}, f32[128,512]{1,0:T(8,128)S(1)}, u32[]{:S(2)}, u32[]{:S(2)}) collective-permute-start(f32[128,512]{1,0:T(8,128)S(1)} %get-tuple-element.99), channel_id=1, source_target_pairs={{0,16},{8,24},{1,17},{9,25},{2,18},{10,26},{3,19},{11,27},{4,20},{... | collective-permute-start | bytes 786440 | tf_op jit(solution)/shard_map/ppermute | solution.py:333
  79.1 14.1 %collective-permute-start.49 = (f32[128,512]{1,0:T(8,128)S(1)}, f32[128,512]{1,0:T(8,128)S(1)}, u32[]{:S(2)}, u32[]{:S(2)}) collective-permute-start(f32[128,512]{1,0:T(8,128)S(1)} %get-tuple-element.116), channel_id=1, source_target_pairs={{0,8},{8,16},{16,24},{1,9},{9,17},{17,25},{2,10},{10,18},{18,26},{... | collective-permute-start | bytes 786440 | tf_op jit(solution)/shard_map/ppermute | solution.py:333
  81.6 17.3 %collective-permute-start.50 = (f32[128,512]{1,0:T(8,128)S(1)}, f32[128,512]{1,0:T(8,128)S(1)}, u32[]{:S(2)}, u32[]{:S(2)}) collective-permute-start(f32[128,512]{1,0:T(8,128)S(1)} %get-tuple-element.117), channel_id=1, source_target_pairs={{0,8},{8,16},{16,24},{1,9},{9,17},{17,25},{2,10},{10,18},{18,26},{... | collective-permute-start | bytes 786440 | tf_op jit(solution)/shard_map/ppermute | solution.py:333
  83.5 21.0 %collective-permute-start.51 = (f32[128,512]{1,0:T(8,128)S(1)}, f32[128,512]{1,0:T(8,128)S(1)}, u32[]{:S(2)}, u32[]{:S(2)}) collective-permute-start(f32[128,512]{1,0:T(8,128)S(1)} %get-tuple-element.118), channel_id=1, source_target_pairs={{0,8},{8,16},{16,24},{1,9},{9,17},{17,25},{2,10},{10,18},{18,26},{... | collective-permute-start | bytes 786440 | tf_op jit(solution)/shard_map/ppermute | solution.py:333
  88.6 16.8 %collective-permute-start.52 = (f32[3,56,512]{2,1,0:T(8,128)S(1)}, f32[3,56,512]{2,1,0:T(8,128)S(1)}, u32[]{:S(2)}, u32[]{:S(2)}) collective-permute-start(f32[3,56,512]{2,1,0:T(8,128)S(1)} %get-tuple-element.123), channel_id=1, source_target_pairs={{0,1},{1,0},{2,3},{3,2},{4,5},{5,4},{6,7},{7,6},{8,9},{9,8},{10,11... | collective-permute-start | bytes 1032200 | tf_op jit(solution)/shard_map/ppermute | solution.py:338
  105.5 6.9 %collective-permute-start.53 = (f32[3,16,512]{2,1,0:T(8,128)S(1)}, f32[3,16,512]{2,1,0:T(8,128)S(1)}, u32[]{:S(2)}, u32[]{:S(2)}) collective-permute-start(f32[3,16,512]{2,1,0:T(8,128)S(1)} %get-tuple-element.128), channel_id=1, source_target_pairs={{0,3},{1,2},{2,5},{3,4},{4,7},{5,6},{6,1},{7,0},{8,11},{9,10},{10,... | collective-permute-start | bytes 294920 | tf_op jit(solution)/shard_map/ppermute | solution.py:350
  106.6 5.8 %collective-permute-start.54 = (f32[3,8,512]{2,1,0:T(8,128)S(1)}, f32[3,8,512]{2,1,0:T(8,128)S(1)}, u32[]{:S(2)}, u32[]{:S(2)}) collective-permute-start(f32[3,8,512]{2,1,0:T(8,128)S(1)} %slice.194), channel_id=1, source_target_pairs={{0,5},{1,4},{2,7},{3,6},{4,1},{5,0},{6,3},{7,2},{8,13},{9,12},{10,... | collective-permute-start | bytes 147464 | tf_op jit(solution)/shard_map/ppermute | solution.py:350
  107.2 6.0 %collective-permute-start.55 = (f32[3,16,512]{2,1,0:T(8,128)S(1)}, f32[3,16,512]{2,1,0:T(8,128)S(1)}, u32[]{:S(2)}, u32[]{:S(2)}) collective-permute-start(f32[3,16,512]{2,1,0:T(8,128)S(1)} %get-tuple-element.127), channel_id=1, source_target_pairs={{0,7},{1,6},{2,1},{3,0},{4,3},{5,2},{6,5},{7,4},{8,15},{9,14},{10,... | collective-permute-start | bytes 294920 | tf_op jit(solution)/shard_map/ppermute | solution.py:350
  (40 other events, 110.1 us)

commit v4 on v3

--- a/solution.py
+++ b/solution.py
@@ -20,6 +20,8 @@
 ROWS = 8
 KERNEL_BYTES = 8 * 2**20
 KERNEL_FLOPS = 10**10
+FAR = (3,)
+NEAR = (3,)
 F32 = jnp.float32
 BF16 = jnp.bfloat16
 
@@ -122,22 +124,21 @@
 
 
 VMEM = pl.BlockSpec(memory_space=pltpu.VMEM)
-SMEM = pl.BlockSpec(memory_space=pltpu.SMEM)
-ANY = pl.BlockSpec(memory_space=pl.ANY)
-
-
-def on_chip_call(body, operands, shapes, scalars=1, keep=True, **options):
-    held = [pltpu.with_memory_space_constraint(a, pltpu.VMEM) for a in operands[scalars:]]
+HBM = pl.BlockSpec(memory_space=pltpu.HBM)
+
+
+def on_chip_call(body, operands, shapes, keep=True, **options):
+    held = [pltpu.with_memory_space_constraint(a, pltpu.VMEM) for a in operands]
     outs = [pltpu.VMEM(s.shape, s.dtype) for s in shapes] if keep else shapes
     return pl.pallas_call(
         body,
-        in_specs=[SMEM] * scalars + [VMEM] * len(held),
-        out_specs=[VMEM] * len(outs),
+        in_specs=[VMEM] * len(held),
+        out_specs=[VMEM if keep else HBM] * len(outs),
         out_shape=outs,
         compiler_params=pltpu.CompilerParams(vmem_limit_bytes=KERNEL_BYTES),
         cost_estimate=COST,
         **options,
-    )(*operands[:scalars], *held)
+    )(*held)
 
 
 def x_kernel(theirs_ref, mine_ref, table_ref, grad_theirs_ref, grad_mine_ref):
@@ -157,8 +158,12 @@
     fields, rows, half = mine.shape
     flat = [a.reshape(fields * rows, half) for a in (theirs, mine)]
     shape = jax.ShapeDtypeStruct(flat[0].shape, F32)
-    grads = on_chip_call(x_kernel, [*flat, table], [shape, shape], scalars=0, name="along_x")
+    grads = on_chip_call(x_kernel, [*flat, table], [shape, shape], name="along_x")
     return [g.reshape(mine.shape) for g in grads]
+
+
+def member_of_pair():
+    return lax.rem(lax.axis_index("grid"), 2)
 
 
 class Plan:
@@ -169,9 +174,8 @@
         self.whole = jax.ShapeDtypeStruct((3, rows, length), F32)
         self.moments = [jax.ShapeDtypeStruct((3, self.total + mate_rank, self.half), F32)]
 
-    def columns(self, flags_ref, mine):
-        member = flags_ref[0]
-        at = member if mine else 1 - member
+    def columns(self, mine):
+        at = member_of_pair() if mine else 1 - member_of_pair()
         return pl.ds(pl.multiple_of(at * self.half, 128), self.half)
 
     def emit_moments(self, next_ref, send_ref, moments_ref):
@@ -198,15 +202,18 @@
     return rate_h, rate_u, rate_v
 
 
-def enter_call(plan, flags, state, received, send):
+def enter_call(plan, state, received, send, coriolis=None, both_apply=None):
     sources = [state, *received]
-
-    def body(flags_ref, own_ref, *refs):
-        received_refs, (send_ref, *outs) = refs[: len(received)], refs[len(received) :]
+    opening = coriolis is not None
+    more = [both_apply, coriolis] if opening else []
+
+    def body(own_ref, *refs):
+        received_refs, (send_ref, *refs) = refs[: len(received)], refs[len(received) :]
+        more_refs, outs = refs[: len(more)], refs[len(more) :]
         nexts, moments, arrived = outs[0:4:2], outs[1:4:2], outs[-1]
 
         def copy(source_ref, at):
-            cols = plan.columns(flags_ref, at == 1)
+            cols = plan.columns(at == 1)
             return pltpu.make_async_copy(source_ref.at[:, :, cols], nexts[at], arrived.at[at])
 
         def start(source_ref):
@@ -214,55 +221,79 @@
                 copy(source_ref, at).start()
 
         if received:
-            pl.when(flags_ref[1] == 0)(lambda: start(own_ref))
-            pl.when(flags_ref[1] != 0)(lambda: start(received_refs[0]))
+            pl.when(lax.axis_index("tm") == 0)(lambda: start(own_ref))
+            pl.when(lax.axis_index("tm") != 0)(lambda: start(received_refs[0]))
         else:
             start(own_ref)
+        if opening:
+            outs[4][...] = send_ref[member_of_pair()]
+            outs[5][...] = more_refs[0][member_of_pair()]
+            square = (plan.rows, plan.rows)
+            here = lax.broadcasted_iota(jnp.int32, square, 0) == lax.broadcasted_iota(jnp.int32, square, 1)
+            outs[6][...] = jnp.sum(jnp.where(here, more_refs[1][...], 0.0), axis=1, keepdims=True)
+            send_ref = outs[4]
         for at in range(2):
             copy(own_ref, at).wait()
             plan.emit_moments(nexts[at], send_ref, moments[at])
 
     shapes = [plan.state, *plan.moments] * 2
+    if opening:
+        shapes += [jax.ShapeDtypeStruct(a.shape[1:], a.dtype) for a in (send, both_apply)]
+        shapes.append(jax.ShapeDtypeStruct((plan.rows, 1), F32))
     return pl.pallas_call(
         body,
-        in_specs=[SMEM] + [ANY] * len(sources) + [VMEM],
-        out_specs=[VMEM] * 4,
+        in_specs=[HBM] * len(sources) + [VMEM] * (1 + len(more)),
+        out_specs=[VMEM] * len(shapes),
         out_shape=[pltpu.VMEM(s.shape, s.dtype) for s in shapes],
         scratch_shapes=[pltpu.SemaphoreType.DMA((2,))],
         compiler_params=pltpu.CompilerParams(vmem_limit_bytes=KERNEL_BYTES),
         cost_estimate=COST,
         name="enter",
-    )(flags, *sources, pltpu.with_memory_space_constraint(send, pltpu.VMEM))
-
-
-def restart_call(plan, flags, received, second, node_one, added, send):
-    extra = list(second)
-    fields = len(received)
-
-    def body(flags_ref, *refs):
-        received_refs, (node_ref, added_ref, *rest) = refs[:fields], refs[fields:]
-        send_ref, next_ref, moments_ref = rest[len(extra) :]
+    )(*sources, *[pltpu.with_memory_space_constraint(a, pltpu.VMEM) for a in (send, *more)])
+
+
+def field_of(refs, f):
+    for ref in refs:
+        if f < ref.shape[0]:
+            return ref[f]
+        f -= ref.shape[0]
+
+
+def restart_call(plan, received, second, node_one, added, send):
+    count = len(received)
+
+    def body(*refs):
+        received_refs, (node_ref, added_ref, *rest) = refs[:count], refs[count:]
+        second_refs, (send_ref, next_ref, moments_ref) = rest[: len(second)], rest[len(second) :]
         for f in range(3):
-            value = received_refs[f][...]
-            if extra:
-                value = jnp.where(flags_ref[1] == 1, rest[f][...], value)
-            next_ref[f] = jnp.where(flags_ref[1] == 0, node_ref[f], value) + added_ref[f]
+            value = field_of(received_refs, f)
+            if second:
+                value = jnp.where(lax.axis_index("tm") == 1, field_of(second_refs, f), value)
+            next_ref[f] = jnp.where(lax.axis_index("tm") == 0, node_ref[f], value) + added_ref[f]
         plan.emit_moments(next_ref, send_ref, moments_ref)
 
-    operands = [flags, *received, node_one, added, *extra, send]
+    operands = [*received, node_one, added, *second, send]
     return on_chip_call(body, operands, [plan.state, *plan.moments], name="restart")
 
 
-def stage_call(plan, kind, state, grad_x, pair_in, mate_in, turning, apply, send=None, others=()):
+def stage_call(plan, kind, state, grad_x, pair_in, mate_in, turning, apply, send=None, others=(), groups=()):
     count = len(pair_in)
-    split = kind in ("lead", "correct")
+    join = kind == "join"
 
     def body(state_ref, grad_ref, turning_ref, *rest):
         pair_refs, (mate_ref, apply_ref), rest = rest[:count], rest[count : count + 2], rest[count + 2 :]
         other_refs, rest = rest[: len(others)], rest[len(others) :]
         if send is not None:
             send_ref, rest = rest[0], rest[1:]
-        grad_y = rest[-1]
+        leads, outs, grad_y = rest[: len(groups)], rest[len(groups) : len(shapes)], rest[len(shapes)]
+        if join:
+            made_ref, done = rest[len(shapes) + 1 :]
+            whole_ref, outs = outs[0], [made_ref]
+            copies = [
+                pltpu.make_async_copy(ref, whole_ref.at[:, :, plan.columns(at == 1)], done.at[at])
+                for at, ref in enumerate((other_refs[1], made_ref))
+            ]
+            copies[0].start()
         for f in range(3):
             grad_y[f] = plan.y_gradient(f, state_ref, pair_refs, mate_ref, apply_ref)
         for start in range(0, plan.rows, ROWS):
@@ -273,59 +304,37 @@
             )
             for f in range(3):
                 ahead = now[f] + HALF_STEP * rates[f]
-                if kind == "end":
-                    ahead = ahead + other_refs[0][f, at]
-                if split:
-                    rest[f][at] = ahead
+                if groups:
+                    group = next(g for g in range(len(groups)) if f < sum(groups[: g + 1]))
+                    leads[group][f - sum(groups[:group]), at] = ahead
+                elif kind in ("end", "join"):
+                    outs[0][f, at] = ahead + other_refs[0][f, at]
                 else:
-                    rest[0][f, at] = ahead
+                    outs[0][f, at] = ahead
                 if kind == "keep":
-                    rest[1][f, at] = rates[f]
+                    outs[1][f, at] = rates[f]
                 if kind == "correct":
                     olds = (other_refs[0][f, at], other_refs[1][f, at], rates[f])
-                    for out, weights in ((rest[-3], CORRECT_FIRST), (rest[-2], CORRECT_SECOND)):
+                    for out, weights in zip(outs, (CORRECT_FIRST, CORRECT_SECOND)):
                         out[f, at] = sum((STEP_LENGTH * w) * r for w, r in zip(weights, olds))
         if send is not None:
-            plan.emit_moments(rest[0], send_ref, rest[-2])
+            plan.emit_moments(outs[0], send_ref, outs[-1])
+        if join:
+            copies[1].start()
+            for copy in copies:
+                copy.wait()
 
     operands = [state, grad_x, turning, *pair_in, mate_in, apply, *others]
-    shapes = [plan.state] * {"move": 1, "keep": 2, "lead": 0, "correct": 2, "end": 1}[kind]
-    if split:
-        shapes = [jax.ShapeDtypeStruct(plan.state.shape[1:], F32)] * 3 + shapes
+    shapes = [jax.ShapeDtypeStruct((g, *plan.state.shape[1:]), F32) for g in groups]
+    shapes += [plan.state] * {"move": 1, "keep": 2, "lead": 0, "correct": 2, "end": 1, "join": 0}[kind]
+    scratch = [pltpu.VMEM(plan.state.shape, F32)]
     if send is not None:
         operands.append(send)
         shapes += plan.moments
-    return on_chip_call(
-        body,
-        operands,
-        shapes,
-        scalars=0,
-        scratch_shapes=[pltpu.VMEM((3, plan.rows, plan.half), F32)],
-        name=f"stage_{kind}",
-    )
-
-
-def join_call(plan, flags, theirs, mine):
-    def body(flags_ref, theirs_ref, mine_ref, out_ref, done):
-        copies = [
-            pltpu.make_async_copy(ref, out_ref.at[:, :, plan.columns(flags_ref, at == 1)], done.at[at])
-            for at, ref in enumerate((theirs_ref, mine_ref))
-        ]
-        for copy in copies:
-            copy.start()
-        for copy in copies:
-            copy.wait()
-
-    held = [pltpu.with_memory_space_constraint(a, pltpu.VMEM) for a in (theirs, mine)]
-    return pl.pallas_call(
-        body,
-        in_specs=[SMEM, VMEM, VMEM],
-        out_specs=ANY,
-        out_shape=plan.whole,
-        scratch_shapes=[pltpu.SemaphoreType.DMA((2,))],
-        compiler_params=pltpu.CompilerParams(vmem_limit_bytes=KERNEL_BYTES),
-        name="join",
-    )(flags, *held)
+    if join:
+        shapes = [plan.whole]
+        scratch += [pltpu.VMEM(plan.state.shape, F32), pltpu.SemaphoreType.DMA((2,))]
+    return on_chip_call(body, operands, shapes, keep=not join, scratch_shapes=scratch, name=f"stage_{kind}")
 
 
 def ahead_in_time(array, by):
@@ -356,53 +365,44 @@
     _, rows, length = own.shape
     ranks, mate_rank, send_tables, apply_tables = y_tables(length, lax.axis_size("grid"))
     plan = Plan(rows, length, ranks, mate_rank)
-    member = lax.axis_index("grid") % 2
-    flags = jnp.stack([member, lax.axis_index("tm")]).astype(jnp.int32)
     table = jnp.asarray(x_tables(length))
-    send = lax.dynamic_index_in_dim(jnp.asarray(send_tables), member, 0, keepdims=False)
-    apply = lax.dynamic_index_in_dim(jnp.asarray(apply_tables), member, 0, keepdims=False)
-    turning = coriolis[:, None]
-
-    def stage(kind, states, moments, others=((), ()), sends=True, only_first=False):
+    def stage(kinds, states, moments, others=((), ()), sends=False, groups=((), ())):
         received = exchange(plan, *moments)
         grads = along_x(*states, table)
         results = []
-        for at in range(1 if only_first else 2):
-            pair_in, mate_in = received[at]
-            results.append(
-                stage_call(
-                    plan, kind, states[at], grads[at], pair_in, mate_in, turning, apply, send if sends else None, others[at]
-                )
-            )
+        for at, kind in enumerate(kinds):
+            more = others[at] if kind != "join" else (*others[at], results[0][0])
+            operands = (states[at], grads[at], *received[at], turning, apply)
+            results.append(stage_call(plan, kind, *operands, send if sends else None, more, groups[at]))
         if not sends:
             return results
         return *zip(*[r[:-1] for r in results]), [r[-1] for r in results]
 
-    def enter(received):
-        theirs, theirs_moments, mine, mine_moments = enter_call(plan, flags, own, received, send)
-        return [theirs, mine], [theirs_moments, mine_moments]
-
-    before = [ahead_in_time(own, 1)]
-    states, moments = enter([])
-    states, moments = stage("move", states, moments)
-    states, moments = stage("move", states, moments)
-    (lead,) = stage("lead", states, moments, sends=False, only_first=True)
-    far = [ahead_in_time(field, 2) for field in lead]
-
-    *before, _ = lax.optimization_barrier((*before, lead[0]))
-    states, moments = enter(before)
-    nodes_one, rates_zero, moments = stage("keep", states, moments)
-    states, rates_one, moments = stage("keep", nodes_one, moments)
-    moments[0], far[0] = lax.optimization_barrier((moments[0], far[0]))
-    theirs, mine = stage("correct", states, moments, list(zip(rates_zero, rates_one)), sends=False)
-    near = [ahead_in_time(field, 1) for field in mine[:3]]
+    before = ahead_in_time(own, 1)
+    both_send, both_apply = jnp.asarray(send_tables), jnp.asarray(apply_tables)
+    opened = enter_call(plan, own, [], both_send, coriolis[None, :], both_apply)
+    states, moments, (send, apply, turning) = opened[0:4:2], list(opened[1:4:2]), opened[4:]
+    states, moments = stage(("move", "move"), states, moments, sends=True)
+    states, moments = stage(("move", "move"), states, moments, sends=True)
+    (lead,) = stage(("lead",), states, moments, groups=(FAR,))
+    far = [ahead_in_time(fields, 2) for fields in lead]
+
+    before, _ = lax.optimization_barrier((before, lead[0]))
+    entered = enter_call(plan, own, [before], send)
+    states, moments = entered[0::2], list(entered[1::2])
+    nodes_one, rates_zero, moments = stage(("keep", "keep"), states, moments, sends=True)
+    states, rates_one, moments = stage(("keep", "keep"), nodes_one, moments, sends=True)
+    olds = list(zip(rates_zero, rates_one))
+    theirs, mine = stage(("correct", "correct"), states, moments, olds, groups=((3,), NEAR))
+    near = [ahead_in_time(fields, 1) for fields in mine[: len(NEAR)]]
 
     results = [
-        restart_call(plan, flags, far, theirs[:3], nodes_one[0], theirs[3], send),
-        restart_call(plan, flags, near, (), nodes_one[1], mine[3], send),
+        restart_call(plan, far, theirs[:1], nodes_one[0], theirs[1], send),
+        restart_call(plan, near, (), nodes_one[1], mine[-2], send),
     ]
-    ends = stage("end", [r[0] for r in results], [r[1] for r in results], ((theirs[4],), (mine[4],)), sends=False)
-    return join_call(plan, flags, ends[0][0], ends[1][0])[None]
+    lasts = ((theirs[2],), (mine[-1],))
+    ends = stage(("end", "join"), [r[0] for r in results], [r[1] for r in results], lasts)
+    return ends[1][0][None]
 
 
 def solution(mesh):

time: 119 us -> 115 us (0.966)
  waiting for transfers between devices: 28.8 us -> 37.6 us
  starting transfers between devices: 51.5 us -> 46.4 us
  local copies, waits for them, and re-layouts: 7.1 us -> 2.65 us
  Pallas kernels: 28.8 us -> 26 us
    ppermute x7 -> x3, waiting for transfers between devices: 16.5 us -> 22.5 us  [ahead_in_time(): return lax.ppermute(array, 'tm', [(i, i + by) for i in range(size - by)])]
    ppermute x7 -> x3, starting transfers between devices: 14.5 us -> 9.37 us  [ahead_in_time(): return lax.ppermute(array, 'tm', [(i, i + by) for i in range(size - by)])]
    unnamed x24 -> x8, local copies, waits for them, and re-layouts: 5.3 us -> 2.45 us
    pallas_call x25 -> x24, Pallas kernels: 28.8 us -> 26 us  [the longest x22 23.3 us: on_chip_call(): pl.pallas_call(body, in_specs=[VMEM] * len(held), out_specs=[VMEM if keep...]
    ppermute x21, waiting for transfers between devices: 11.8 us -> 13.8 us  [exchange(): lax.ppermute(part, 'grid', [(i, (i + 2 * d) % size ^ 1) for i in range(si...]
    ppermute x21, starting transfers between devices: 25.5 us -> 27 us  [exchange(): lax.ppermute(part, 'grid', [(i, (i + 2 * d) % size ^ 1) for i in range(si...]
    ppermute x32, starting transfers between devices: 11.5 us -> 10 us  [mate_swap(): return lax.ppermute(array, 'grid', [(i, i ^ 1) for i in range(size)])]
  transfers between devices with their start and end apart: 60 -> 56, of which waited for: 16 -> 20; matrix products, arithmetic and copies ran while one was open for 2% -> 0% of each run, Pallas kernels for 21% -> 19%
where the time goes in v4:
time: 115 us; the launch traced here: 114 us
  starting transfers between devices  46.4 us (40%)
  waiting for transfers between devices  37.6 us (33%)
  Pallas kernels  26 us (23%)
  local copies, waits for them, and re-layouts  2.65 us (2%)
    ppermute x21, starting transfers between devices, exchange(): lax.ppermute(part, 'grid', [(i, (i + 2 * d) % size ^ 1) for i in range(si...  27 us
    pallas_call x22, Pallas kernels, on_chip_call(): pl.pallas_call(body, in_specs=[VMEM] * len(held), out_specs=[VMEM if keep...  23.3 us
    ppermute x3, waiting for transfers between devices, ahead_in_time(): return lax.ppermute(array, 'tm', [(i, i + by) for i in range(size - by)])  22.5 us
    ppermute x21, waiting for transfers between devices, exchange(): lax.ppermute(part, 'grid', [(i, (i + 2 * d) % size ^ 1) for i in range(si...  13.8 us
    ppermute x32, starting transfers between devices, mate_swap(): return lax.ppermute(array, 'grid', [(i, i ^ 1) for i in range(size)])  10 us
    ppermute x3, starting transfers between devices, ahead_in_time(): return lax.ppermute(array, 'tm', [(i, i + by) for i in range(size - by)])  9.37 us
    pallas_call x2, Pallas kernels, enter_call(): pl.pallas_call(body, in_specs=[HBM] * len(sources) + [VMEM] * (1 + len(mo...  2.7 us
    unnamed x8, local copies, waits for them, and re-layouts  2.45 us
  transfers between devices with their start and end apart: 56, of which 20 were waited for; matrix products, arithmetic and copies ran while one was open for 0% of the time, Pallas kernels for 19%

profile of v4, /device:TPU:9, one launch (start us, length us, event | category | flops | bytes accessed | tf_op | source)
XLA Modules:
  0.0 113.5 jit_solution(11167916032177752253)
XLA Ops:
  2.4 1.9 %enter.2 = (f32[3,128,512]{2,1,0:T(8,128)S(1)}, f32[3,56,512]{2,1,0:T(8,128)S(1)}, f32[3,128,512]{2,1,0:T(8,128)S(1)}, f32[3,56,512]{2,1,0:T(8,128)S(1)}, bf16[1...) custom-call(f32[3,128,1024]{2,1,0:T(8,128)} %bitcast.own_ref, ...), custom_call_target="tpu_custom_call" | custom-call | flops 10000000000 | bytes 1048576 | tf_op jit(solution)/shard_map/enter/pallas_call | solution.py:243
  5.1 3.2 %collective-permute-start = (f32[3,128,1024]{2,1,0:T(8,128)}, f32[3,128,1024]{2,1,0:T(8,128)S(1)}, u32[]{:S(2)}, u32[]{:S(2)}) collective-permute-start(f32[3,128,1024]{2,1,0:T(8,128)} %bitcast.own_ref), channel_id=1, source_target_pairs={{0,8},{8,16},{16,24},{1,9},{9,17},{17,25},{2,10},{10,18},{18,26},{... | collective-permute-start | bytes 4718600 | tf_op jit(solution)/shard_map/ppermute | solution.py:342
  8.8 1.4 %collective-permute-start.2 = (f32[3,16,512]{2,1,0:T(8,128)S(1)}, f32[3,16,512]{2,1,0:T(8,128)S(1)}, u32[]{:S(2)}, u32[]{:S(2)}) collective-permute-start(f32[3,16,512]{2,1,0:T(8,128)S(1)} %get-tuple-element.128), channel_id=1, source_target_pairs={{0,3},{1,2},{2,5},{3,4},{4,7},{5,6},{6,1},{7,0},{8,11},{9,10},{10,... | collective-permute-start | bytes 294920 | tf_op jit(solution)/shard_map/ppermute | solution.py:359
  10.1 1.3 %collective-permute-start.4 = (f32[3,16,512]{2,1,0:T(8,128)S(1)}, f32[3,16,512]{2,1,0:T(8,128)S(1)}, u32[]{:S(2)}, u32[]{:S(2)}) collective-permute-start(f32[3,16,512]{2,1,0:T(8,128)S(1)} %get-tuple-element.127), channel_id=1, source_target_pairs={{0,7},{1,6},{2,1},{3,0},{4,3},{5,2},{6,5},{7,4},{8,15},{9,14},{10,... | collective-permute-start | bytes 294920 | tf_op jit(solution)/shard_map/ppermute | solution.py:359
  11.5 1.3 %collective-permute-start.3 = (f32[3,8,512]{2,1,0:T(8,128)S(1)}, f32[3,8,512]{2,1,0:T(8,128)S(1)}, u32[]{:S(2)}, u32[]{:S(2)}) collective-permute-start(f32[3,8,512]{2,1,0:T(8,128)S(1)} %slice.170), channel_id=1, source_target_pairs={{0,5},{1,4},{2,7},{3,6},{4,1},{5,0},{6,3},{7,2},{8,13},{9,12},{10,... | collective-permute-start | bytes 147464 | tf_op jit(solution)/shard_map/ppermute | solution.py:359
  12.8 1.4 %along_x.7 = (f32[384,512]{1,0:T(8,128)S(1)}, f32[384,512]{1,0:T(8,128)S(1)}) custom-call(f32[384,512]{1,0:T(8,128)S(1)} %bitcast.42, f32[384,512]{1,0:T(8,128)S(1)} %bitcast.33, bf16[4,512,512]{2,1,0:T(8,128)(2,1)S(1)} %copy-done.1), custom_call_target="tpu_custom_call" | custom-call | flops 10000000000 | bytes 1048576 | tf_op jit(solution)/shard_map/along_x/pallas_call | solution.py:133
  14.2 1.5 %collective-permute-done.3.rest_1_ = f32[3,8,512]{2,1,0:T(8,128)S(1)} collective-permute-done((f32[3,8,512]{2,1,0:T(8,128)S(1)}, f32[3,8,512]{2,1,0:T(8,128)S(1)}, u32[]{:S(2)}, u32[]{:S(2)}) %collective-permute-start.3) | collective-permute-done | bytes 49184 | tf_op jit(solution)/shard_map/ppermute | solution.py:359
  20.9 1.5 %collective-permute-start.12 = (f32[3,16,512]{2,1,0:T(8,128)S(1)}, f32[3,16,512]{2,1,0:T(8,128)S(1)}, u32[]{:S(2)}, u32[]{:S(2)}) collective-permute-start(f32[3,16,512]{2,1,0:T(8,128)S(1)} %get-tuple-element.125), channel_id=1, source_target_pairs={{0,7},{1,6},{2,1},{3,0},{4,3},{5,2},{6,5},{7,4},{8,15},{9,14},{10,... | collective-permute-start | bytes 294920 | tf_op jit(solution)/shard_map/ppermute | solution.py:359
  23.3 1.4 %along_x.8 = (f32[384,512]{1,0:T(8,128)S(1)}, f32[384,512]{1,0:T(8,128)S(1)}) custom-call(f32[384,512]{1,0:T(8,128)S(1)} %bitcast.38, f32[384,512]{1,0:T(8,128)S(1)} %bitcast.37, bf16[4,512,512]{2,1,0:T(8,128)(2,1)S(1)} %copy-done.1), custom_call_target="tpu_custom_call" | custom-call | flops 10000000000 | bytes 1048576 | tf_op jit(solution)/shard_map/along_x/pallas_call | solution.py:133
  24.7 2.0 %collective-permute-done.11.rest_1_ = f32[3,8,512]{2,1,0:T(8,128)S(1)} collective-permute-done((f32[3,8,512]{2,1,0:T(8,128)S(1)}, f32[3,8,512]{2,1,0:T(8,128)S(1)}, u32[]{:S(2)}, u32[]{:S(2)}) %collective-permute-start.11) | collective-permute-done | bytes 49184 | tf_op jit(solution)/shard_map/ppermute | solution.py:359
  30.2 1.9 %collective-permute-start.18 = (f32[3,16,512]{2,1,0:T(8,128)S(1)}, f32[3,16,512]{2,1,0:T(8,128)S(1)}, u32[]{:S(2)}, u32[]{:S(2)}) collective-permute-start(f32[3,16,512]{2,1,0:T(8,128)S(1)} %get-tuple-element.124), channel_id=1, source_target_pairs={{0,3},{1,2},{2,5},{3,4},{4,7},{5,6},{6,1},{7,0},{8,11},{9,10},{10,... | collective-permute-start | bytes 294920 | tf_op jit(solution)/shard_map/ppermute | solution.py:359
  33.9 2.3 %along_x.9 = (f32[384,512]{1,0:T(8,128)S(1)}, f32[384,512]{1,0:T(8,128)}) custom-call(f32[384,512]{1,0:T(8,128)S(1)} %bitcast.41, f32[384,512]{1,0:T(8,128)S(1)} %bitcast.50, bf16[4,512,512]{2,1,0:T(8,128)(2,1)S(1)} %copy-done.1), custom_call_target="tpu_custom_call" | custom-call | flops 10000000000 | bytes 1048576 | tf_op jit(solution)/shard_map/along_x/pallas_call | solution.py:133
  36.2 1.4 %collective-permute-done.19.rest_1_ = f32[3,8,512]{2,1,0:T(8,128)S(1)} collective-permute-done((f32[3,8,512]{2,1,0:T(8,128)S(1)}, f32[3,8,512]{2,1,0:T(8,128)S(1)}, u32[]{:S(2)}, u32[]{:S(2)}) %collective-permute-start.19) | collective-permute-done | bytes 49184 | tf_op jit(solution)/shard_map/ppermute | solution.py:359
  38.5 4.7 %collective-permute-done.refs_0_ = f32[3,128,1024]{2,1,0:T(8,128)S(1)} collective-permute-done((f32[3,128,1024]{2,1,0:T(8,128)}, f32[3,128,1024]{2,1,0:T(8,128)S(1)}, u32[]{:S(2)}, u32[]{:S(2)}) %collective-permute-start) | collective-permute-done | bytes 1572896 | tf_op jit(solution)/shard_map/ppermute | solution.py:342
  44.9 4.3 %collective-permute-start.46 = (f32[3,128,512]{2,1,0:T(8,128)S(1)}, f32[3,128,512]{2,1,0:T(8,128)S(1)}, u32[]{:S(2)}, u32[]{:S(2)}) collective-permute-start(f32[3,128,512]{2,1,0:T(8,128)S(1)} %stage_lead.1), channel_id=1, source_target_pairs={{0,16},{8,24},{1,17},{9,25},{2,18},{10,26},{3,19},{11,27},{4,20},{... | collective-permute-start | bytes 2359304 | tf_op jit(solution)/shard_map/ppermute | solution.py:342
  49.6 1.4 %collective-permute-start.23 = (f32[3,16,512]{2,1,0:T(8,128)S(1)}, f32[3,16,512]{2,1,0:T(8,128)S(1)}, u32[]{:S(2)}, u32[]{:S(2)}) collective-permute-start(f32[3,16,512]{2,1,0:T(8,128)S(1)} %get-tuple-element.122), channel_id=1, source_target_pairs={{0,3},{1,2},{2,5},{3,4},{4,7},{5,6},{6,1},{7,0},{8,11},{9,10},{10,... | collective-permute-start | bytes 294920 | tf_op jit(solution)/shard_map/ppermute | solution.py:359
  50.9 1.3 %collective-permute-start.27 = (f32[3,16,512]{2,1,0:T(8,128)S(1)}, f32[3,16,512]{2,1,0:T(8,128)S(1)}, u32[]{:S(2)}, u32[]{:S(2)}) collective-permute-start(f32[3,16,512]{2,1,0:T(8,128)S(1)} %get-tuple-element.121), channel_id=1, source_target_pairs={{0,7},{1,6},{2,1},{3,0},{4,3},{5,2},{6,5},{7,4},{8,15},{9,14},{10,... | collective-permute-start | bytes 294920 | tf_op jit(solution)/shard_map/ppermute | solution.py:359
  53.6 1.4 %along_x.10 = (f32[384,512]{1,0:T(8,128)S(1)}, f32[384,512]{1,0:T(8,128)S(1)}) custom-call(f32[384,512]{1,0:T(8,128)S(1)} %bitcast.43, f32[384,512]{1,0:T(8,128)S(1)} %bitcast.34, bf16[4,512,512]{2,1,0:T(8,128)(2,1)S(1)} %copy-done.1), custom_call_target="tpu_custom_call" | custom-call | flops 10000000000 | bytes 1048576 | tf_op jit(solution)/shard_map/along_x/pallas_call | solution.py:133
  55.0 1.5 %collective-permute-done.25.rest_1_ = f32[3,8,512]{2,1,0:T(8,128)S(1)} collective-permute-done((f32[3,8,512]{2,1,0:T(8,128)S(1)}, f32[3,8,512]{2,1,0:T(8,128)S(1)}, u32[]{:S(2)}, u32[]{:S(2)}) %collective-permute-start.25) | collective-permute-done | bytes 49184 | tf_op jit(solution)/shard_map/ppermute | solution.py:359
  60.3 1.4 %collective-permute-start.31 = (f32[3,16,512]{2,1,0:T(8,128)S(1)}, f32[3,16,512]{2,1,0:T(8,128)S(1)}, u32[]{:S(2)}, u32[]{:S(2)}) collective-permute-start(f32[3,16,512]{2,1,0:T(8,128)S(1)} %get-tuple-element.120), channel_id=1, source_target_pairs={{0,3},{1,2},{2,5},{3,4},{4,7},{5,6},{6,1},{7,0},{8,11},{9,10},{10,... | collective-permute-start | bytes 294920 | tf_op jit(solution)/shard_map/ppermute | solution.py:359
  63.9 1.4 %along_x.11 = (f32[384,512]{1,0:T(8,128)S(1)}, f32[384,512]{1,0:T(8,128)S(1)}) custom-call(f32[384,512]{1,0:T(8,128)S(1)} %bitcast.31, f32[384,512]{1,0:T(8,128)S(1)} %bitcast.32, bf16[4,512,512]{2,1,0:T(8,128)(2,1)S(1)} %copy-done.1), custom_call_target="tpu_custom_call" | custom-call | flops 10000000000 | bytes 1048576 | tf_op jit(solution)/shard_map/along_x/pallas_call | solution.py:133
  65.3 2.0 %collective-permute-done.33.rest_1_ = f32[3,8,512]{2,1,0:T(8,128)S(1)} collective-permute-done((f32[3,8,512]{2,1,0:T(8,128)S(1)}, f32[3,8,512]{2,1,0:T(8,128)S(1)}, u32[]{:S(2)}, u32[]{:S(2)}) %collective-permute-start.33) | collective-permute-done | bytes 49184 | tf_op jit(solution)/shard_map/ppermute | solution.py:359
  70.8 2.0 %collective-permute-start.39 = (f32[3,16,512]{2,1,0:T(8,128)S(1)}, f32[3,16,512]{2,1,0:T(8,128)S(1)}, u32[]{:S(2)}, u32[]{:S(2)}) collective-permute-start(f32[3,16,512]{2,1,0:T(8,128)S(1)} %get-tuple-element.118), channel_id=1, source_target_pairs={{0,3},{1,2},{2,5},{3,4},{4,7},{5,6},{6,1},{7,0},{8,11},{9,10},{10,... | collective-permute-start | bytes 294920 | tf_op jit(solution)/shard_map/ppermute | solution.py:359
  74.4 1.4 %along_x.12 = (f32[384,512]{1,0:T(8,128)S(1)}, f32[384,512]{1,0:T(8,128)S(1)}) custom-call(f32[384,512]{1,0:T(8,128)S(1)} %bitcast.36, f32[384,512]{1,0:T(8,128)S(1)} %bitcast.35, bf16[4,512,512]{2,1,0:T(8,128)(2,1)S(1)} %copy-done.1), custom_call_target="tpu_custom_call" | custom-call | flops 10000000000 | bytes 1048576 | tf_op jit(solution)/shard_map/along_x/pallas_call | solution.py:133
  75.8 2.3 %collective-permute-done.41.rest_1_ = f32[3,8,512]{2,1,0:T(8,128)S(1)} collective-permute-done((f32[3,8,512]{2,1,0:T(8,128)S(1)}, f32[3,8,512]{2,1,0:T(8,128)S(1)}, u32[]{:S(2)}, u32[]{:S(2)}) %collective-permute-start.41) | collective-permute-done | bytes 49184 | tf_op jit(solution)/shard_map/ppermute | solution.py:359
  80.8 1.9 %collective-permute-start.45 = (f32[3,128,512]{2,1,0:T(8,128)S(1)}, f32[3,128,512]{2,1,0:T(8,128)S(1)}, u32[]{:S(2)}, u32[]{:S(2)}) collective-permute-start(f32[3,128,512]{2,1,0:T(8,128)S(1)} %get-tuple-element.100), channel_id=1, source_target_pairs={{0,8},{8,16},{16,24},{1,9},{9,17},{17,25},{2,10},{10,18},{18,26},{... | collective-permute-start | bytes 2359304 | tf_op jit(solution)/shard_map/ppermute | solution.py:342
  84.0 17.4 %collective-permute-done.45.refs_0_ = f32[3,128,512]{2,1,0:T(8,128)S(1)} collective-permute-done((f32[3,128,512]{2,1,0:T(8,128)S(1)}, f32[3,128,512]{2,1,0:T(8,128)S(1)}, u32[]{:S(2)}, u32[]{:S(2)}) %collective-permute-start.45) | collective-permute-done | bytes 786464 | tf_op jit(solution)/shard_map/ppermute | solution.py:342
  101.9 2.9 %collective-permute-start.49 = (f32[3,16,512]{2,1,0:T(8,128)S(1)}, f32[3,16,512]{2,1,0:T(8,128)S(1)}, u32[]{:S(2)}, u32[]{:S(2)}) collective-permute-start(f32[3,16,512]{2,1,0:T(8,128)S(1)} %get-tuple-element.116), channel_id=1, source_target_pairs={{0,3},{1,2},{2,5},{3,4},{4,7},{5,6},{6,1},{7,0},{8,11},{9,10},{10,... | collective-permute-start | bytes 294920 | tf_op jit(solution)/shard_map/ppermute | solution.py:359
  104.9 1.5 %collective-permute-start.53 = (f32[3,16,512]{2,1,0:T(8,128)S(1)}, f32[3,16,512]{2,1,0:T(8,128)S(1)}, u32[]{:S(2)}, u32[]{:S(2)}) collective-permute-start(f32[3,16,512]{2,1,0:T(8,128)S(1)} %get-tuple-element.115), channel_id=1, source_target_pairs={{0,7},{1,6},{2,1},{3,0},{4,3},{5,2},{6,5},{7,4},{8,15},{9,14},{10,... | collective-permute-start | bytes 294920 | tf_op jit(solution)/shard_map/ppermute | solution.py:359
  106.8 1.4 %along_x.13 = (f32[384,512]{1,0:T(8,128)S(1)}, f32[384,512]{1,0:T(8,128)S(1)}) custom-call(f32[384,512]{1,0:T(8,128)S(1)} %bitcast.40, f32[384,512]{1,0:T(8,128)S(1)} %bitcast.39, bf16[4,512,512]{2,1,0:T(8,128)(2,1)S(1)} %copy-done.1), custom_call_target="tpu_custom_call" | custom-call | flops 10000000000 | bytes 1048576 | tf_op jit(solution)/shard_map/along_x/pallas_call | solution.py:133
  108.2 1.8 %collective-permute-done.51.rest_1_ = f32[3,8,512]{2,1,0:T(8,128)S(1)} collective-permute-done((f32[3,8,512]{2,1,0:T(8,128)S(1)}, f32[3,8,512]{2,1,0:T(8,128)S(1)}, u32[]{:S(2)}, u32[]{:S(2)}) %collective-permute-start.51) | collective-permute-done | bytes 49184 | tf_op jit(solution)/shard_map/ppermute | solution.py:359
  111.8 1.5 %stage_join.1 = f32[3,128,1024]{2,1,0:T(8,128)} custom-call(f32[3,128,512]{2,1,0:T(8,128)S(1)} %get-tuple-element.102.state_ref, f32[3,128,512]{2,1,0:T(8,128)S(1)} %bitcast.49, f32[128,1]{1,0:T(8,128)S(1)} %get-tuple-element.63.turning_ref, f32[3,16,512]{2,1,0:T(8,128)S(1)} %collective-permute-done.50.rest_0_, ...), custom_call_target="tpu_custom_call" | custom-call | flops 10000000000 | bytes 1048576 | tf_op jit(solution)/shard_map/stage_join/pallas_call | solution.py:133
  (140 shorter events, 36.8 us)
Async XLA Ops:
  4.4 4.3 %collective-permute-start.1 = (f32[3,56,512]{2,1,0:T(8,128)S(1)}, f32[3,56,512]{2,1,0:T(8,128)S(1)}, u32[]{:S(2)}, u32[]{:S(2)}) collective-permute-start(f32[3,56,512]{2,1,0:T(8,128)S(1)} %get-tuple-element.65), channel_id=1, source_target_pairs={{0,1},{1,0},{2,3},{3,2},{4,5},{5,4},{6,7},{7,6},{8,9},{9,8},{10,11... | collective-permute-start | bytes 1032200 | tf_op jit(solution)/shard_map/ppermute | solution.py:347
  5.1 38.1 %collective-permute-start = (f32[3,128,1024]{2,1,0:T(8,128)}, f32[3,128,1024]{2,1,0:T(8,128)S(1)}, u32[]{:S(2)}, u32[]{:S(2)}) collective-permute-start(f32[3,128,1024]{2,1,0:T(8,128)} %bitcast.own_ref), channel_id=1, source_target_pairs={{0,8},{8,16},{16,24},{1,9},{9,17},{17,25},{2,10},{10,18},{18,26},{... | collective-permute-start | bytes 4718600 | tf_op jit(solution)/shard_map/ppermute | solution.py:342
  8.3 8.5 %collective-permute-start.5 = (f32[3,16,512]{2,1,0:T(8,128)S(1)}, f32[3,16,512]{2,1,0:T(8,128)S(1)}, u32[]{:S(2)}, u32[]{:S(2)}) collective-permute-start(f32[3,16,512]{2,1,0:T(8,128)S(1)} %slice.131), channel_id=1, source_target_pairs={{0,1},{1,0},{2,3},{3,2},{4,5},{5,4},{6,7},{7,6},{8,9},{9,8},{10,11... | collective-permute-start | bytes 294920 | tf_op jit(solution)/shard_map/ppermute | solution.py:347
  8.8 7.1 %collective-permute-start.2 = (f32[3,16,512]{2,1,0:T(8,128)S(1)}, f32[3,16,512]{2,1,0:T(8,128)S(1)}, u32[]{:S(2)}, u32[]{:S(2)}) collective-permute-start(f32[3,16,512]{2,1,0:T(8,128)S(1)} %get-tuple-element.128), channel_id=1, source_target_pairs={{0,3},{1,2},{2,5},{3,4},{4,7},{5,6},{6,1},{7,0},{8,11},{9,10},{10,... | collective-permute-start | bytes 294920 | tf_op jit(solution)/shard_map/ppermute | solution.py:359
  10.1 6.7 %collective-permute-start.4 = (f32[3,16,512]{2,1,0:T(8,128)S(1)}, f32[3,16,512]{2,1,0:T(8,128)S(1)}, u32[]{:S(2)}, u32[]{:S(2)}) collective-permute-start(f32[3,16,512]{2,1,0:T(8,128)S(1)} %get-tuple-element.127), channel_id=1, source_target_pairs={{0,7},{1,6},{2,1},{3,0},{4,3},{5,2},{6,5},{7,4},{8,15},{9,14},{10,... | collective-permute-start | bytes 294920 | tf_op jit(solution)/shard_map/ppermute | solution.py:359
  11.5 4.2 %collective-permute-start.3 = (f32[3,8,512]{2,1,0:T(8,128)S(1)}, f32[3,8,512]{2,1,0:T(8,128)S(1)}, u32[]{:S(2)}, u32[]{:S(2)}) collective-permute-start(f32[3,8,512]{2,1,0:T(8,128)S(1)} %slice.170), channel_id=1, source_target_pairs={{0,5},{1,4},{2,7},{3,6},{4,1},{5,0},{6,3},{7,2},{8,13},{9,12},{10,... | collective-permute-start | bytes 147464 | tf_op jit(solution)/shard_map/ppermute | solution.py:359
  19.3 8.2 %collective-permute-start.13 = (f32[3,16,512]{2,1,0:T(8,128)S(1)}, f32[3,16,512]{2,1,0:T(8,128)S(1)}, u32[]{:S(2)}, u32[]{:S(2)}) collective-permute-start(f32[3,16,512]{2,1,0:T(8,128)S(1)} %slice.137), channel_id=1, source_target_pairs={{0,1},{1,0},{2,3},{3,2},{4,5},{5,4},{6,7},{7,6},{8,9},{9,8},{10,11... | collective-permute-start | bytes 294920 | tf_op jit(solution)/shard_map/ppermute | solution.py:347
  19.7 7.3 %collective-permute-start.10 = (f32[3,16,512]{2,1,0:T(8,128)S(1)}, f32[3,16,512]{2,1,0:T(8,128)S(1)}, u32[]{:S(2)}, u32[]{:S(2)}) collective-permute-start(f32[3,16,512]{2,1,0:T(8,128)S(1)} %get-tuple-element.126), channel_id=1, source_target_pairs={{0,3},{1,2},{2,5},{3,4},{4,7},{5,6},{6,1},{7,0},{8,11},{9,10},{10,... | collective-permute-start | bytes 294920 | tf_op jit(solution)/shard_map/ppermute | solution.py:359
  20.9 6.4 %collective-permute-start.12 = (f32[3,16,512]{2,1,0:T(8,128)S(1)}, f32[3,16,512]{2,1,0:T(8,128)S(1)}, u32[]{:S(2)}, u32[]{:S(2)}) collective-permute-start(f32[3,16,512]{2,1,0:T(8,128)S(1)} %get-tuple-element.125), channel_id=1, source_target_pairs={{0,7},{1,6},{2,1},{3,0},{4,3},{5,2},{6,5},{7,4},{8,15},{9,14},{10,... | collective-permute-start | bytes 294920 | tf_op jit(solution)/shard_map/ppermute | solution.py:359
  22.4 4.3 %collective-permute-start.11 = (f32[3,8,512]{2,1,0:T(8,128)S(1)}, f32[3,8,512]{2,1,0:T(8,128)S(1)}, u32[]{:S(2)}, u32[]{:S(2)}) collective-permute-start(f32[3,8,512]{2,1,0:T(8,128)S(1)} %slice.174), channel_id=1, source_target_pairs={{0,5},{1,4},{2,7},{3,6},{4,1},{5,0},{6,3},{7,2},{8,13},{9,12},{10,... | collective-permute-start | bytes 147464 | tf_op jit(solution)/shard_map/ppermute | solution.py:359
  29.7 6.4 %collective-permute-start.21 = (f32[3,16,512]{2,1,0:T(8,128)S(1)}, f32[3,16,512]{2,1,0:T(8,128)S(1)}, u32[]{:S(2)}, u32[]{:S(2)}) collective-permute-start(f32[3,16,512]{2,1,0:T(8,128)S(1)} %slice.143), channel_id=1, source_target_pairs={{0,1},{1,0},{2,3},{3,2},{4,5},{5,4},{6,7},{7,6},{8,9},{9,8},{10,11... | collective-permute-start | bytes 294920 | tf_op jit(solution)/shard_map/ppermute | solution.py:347
  30.2 7.4 %collective-permute-start.18 = (f32[3,16,512]{2,1,0:T(8,128)S(1)}, f32[3,16,512]{2,1,0:T(8,128)S(1)}, u32[]{:S(2)}, u32[]{:S(2)}) collective-permute-start(f32[3,16,512]{2,1,0:T(8,128)S(1)} %get-tuple-element.124), channel_id=1, source_target_pairs={{0,3},{1,2},{2,5},{3,4},{4,7},{5,6},{6,1},{7,0},{8,11},{9,10},{10,... | collective-permute-start | bytes 294920 | tf_op jit(solution)/shard_map/ppermute | solution.py:359
  32.1 5.7 %collective-permute-start.20 = (f32[3,16,512]{2,1,0:T(8,128)S(1)}, f32[3,16,512]{2,1,0:T(8,128)S(1)}, u32[]{:S(2)}, u32[]{:S(2)}) collective-permute-start(f32[3,16,512]{2,1,0:T(8,128)S(1)} %get-tuple-element.123), channel_id=1, source_target_pairs={{0,7},{1,6},{2,1},{3,0},{4,3},{5,2},{6,5},{7,4},{8,15},{9,14},{10,... | collective-permute-start | bytes 294920 | tf_op jit(solution)/shard_map/ppermute | solution.py:359
  44.0 5.5 %collective-permute-start.22 = (f32[3,56,512]{2,1,0:T(8,128)S(1)}, f32[3,56,512]{2,1,0:T(8,128)S(1)}, u32[]{:S(2)}, u32[]{:S(2)}) collective-permute-start(f32[3,56,512]{2,1,0:T(8,128)S(1)} %get-tuple-element.85), channel_id=1, source_target_pairs={{0,1},{1,0},{2,3},{3,2},{4,5},{5,4},{6,7},{7,6},{8,9},{9,8},{10,11... | collective-permute-start | bytes 1032200 | tf_op jit(solution)/shard_map/ppermute | solution.py:347
  44.9 38.2 %collective-permute-start.46 = (f32[3,128,512]{2,1,0:T(8,128)S(1)}, f32[3,128,512]{2,1,0:T(8,128)S(1)}, u32[]{:S(2)}, u32[]{:S(2)}) collective-permute-start(f32[3,128,512]{2,1,0:T(8,128)S(1)} %stage_lead.1), channel_id=1, source_target_pairs={{0,16},{8,24},{1,17},{9,25},{2,18},{10,26},{3,19},{11,27},{4,20},{... | collective-permute-start | bytes 2359304 | tf_op jit(solution)/shard_map/ppermute | solution.py:342
  49.1 8.5 %collective-permute-start.29 = (f32[3,16,512]{2,1,0:T(8,128)S(1)}, f32[3,16,512]{2,1,0:T(8,128)S(1)}, u32[]{:S(2)}, u32[]{:S(2)}) collective-permute-start(f32[3,16,512]{2,1,0:T(8,128)S(1)} %slice.149), channel_id=1, source_target_pairs={{0,1},{1,0},{2,3},{3,2},{4,5},{5,4},{6,7},{7,6},{8,9},{9,8},{10,11... | collective-permute-start | bytes 294920 | tf_op jit(solution)/shard_map/ppermute | solution.py:347
  49.6 7.1 %collective-permute-start.23 = (f32[3,16,512]{2,1,0:T(8,128)S(1)}, f32[3,16,512]{2,1,0:T(8,128)S(1)}, u32[]{:S(2)}, u32[]{:S(2)}) collective-permute-start(f32[3,16,512]{2,1,0:T(8,128)S(1)} %get-tuple-element.122), channel_id=1, source_target_pairs={{0,3},{1,2},{2,5},{3,4},{4,7},{5,6},{6,1},{7,0},{8,11},{9,10},{10,... | collective-permute-start | bytes 294920 | tf_op jit(solution)/shard_map/ppermute | solution.py:359
  50.9 6.4 %collective-permute-start.27 = (f32[3,16,512]{2,1,0:T(8,128)S(1)}, f32[3,16,512]{2,1,0:T(8,128)S(1)}, u32[]{:S(2)}, u32[]{:S(2)}) collective-permute-start(f32[3,16,512]{2,1,0:T(8,128)S(1)} %get-tuple-element.121), channel_id=1, source_target_pairs={{0,7},{1,6},{2,1},{3,0},{4,3},{5,2},{6,5},{7,4},{8,15},{9,14},{10,... | collective-permute-start | bytes 294920 | tf_op jit(solution)/shard_map/ppermute | solution.py:359
  52.3 4.2 %collective-permute-start.25 = (f32[3,8,512]{2,1,0:T(8,128)S(1)}, f32[3,8,512]{2,1,0:T(8,128)S(1)}, u32[]{:S(2)}, u32[]{:S(2)}) collective-permute-start(f32[3,8,512]{2,1,0:T(8,128)S(1)} %slice.182), channel_id=1, source_target_pairs={{0,5},{1,4},{2,7},{3,6},{4,1},{5,0},{6,3},{7,2},{8,13},{9,12},{10,... | collective-permute-start | bytes 147464 | tf_op jit(solution)/shard_map/ppermute | solution.py:359
  59.8 8.3 %collective-permute-start.37 = (f32[3,16,512]{2,1,0:T(8,128)S(1)}, f32[3,16,512]{2,1,0:T(8,128)S(1)}, u32[]{:S(2)}, u32[]{:S(2)}) collective-permute-start(f32[3,16,512]{2,1,0:T(8,128)S(1)} %slice.155), channel_id=1, source_target_pairs={{0,1},{1,0},{2,3},{3,2},{4,5},{5,4},{6,7},{7,6},{8,9},{9,8},{10,11... | collective-permute-start | bytes 294920 | tf_op jit(solution)/shard_map/ppermute | solution.py:347
  60.3 7.2 %collective-permute-start.31 = (f32[3,16,512]{2,1,0:T(8,128)S(1)}, f32[3,16,512]{2,1,0:T(8,128)S(1)}, u32[]{:S(2)}, u32[]{:S(2)}) collective-permute-start(f32[3,16,512]{2,1,0:T(8,128)S(1)} %get-tuple-element.120), channel_id=1, source_target_pairs={{0,3},{1,2},{2,5},{3,4},{4,7},{5,6},{6,1},{7,0},{8,11},{9,10},{10,... | collective-permute-start | bytes 294920 | tf_op jit(solution)/shard_map/ppermute | solution.py:359
  61.7 6.1 %collective-permute-start.35 = (f32[3,16,512]{2,1,0:T(8,128)S(1)}, f32[3,16,512]{2,1,0:T(8,128)S(1)}, u32[]{:S(2)}, u32[]{:S(2)}) collective-permute-start(f32[3,16,512]{2,1,0:T(8,128)S(1)} %get-tuple-element.119), channel_id=1, source_target_pairs={{0,7},{1,6},{2,1},{3,0},{4,3},{5,2},{6,5},{7,4},{8,15},{9,14},{10,... | collective-permute-start | bytes 294920 | tf_op jit(solution)/shard_map/ppermute | solution.py:359
  63.0 4.3 %collective-permute-start.33 = (f32[3,8,512]{2,1,0:T(8,128)S(1)}, f32[3,8,512]{2,1,0:T(8,128)S(1)}, u32[]{:S(2)}, u32[]{:S(2)}) collective-permute-start(f32[3,8,512]{2,1,0:T(8,128)S(1)} %slice.186), channel_id=1, source_target_pairs={{0,5},{1,4},{2,7},{3,6},{4,1},{5,0},{6,3},{7,2},{8,13},{9,12},{10,... | collective-permute-start | bytes 147464 | tf_op jit(solution)/shard_map/ppermute | solution.py:359
  70.3 8.6 %collective-permute-start.47 = (f32[3,16,512]{2,1,0:T(8,128)S(1)}, f32[3,16,512]{2,1,0:T(8,128)S(1)}, u32[]{:S(2)}, u32[]{:S(2)}) collective-permute-start(f32[3,16,512]{2,1,0:T(8,128)S(1)} %slice.161), channel_id=1, source_target_pairs={{0,1},{1,0},{2,3},{3,2},{4,5},{5,4},{6,7},{7,6},{8,9},{9,8},{10,11... | collective-permute-start | bytes 294920 | tf_op jit(solution)/shard_map/ppermute | solution.py:347
  70.8 7.6 %collective-permute-start.39 = (f32[3,16,512]{2,1,0:T(8,128)S(1)}, f32[3,16,512]{2,1,0:T(8,128)S(1)}, u32[]{:S(2)}, u32[]{:S(2)}) collective-permute-start(f32[3,16,512]{2,1,0:T(8,128)S(1)} %get-tuple-element.118), channel_id=1, source_target_pairs={{0,3},{1,2},{2,5},{3,4},{4,7},{5,6},{6,1},{7,0},{8,11},{9,10},{10,... | collective-permute-start | bytes 294920 | tf_op jit(solution)/shard_map/ppermute | solution.py:359
  72.7 5.9 %collective-permute-start.43 = (f32[3,16,512]{2,1,0:T(8,128)S(1)}, f32[3,16,512]{2,1,0:T(8,128)S(1)}, u32[]{:S(2)}, u32[]{:S(2)}) collective-permute-start(f32[3,16,512]{2,1,0:T(8,128)S(1)} %get-tuple-element.117), channel_id=1, source_target_pairs={{0,7},{1,6},{2,1},{3,0},{4,3},{5,2},{6,5},{7,4},{8,15},{9,14},{10,... | collective-permute-start | bytes 294920 | tf_op jit(solution)/shard_map/ppermute | solution.py:359
  73.9 4.2 %collective-permute-start.41 = (f32[3,8,512]{2,1,0:T(8,128)S(1)}, f32[3,8,512]{2,1,0:T(8,128)S(1)}, u32[]{:S(2)}, u32[]{:S(2)}) collective-permute-start(f32[3,8,512]{2,1,0:T(8,128)S(1)} %slice.190), channel_id=1, source_target_pairs={{0,5},{1,4},{2,7},{3,6},{4,1},{5,0},{6,3},{7,2},{8,13},{9,12},{10,... | collective-permute-start | bytes 147464 | tf_op jit(solution)/shard_map/ppermute | solution.py:359
  80.8 20.7 %collective-permute-start.45 = (f32[3,128,512]{2,1,0:T(8,128)S(1)}, f32[3,128,512]{2,1,0:T(8,128)S(1)}, u32[]{:S(2)}, u32[]{:S(2)}) collective-permute-start(f32[3,128,512]{2,1,0:T(8,128)S(1)} %get-tuple-element.100), channel_id=1, source_target_pairs={{0,8},{8,16},{16,24},{1,9},{9,17},{17,25},{2,10},{10,18},{18,26},{... | collective-permute-start | bytes 2359304 | tf_op jit(solution)/shard_map/ppermute | solution.py:342
  83.5 18.3 %collective-permute-start.48 = (f32[3,56,512]{2,1,0:T(8,128)S(1)}, f32[3,56,512]{2,1,0:T(8,128)S(1)}, u32[]{:S(2)}, u32[]{:S(2)}) collective-permute-start(f32[3,56,512]{2,1,0:T(8,128)S(1)} %get-tuple-element.111), channel_id=1, source_target_pairs={{0,1},{1,0},{2,3},{3,2},{4,5},{5,4},{6,7},{7,6},{8,9},{9,8},{10,11... | collective-permute-start | bytes 1032200 | tf_op jit(solution)/shard_map/ppermute | solution.py:347
  101.9 8.1 %collective-permute-start.49 = (f32[3,16,512]{2,1,0:T(8,128)S(1)}, f32[3,16,512]{2,1,0:T(8,128)S(1)}, u32[]{:S(2)}, u32[]{:S(2)}) collective-permute-start(f32[3,16,512]{2,1,0:T(8,128)S(1)} %get-tuple-element.116), channel_id=1, source_target_pairs={{0,3},{1,2},{2,5},{3,4},{4,7},{5,6},{6,1},{7,0},{8,11},{9,10},{10,... | collective-permute-start | bytes 294920 | tf_op jit(solution)/shard_map/ppermute | solution.py:359
  104.9 5.6 %collective-permute-start.53 = (f32[3,16,512]{2,1,0:T(8,128)S(1)}, f32[3,16,512]{2,1,0:T(8,128)S(1)}, u32[]{:S(2)}, u32[]{:S(2)}) collective-permute-start(f32[3,16,512]{2,1,0:T(8,128)S(1)} %get-tuple-element.115), channel_id=1, source_target_pairs={{0,7},{1,6},{2,1},{3,0},{4,3},{5,2},{6,5},{7,4},{8,15},{9,14},{10,... | collective-permute-start | bytes 294920 | tf_op jit(solution)/shard_map/ppermute | solution.py:359
  106.4 4.2 %collective-permute-start.55 = (f32[3,16,512]{2,1,0:T(8,128)S(1)}, f32[3,16,512]{2,1,0:T(8,128)S(1)}, u32[]{:S(2)}, u32[]{:S(2)}) collective-permute-start(f32[3,16,512]{2,1,0:T(8,128)S(1)} %slice.167), channel_id=1, source_target_pairs={{0,1},{1,0},{2,3},{3,2},{4,5},{5,4},{6,7},{7,6},{8,9},{9,8},{10,11... | collective-permute-start | bytes 294920 | tf_op jit(solution)/shard_map/ppermute | solution.py:347
  (28 other events, 59.3 us)

commit v5 on v4

--- a/solution.py
+++ b/solution.py
@@ -202,54 +202,62 @@
     return rate_h, rate_u, rate_v
 
 
-def enter_call(plan, state, received, send, coriolis=None, both_apply=None):
-    sources = [state, *received]
-    opening = coriolis is not None
-    more = [both_apply, coriolis] if opening else []
-
-    def body(own_ref, *refs):
-        received_refs, (send_ref, *refs) = refs[: len(received)], refs[len(received) :]
+def enter_call(plan, state, received=None, tables=None, send=None):
+    sources = [state] if received is None else [state, received]
+    opening = tables is not None
+    held_in = pltpu.HBM if opening else pltpu.VMEM
+    more = [pltpu.with_memory_space_constraint(a, held_in) for a in (tables if opening else [send])]
+
+    def body(*refs):
+        source_refs, refs = refs[: len(sources)], refs[len(sources) :]
         more_refs, outs = refs[: len(more)], refs[len(more) :]
         nexts, moments, arrived = outs[0:4:2], outs[1:4:2], outs[-1]
 
         def copy(source_ref, at):
-            cols = plan.columns(at == 1)
-            return pltpu.make_async_copy(source_ref.at[:, :, cols], nexts[at], arrived.at[at])
+            return pltpu.make_async_copy(source_ref.at[:, :, plan.columns(at == 1)], nexts[at], arrived.at[at])
 
         def start(source_ref):
             for at in range(2):
                 copy(source_ref, at).start()
 
-        if received:
-            pl.when(lax.axis_index("tm") == 0)(lambda: start(own_ref))
-            pl.when(lax.axis_index("tm") != 0)(lambda: start(received_refs[0]))
-        else:
-            start(own_ref)
         if opening:
-            outs[4][...] = send_ref[member_of_pair()]
-            outs[5][...] = more_refs[0][member_of_pair()]
+            picks = [
+                pltpu.make_async_copy(more_refs[n].at[member_of_pair()], outs[4 + n], arrived.at[2 + n]) for n in range(2)
+            ]
+            picks.append(pltpu.make_async_copy(more_refs[2], outs[-2], arrived.at[4]))
+            for pick in picks:
+                pick.start()
+            start(source_refs[0])
+            for pick in picks:
+                pick.wait()
             square = (plan.rows, plan.rows)
             here = lax.broadcasted_iota(jnp.int32, square, 0) == lax.broadcasted_iota(jnp.int32, square, 1)
-            outs[6][...] = jnp.sum(jnp.where(here, more_refs[1][...], 0.0), axis=1, keepdims=True)
-            send_ref = outs[4]
+            outs[6][...] = jnp.sum(jnp.where(here, outs[-2][...], 0.0), axis=1, keepdims=True)
+        else:
+            first = lax.axis_index("tm") == 0
+            pl.when(first)(lambda: start(source_refs[0]))
+            pl.when(jnp.logical_not(first))(lambda: start(source_refs[1]))
+        send_ref = outs[4] if opening else more_refs[0]
         for at in range(2):
-            copy(own_ref, at).wait()
+            copy(source_refs[0], at).wait()
             plan.emit_moments(nexts[at], send_ref, moments[at])
 
     shapes = [plan.state, *plan.moments] * 2
+    scratch = [pltpu.SemaphoreType.DMA((5,))]
     if opening:
-        shapes += [jax.ShapeDtypeStruct(a.shape[1:], a.dtype) for a in (send, both_apply)]
+        shapes += [jax.ShapeDtypeStruct(a.shape[1:], a.dtype) for a in tables[:2]]
         shapes.append(jax.ShapeDtypeStruct((plan.rows, 1), F32))
+        scratch.insert(0, pltpu.VMEM((1, plan.rows), F32))
     return pl.pallas_call(
         body,
-        in_specs=[HBM] * len(sources) + [VMEM] * (1 + len(more)),
+        in_specs=[HBM] * len(sources) + [HBM if opening else VMEM] * len(more),
         out_specs=[VMEM] * len(shapes),
         out_shape=[pltpu.VMEM(s.shape, s.dtype) for s in shapes],
-        scratch_shapes=[pltpu.SemaphoreType.DMA((2,))],
+        scratch_shapes=scratch,
         compiler_params=pltpu.CompilerParams(vmem_limit_bytes=KERNEL_BYTES),
         cost_estimate=COST,
         name="enter",
-    )(*sources, *[pltpu.with_memory_space_constraint(a, pltpu.VMEM) for a in (send, *more)])
+    )(*sources, *more)
 
 
 def field_of(refs, f):
@@ -380,7 +388,7 @@
 
     before = ahead_in_time(own, 1)
     both_send, both_apply = jnp.asarray(send_tables), jnp.asarray(apply_tables)
-    opened = enter_call(plan, own, [], both_send, coriolis[None, :], both_apply)
+    opened = enter_call(plan, own, tables=(both_send, both_apply, coriolis[None, :]))
     states, moments, (send, apply, turning) = opened[0:4:2], list(opened[1:4:2]), opened[4:]
     states, moments = stage(("move", "move"), states, moments, sends=True)
     states, moments = stage(("move", "move"), states, moments, sends=True)
@@ -388,7 +396,7 @@
     far = [ahead_in_time(fields, 2) for fields in lead]
 
     before, _ = lax.optimization_barrier((before, lead[0]))
-    entered = enter_call(plan, own, [before], send)
+    entered = enter_call(plan, own, before, send=send)
     states, moments = entered[0::2], list(entered[1::2])
     nodes_one, rates_zero, moments = stage(("keep", "keep"), states, moments, sends=True)
     states, rates_one, moments = stage(("keep", "keep"), nodes_one, moments, sends=True)

time: 115 us -> 112 us (0.974)
  local copies, waits for them, and re-layouts: 2.65 us -> 0.21 us
    unnamed x8 -> x2, local copies, waits for them, and re-layouts: 2.45 us -> 0.01 us
  transfers between devices with their start and end apart: 56 -> 56, of which waited for: 20 -> 20; matrix products, arithmetic and copies ran while one was open for 0% -> 0% of each run, Pallas kernels for 19% -> 20%
where the time goes in v5:
time: 112 us; the launch traced here: 111 us
  starting transfers between devices  46.4 us (41%)
  waiting for transfers between devices  37.6 us (34%)
  Pallas kernels  26.1 us (23%)
    ppermute x21, starting transfers between devices, exchange(): lax.ppermute(part, 'grid', [(i, (i + 2 * d) % size ^ 1) for i in range(si...  27 us
    pallas_call x22, Pallas kernels, on_chip_call(): pl.pallas_call(body, in_specs=[VMEM] * len(held), out_specs=[VMEM if keep...  23.3 us
    ppermute x3, waiting for transfers between devices, ahead_in_time(): return lax.ppermute(array, 'tm', [(i, i + by) for i in range(size - by)])  22.6 us
    ppermute x21, waiting for transfers between devices, exchange(): lax.ppermute(part, 'grid', [(i, (i + 2 * d) % size ^ 1) for i in range(si...  13.7 us
    ppermute x32, starting transfers between devices, mate_swap(): return lax.ppermute(array, 'grid', [(i, i ^ 1) for i in range(size)])  10 us
    ppermute x3, starting transfers between devices, ahead_in_time(): return lax.ppermute(array, 'tm', [(i, i + by) for i in range(size - by)])  9.37 us
    pallas_call x2, Pallas kernels, enter_call(): pl.pallas_call(body, in_specs=[HBM] * len(sources) + [HBM if opening else...  2.83 us
  transfers between devices with their start and end apart: 56, of which 20 were waited for; matrix products, arithmetic and copies ran while one was open for 0% of the time, Pallas kernels for 20%

profile of v5, /device:TPU:9, one launch (start us, length us, event | category | flops | bytes accessed | tf_op | source)
XLA Modules:
  0.0 111.2 jit_solution(13717863057053004018)
XLA Ops:
  0.0 2.0 %enter.2 = (f32[3,128,512]{2,1,0:T(8,128)S(1)}, f32[3,56,512]{2,1,0:T(8,128)S(1)}, f32[3,128,512]{2,1,0:T(8,128)S(1)}, f32[3,56,512]{2,1,0:T(8,128)S(1)}, bf16[1...) custom-call(f32[3,128,1024]{2,1,0:T(8,128)} %bitcast.refs_0_, ...), custom_call_target="tpu_custom_call" | custom-call | flops 10000000000 | bytes 1048576 | tf_op jit(solution)/shard_map/enter/pallas_call | solution.py:251
  2.8 3.2 %collective-permute-start = (f32[3,128,1024]{2,1,0:T(8,128)}, f32[3,128,1024]{2,1,0:T(8,128)S(1)}, u32[]{:S(2)}, u32[]{:S(2)}) collective-permute-start(f32[3,128,1024]{2,1,0:T(8,128)} %bitcast.refs_0_), channel_id=1, source_target_pairs={{0,8},{8,16},{16,24},{1,9},{9,17},{17,25},{2,10},{10,18},{18,26},{... | collective-permute-start | bytes 4718600 | tf_op jit(solution)/shard_map/ppermute | solution.py:350
  6.5 1.4 %collective-permute-start.2 = (f32[3,16,512]{2,1,0:T(8,128)S(1)}, f32[3,16,512]{2,1,0:T(8,128)S(1)}, u32[]{:S(2)}, u32[]{:S(2)}) collective-permute-start(f32[3,16,512]{2,1,0:T(8,128)S(1)} %get-tuple-element.128), channel_id=1, source_target_pairs={{0,3},{1,2},{2,5},{3,4},{4,7},{5,6},{6,1},{7,0},{8,11},{9,10},{10,... | collective-permute-start | bytes 294920 | tf_op jit(solution)/shard_map/ppermute | solution.py:367
  7.8 1.3 %collective-permute-start.4 = (f32[3,16,512]{2,1,0:T(8,128)S(1)}, f32[3,16,512]{2,1,0:T(8,128)S(1)}, u32[]{:S(2)}, u32[]{:S(2)}) collective-permute-start(f32[3,16,512]{2,1,0:T(8,128)S(1)} %get-tuple-element.127), channel_id=1, source_target_pairs={{0,7},{1,6},{2,1},{3,0},{4,3},{5,2},{6,5},{7,4},{8,15},{9,14},{10,... | collective-permute-start | bytes 294920 | tf_op jit(solution)/shard_map/ppermute | solution.py:367
  10.5 1.4 %along_x.7 = (f32[384,512]{1,0:T(8,128)S(1)}, f32[384,512]{1,0:T(8,128)S(1)}) custom-call(f32[384,512]{1,0:T(8,128)S(1)} %bitcast.41, f32[384,512]{1,0:T(8,128)S(1)} %bitcast.32, bf16[4,512,512]{2,1,0:T(8,128)(2,1)S(1)} %copy-done), custom_call_target="tpu_custom_call" | custom-call | flops 10000000000 | bytes 1048576 | tf_op jit(solution)/shard_map/along_x/pallas_call | solution.py:133
  11.9 1.5 %collective-permute-done.3.rest_1_ = f32[3,8,512]{2,1,0:T(8,128)S(1)} collective-permute-done((f32[3,8,512]{2,1,0:T(8,128)S(1)}, f32[3,8,512]{2,1,0:T(8,128)S(1)}, u32[]{:S(2)}, u32[]{:S(2)}) %collective-permute-start.3) | collective-permute-done | bytes 49184 | tf_op jit(solution)/shard_map/ppermute | solution.py:367
  18.6 1.5 %collective-permute-start.12 = (f32[3,16,512]{2,1,0:T(8,128)S(1)}, f32[3,16,512]{2,1,0:T(8,128)S(1)}, u32[]{:S(2)}, u32[]{:S(2)}) collective-permute-start(f32[3,16,512]{2,1,0:T(8,128)S(1)} %get-tuple-element.125), channel_id=1, source_target_pairs={{0,7},{1,6},{2,1},{3,0},{4,3},{5,2},{6,5},{7,4},{8,15},{9,14},{10,... | collective-permute-start | bytes 294920 | tf_op jit(solution)/shard_map/ppermute | solution.py:367
  21.0 1.4 %along_x.8 = (f32[384,512]{1,0:T(8,128)S(1)}, f32[384,512]{1,0:T(8,128)S(1)}) custom-call(f32[384,512]{1,0:T(8,128)S(1)} %bitcast.37, f32[384,512]{1,0:T(8,128)S(1)} %bitcast.36, bf16[4,512,512]{2,1,0:T(8,128)(2,1)S(1)} %copy-done), custom_call_target="tpu_custom_call" | custom-call | flops 10000000000 | bytes 1048576 | tf_op jit(solution)/shard_map/along_x/pallas_call | solution.py:133
  22.4 2.0 %collective-permute-done.11.rest_1_ = f32[3,8,512]{2,1,0:T(8,128)S(1)} collective-permute-done((f32[3,8,512]{2,1,0:T(8,128)S(1)}, f32[3,8,512]{2,1,0:T(8,128)S(1)}, u32[]{:S(2)}, u32[]{:S(2)}) %collective-permute-start.11) | collective-permute-done | bytes 49184 | tf_op jit(solution)/shard_map/ppermute | solution.py:367
  27.9 1.9 %collective-permute-start.18 = (f32[3,16,512]{2,1,0:T(8,128)S(1)}, f32[3,16,512]{2,1,0:T(8,128)S(1)}, u32[]{:S(2)}, u32[]{:S(2)}) collective-permute-start(f32[3,16,512]{2,1,0:T(8,128)S(1)} %get-tuple-element.124), channel_id=1, source_target_pairs={{0,3},{1,2},{2,5},{3,4},{4,7},{5,6},{6,1},{7,0},{8,11},{9,10},{10,... | collective-permute-start | bytes 294920 | tf_op jit(solution)/shard_map/ppermute | solution.py:367
  31.6 2.3 %along_x.9 = (f32[384,512]{1,0:T(8,128)S(1)}, f32[384,512]{1,0:T(8,128)}) custom-call(f32[384,512]{1,0:T(8,128)S(1)} %bitcast.40, f32[384,512]{1,0:T(8,128)S(1)} %bitcast.49, bf16[4,512,512]{2,1,0:T(8,128)(2,1)S(1)} %copy-done), custom_call_target="tpu_custom_call" | custom-call | flops 10000000000 | bytes 1048576 | tf_op jit(solution)/shard_map/along_x/pallas_call | solution.py:133
  33.9 1.4 %collective-permute-done.19.rest_1_ = f32[3,8,512]{2,1,0:T(8,128)S(1)} collective-permute-done((f32[3,8,512]{2,1,0:T(8,128)S(1)}, f32[3,8,512]{2,1,0:T(8,128)S(1)}, u32[]{:S(2)}, u32[]{:S(2)}) %collective-permute-start.19) | collective-permute-done | bytes 49184 | tf_op jit(solution)/shard_map/ppermute | solution.py:367
  36.2 4.7 %collective-permute-done.refs_1_ = f32[3,128,1024]{2,1,0:T(8,128)S(1)} collective-permute-done((f32[3,128,1024]{2,1,0:T(8,128)}, f32[3,128,1024]{2,1,0:T(8,128)S(1)}, u32[]{:S(2)}, u32[]{:S(2)}) %collective-permute-start) | collective-permute-done | bytes 1572896 | tf_op jit(solution)/shard_map/ppermute | solution.py:350
  42.6 4.3 %collective-permute-start.46 = (f32[3,128,512]{2,1,0:T(8,128)S(1)}, f32[3,128,512]{2,1,0:T(8,128)S(1)}, u32[]{:S(2)}, u32[]{:S(2)}) collective-permute-start(f32[3,128,512]{2,1,0:T(8,128)S(1)} %stage_lead.1), channel_id=1, source_target_pairs={{0,16},{8,24},{1,17},{9,25},{2,18},{10,26},{3,19},{11,27},{4,20},{... | collective-permute-start | bytes 2359304 | tf_op jit(solution)/shard_map/ppermute | solution.py:350
  47.3 1.4 %collective-permute-start.23 = (f32[3,16,512]{2,1,0:T(8,128)S(1)}, f32[3,16,512]{2,1,0:T(8,128)S(1)}, u32[]{:S(2)}, u32[]{:S(2)}) collective-permute-start(f32[3,16,512]{2,1,0:T(8,128)S(1)} %get-tuple-element.122), channel_id=1, source_target_pairs={{0,3},{1,2},{2,5},{3,4},{4,7},{5,6},{6,1},{7,0},{8,11},{9,10},{10,... | collective-permute-start | bytes 294920 | tf_op jit(solution)/shard_map/ppermute | solution.py:367
  48.6 1.3 %collective-permute-start.27 = (f32[3,16,512]{2,1,0:T(8,128)S(1)}, f32[3,16,512]{2,1,0:T(8,128)S(1)}, u32[]{:S(2)}, u32[]{:S(2)}) collective-permute-start(f32[3,16,512]{2,1,0:T(8,128)S(1)} %get-tuple-element.121), channel_id=1, source_target_pairs={{0,7},{1,6},{2,1},{3,0},{4,3},{5,2},{6,5},{7,4},{8,15},{9,14},{10,... | collective-permute-start | bytes 294920 | tf_op jit(solution)/shard_map/ppermute | solution.py:367
  50.0 1.3 %collective-permute-start.25 = (f32[3,8,512]{2,1,0:T(8,128)S(1)}, f32[3,8,512]{2,1,0:T(8,128)S(1)}, u32[]{:S(2)}, u32[]{:S(2)}) collective-permute-start(f32[3,8,512]{2,1,0:T(8,128)S(1)} %slice.182), channel_id=1, source_target_pairs={{0,5},{1,4},{2,7},{3,6},{4,1},{5,0},{6,3},{7,2},{8,13},{9,12},{10,... | collective-permute-start | bytes 147464 | tf_op jit(solution)/shard_map/ppermute | solution.py:367
  51.3 1.4 %along_x.10 = (f32[384,512]{1,0:T(8,128)S(1)}, f32[384,512]{1,0:T(8,128)S(1)}) custom-call(f32[384,512]{1,0:T(8,128)S(1)} %bitcast.42, f32[384,512]{1,0:T(8,128)S(1)} %bitcast.33, bf16[4,512,512]{2,1,0:T(8,128)(2,1)S(1)} %copy-done), custom_call_target="tpu_custom_call" | custom-call | flops 10000000000 | bytes 1048576 | tf_op jit(solution)/shard_map/along_x/pallas_call | solution.py:133
  52.7 1.5 %collective-permute-done.25.rest_1_ = f32[3,8,512]{2,1,0:T(8,128)S(1)} collective-permute-done((f32[3,8,512]{2,1,0:T(8,128)S(1)}, f32[3,8,512]{2,1,0:T(8,128)S(1)}, u32[]{:S(2)}, u32[]{:S(2)}) %collective-permute-start.25) | collective-permute-done | bytes 49184 | tf_op jit(solution)/shard_map/ppermute | solution.py:367
  58.0 1.4 %collective-permute-start.31 = (f32[3,16,512]{2,1,0:T(8,128)S(1)}, f32[3,16,512]{2,1,0:T(8,128)S(1)}, u32[]{:S(2)}, u32[]{:S(2)}) collective-permute-start(f32[3,16,512]{2,1,0:T(8,128)S(1)} %get-tuple-element.120), channel_id=1, source_target_pairs={{0,3},{1,2},{2,5},{3,4},{4,7},{5,6},{6,1},{7,0},{8,11},{9,10},{10,... | collective-permute-start | bytes 294920 | tf_op jit(solution)/shard_map/ppermute | solution.py:367
  61.6 1.4 %along_x.11 = (f32[384,512]{1,0:T(8,128)S(1)}, f32[384,512]{1,0:T(8,128)S(1)}) custom-call(f32[384,512]{1,0:T(8,128)S(1)} %bitcast.30, f32[384,512]{1,0:T(8,128)S(1)} %bitcast.31, bf16[4,512,512]{2,1,0:T(8,128)(2,1)S(1)} %copy-done), custom_call_target="tpu_custom_call" | custom-call | flops 10000000000 | bytes 1048576 | tf_op jit(solution)/shard_map/along_x/pallas_call | solution.py:133
  63.0 2.0 %collective-permute-done.33.rest_1_ = f32[3,8,512]{2,1,0:T(8,128)S(1)} collective-permute-done((f32[3,8,512]{2,1,0:T(8,128)S(1)}, f32[3,8,512]{2,1,0:T(8,128)S(1)}, u32[]{:S(2)}, u32[]{:S(2)}) %collective-permute-start.33) | collective-permute-done | bytes 49184 | tf_op jit(solution)/shard_map/ppermute | solution.py:367
  68.5 1.9 %collective-permute-start.39 = (f32[3,16,512]{2,1,0:T(8,128)S(1)}, f32[3,16,512]{2,1,0:T(8,128)S(1)}, u32[]{:S(2)}, u32[]{:S(2)}) collective-permute-start(f32[3,16,512]{2,1,0:T(8,128)S(1)} %get-tuple-element.118), channel_id=1, source_target_pairs={{0,3},{1,2},{2,5},{3,4},{4,7},{5,6},{6,1},{7,0},{8,11},{9,10},{10,... | collective-permute-start | bytes 294920 | tf_op jit(solution)/shard_map/ppermute | solution.py:367
  72.1 1.4 %along_x.12 = (f32[384,512]{1,0:T(8,128)S(1)}, f32[384,512]{1,0:T(8,128)S(1)}) custom-call(f32[384,512]{1,0:T(8,128)S(1)} %bitcast.35, f32[384,512]{1,0:T(8,128)S(1)} %bitcast.34, bf16[4,512,512]{2,1,0:T(8,128)(2,1)S(1)} %copy-done), custom_call_target="tpu_custom_call" | custom-call | flops 10000000000 | bytes 1048576 | tf_op jit(solution)/shard_map/along_x/pallas_call | solution.py:133
  73.5 2.3 %collective-permute-done.41.rest_1_ = f32[3,8,512]{2,1,0:T(8,128)S(1)} collective-permute-done((f32[3,8,512]{2,1,0:T(8,128)S(1)}, f32[3,8,512]{2,1,0:T(8,128)S(1)}, u32[]{:S(2)}, u32[]{:S(2)}) %collective-permute-start.41) | collective-permute-done | bytes 49184 | tf_op jit(solution)/shard_map/ppermute | solution.py:367
  78.5 1.9 %collective-permute-start.45 = (f32[3,128,512]{2,1,0:T(8,128)S(1)}, f32[3,128,512]{2,1,0:T(8,128)S(1)}, u32[]{:S(2)}, u32[]{:S(2)}) collective-permute-start(f32[3,128,512]{2,1,0:T(8,128)S(1)} %get-tuple-element.100), channel_id=1, source_target_pairs={{0,8},{8,16},{16,24},{1,9},{9,17},{17,25},{2,10},{10,18},{18,26},{... | collective-permute-start | bytes 2359304 | tf_op jit(solution)/shard_map/ppermute | solution.py:350
  81.7 17.5 %collective-permute-done.45.refs_0_ = f32[3,128,512]{2,1,0:T(8,128)S(1)} collective-permute-done((f32[3,128,512]{2,1,0:T(8,128)S(1)}, f32[3,128,512]{2,1,0:T(8,128)S(1)}, u32[]{:S(2)}, u32[]{:S(2)}) %collective-permute-start.45) | collective-permute-done | bytes 786464 | tf_op jit(solution)/shard_map/ppermute | solution.py:350
  99.7 2.9 %collective-permute-start.49 = (f32[3,16,512]{2,1,0:T(8,128)S(1)}, f32[3,16,512]{2,1,0:T(8,128)S(1)}, u32[]{:S(2)}, u32[]{:S(2)}) collective-permute-start(f32[3,16,512]{2,1,0:T(8,128)S(1)} %get-tuple-element.116), channel_id=1, source_target_pairs={{0,3},{1,2},{2,5},{3,4},{4,7},{5,6},{6,1},{7,0},{8,11},{9,10},{10,... | collective-permute-start | bytes 294920 | tf_op jit(solution)/shard_map/ppermute | solution.py:367
  102.6 1.5 %collective-permute-start.53 = (f32[3,16,512]{2,1,0:T(8,128)S(1)}, f32[3,16,512]{2,1,0:T(8,128)S(1)}, u32[]{:S(2)}, u32[]{:S(2)}) collective-permute-start(f32[3,16,512]{2,1,0:T(8,128)S(1)} %get-tuple-element.115), channel_id=1, source_target_pairs={{0,7},{1,6},{2,1},{3,0},{4,3},{5,2},{6,5},{7,4},{8,15},{9,14},{10,... | collective-permute-start | bytes 294920 | tf_op jit(solution)/shard_map/ppermute | solution.py:367
  104.5 1.4 %along_x.13 = (f32[384,512]{1,0:T(8,128)S(1)}, f32[384,512]{1,0:T(8,128)S(1)}) custom-call(f32[384,512]{1,0:T(8,128)S(1)} %bitcast.39, f32[384,512]{1,0:T(8,128)S(1)} %bitcast.38, bf16[4,512,512]{2,1,0:T(8,128)(2,1)S(1)} %copy-done), custom_call_target="tpu_custom_call" | custom-call | flops 10000000000 | bytes 1048576 | tf_op jit(solution)/shard_map/along_x/pallas_call | solution.py:133
  105.9 1.8 %collective-permute-done.51.rest_1_ = f32[3,8,512]{2,1,0:T(8,128)S(1)} collective-permute-done((f32[3,8,512]{2,1,0:T(8,128)S(1)}, f32[3,8,512]{2,1,0:T(8,128)S(1)}, u32[]{:S(2)}, u32[]{:S(2)}) %collective-permute-start.51) | collective-permute-done | bytes 49184 | tf_op jit(solution)/shard_map/ppermute | solution.py:367
  109.5 1.5 %stage_join.1 = f32[3,128,1024]{2,1,0:T(8,128)} custom-call(f32[3,128,512]{2,1,0:T(8,128)S(1)} %get-tuple-element.102.state_ref, f32[3,128,512]{2,1,0:T(8,128)S(1)} %bitcast.48, f32[128,1]{1,0:T(8,128)S(1)} %get-tuple-element.63.turning_ref, f32[3,16,512]{2,1,0:T(8,128)S(1)} %collective-permute-done.50.rest_0_, ...), custom_call_target="tpu_custom_call" | custom-call | flops 10000000000 | bytes 1048576 | tf_op jit(solution)/shard_map/stage_join/pallas_call | solution.py:133
  (134 shorter events, 34.4 us)
Async XLA Ops:
  2.0 4.3 %collective-permute-start.1 = (f32[3,56,512]{2,1,0:T(8,128)S(1)}, f32[3,56,512]{2,1,0:T(8,128)S(1)}, u32[]{:S(2)}, u32[]{:S(2)}) collective-permute-start(f32[3,56,512]{2,1,0:T(8,128)S(1)} %get-tuple-element.65), channel_id=1, source_target_pairs={{0,1},{1,0},{2,3},{3,2},{4,5},{5,4},{6,7},{7,6},{8,9},{9,8},{10,11... | collective-permute-start | bytes 1032200 | tf_op jit(solution)/shard_map/ppermute | solution.py:355
  2.8 38.1 %collective-permute-start = (f32[3,128,1024]{2,1,0:T(8,128)}, f32[3,128,1024]{2,1,0:T(8,128)S(1)}, u32[]{:S(2)}, u32[]{:S(2)}) collective-permute-start(f32[3,128,1024]{2,1,0:T(8,128)} %bitcast.refs_0_), channel_id=1, source_target_pairs={{0,8},{8,16},{16,24},{1,9},{9,17},{17,25},{2,10},{10,18},{18,26},{... | collective-permute-start | bytes 4718600 | tf_op jit(solution)/shard_map/ppermute | solution.py:350
  6.0 8.5 %collective-permute-start.5 = (f32[3,16,512]{2,1,0:T(8,128)S(1)}, f32[3,16,512]{2,1,0:T(8,128)S(1)}, u32[]{:S(2)}, u32[]{:S(2)}) collective-permute-start(f32[3,16,512]{2,1,0:T(8,128)S(1)} %slice.131), channel_id=1, source_target_pairs={{0,1},{1,0},{2,3},{3,2},{4,5},{5,4},{6,7},{7,6},{8,9},{9,8},{10,11... | collective-permute-start | bytes 294920 | tf_op jit(solution)/shard_map/ppermute | solution.py:355
  6.5 7.1 %collective-permute-start.2 = (f32[3,16,512]{2,1,0:T(8,128)S(1)}, f32[3,16,512]{2,1,0:T(8,128)S(1)}, u32[]{:S(2)}, u32[]{:S(2)}) collective-permute-start(f32[3,16,512]{2,1,0:T(8,128)S(1)} %get-tuple-element.128), channel_id=1, source_target_pairs={{0,3},{1,2},{2,5},{3,4},{4,7},{5,6},{6,1},{7,0},{8,11},{9,10},{10,... | collective-permute-start | bytes 294920 | tf_op jit(solution)/shard_map/ppermute | solution.py:367
  7.8 6.7 %collective-permute-start.4 = (f32[3,16,512]{2,1,0:T(8,128)S(1)}, f32[3,16,512]{2,1,0:T(8,128)S(1)}, u32[]{:S(2)}, u32[]{:S(2)}) collective-permute-start(f32[3,16,512]{2,1,0:T(8,128)S(1)} %get-tuple-element.127), channel_id=1, source_target_pairs={{0,7},{1,6},{2,1},{3,0},{4,3},{5,2},{6,5},{7,4},{8,15},{9,14},{10,... | collective-permute-start | bytes 294920 | tf_op jit(solution)/shard_map/ppermute | solution.py:367
  9.2 4.2 %collective-permute-start.3 = (f32[3,8,512]{2,1,0:T(8,128)S(1)}, f32[3,8,512]{2,1,0:T(8,128)S(1)}, u32[]{:S(2)}, u32[]{:S(2)}) collective-permute-start(f32[3,8,512]{2,1,0:T(8,128)S(1)} %slice.170), channel_id=1, source_target_pairs={{0,5},{1,4},{2,7},{3,6},{4,1},{5,0},{6,3},{7,2},{8,13},{9,12},{10,... | collective-permute-start | bytes 147464 | tf_op jit(solution)/shard_map/ppermute | solution.py:367
  16.9 8.2 %collective-permute-start.13 = (f32[3,16,512]{2,1,0:T(8,128)S(1)}, f32[3,16,512]{2,1,0:T(8,128)S(1)}, u32[]{:S(2)}, u32[]{:S(2)}) collective-permute-start(f32[3,16,512]{2,1,0:T(8,128)S(1)} %slice.137), channel_id=1, source_target_pairs={{0,1},{1,0},{2,3},{3,2},{4,5},{5,4},{6,7},{7,6},{8,9},{9,8},{10,11... | collective-permute-start | bytes 294920 | tf_op jit(solution)/shard_map/ppermute | solution.py:355
  17.3 7.3 %collective-permute-start.10 = (f32[3,16,512]{2,1,0:T(8,128)S(1)}, f32[3,16,512]{2,1,0:T(8,128)S(1)}, u32[]{:S(2)}, u32[]{:S(2)}) collective-permute-start(f32[3,16,512]{2,1,0:T(8,128)S(1)} %get-tuple-element.126), channel_id=1, source_target_pairs={{0,3},{1,2},{2,5},{3,4},{4,7},{5,6},{6,1},{7,0},{8,11},{9,10},{10,... | collective-permute-start | bytes 294920 | tf_op jit(solution)/shard_map/ppermute | solution.py:367
  18.6 6.4 %collective-permute-start.12 = (f32[3,16,512]{2,1,0:T(8,128)S(1)}, f32[3,16,512]{2,1,0:T(8,128)S(1)}, u32[]{:S(2)}, u32[]{:S(2)}) collective-permute-start(f32[3,16,512]{2,1,0:T(8,128)S(1)} %get-tuple-element.125), channel_id=1, source_target_pairs={{0,7},{1,6},{2,1},{3,0},{4,3},{5,2},{6,5},{7,4},{8,15},{9,14},{10,... | collective-permute-start | bytes 294920 | tf_op jit(solution)/shard_map/ppermute | solution.py:367
  20.1 4.3 %collective-permute-start.11 = (f32[3,8,512]{2,1,0:T(8,128)S(1)}, f32[3,8,512]{2,1,0:T(8,128)S(1)}, u32[]{:S(2)}, u32[]{:S(2)}) collective-permute-start(f32[3,8,512]{2,1,0:T(8,128)S(1)} %slice.174), channel_id=1, source_target_pairs={{0,5},{1,4},{2,7},{3,6},{4,1},{5,0},{6,3},{7,2},{8,13},{9,12},{10,... | collective-permute-start | bytes 147464 | tf_op jit(solution)/shard_map/ppermute | solution.py:367
  27.4 6.5 %collective-permute-start.21 = (f32[3,16,512]{2,1,0:T(8,128)S(1)}, f32[3,16,512]{2,1,0:T(8,128)S(1)}, u32[]{:S(2)}, u32[]{:S(2)}) collective-permute-start(f32[3,16,512]{2,1,0:T(8,128)S(1)} %slice.143), channel_id=1, source_target_pairs={{0,1},{1,0},{2,3},{3,2},{4,5},{5,4},{6,7},{7,6},{8,9},{9,8},{10,11... | collective-permute-start | bytes 294920 | tf_op jit(solution)/shard_map/ppermute | solution.py:355
  27.9 7.4 %collective-permute-start.18 = (f32[3,16,512]{2,1,0:T(8,128)S(1)}, f32[3,16,512]{2,1,0:T(8,128)S(1)}, u32[]{:S(2)}, u32[]{:S(2)}) collective-permute-start(f32[3,16,512]{2,1,0:T(8,128)S(1)} %get-tuple-element.124), channel_id=1, source_target_pairs={{0,3},{1,2},{2,5},{3,4},{4,7},{5,6},{6,1},{7,0},{8,11},{9,10},{10,... | collective-permute-start | bytes 294920 | tf_op jit(solution)/shard_map/ppermute | solution.py:367
  29.8 5.7 %collective-permute-start.20 = (f32[3,16,512]{2,1,0:T(8,128)S(1)}, f32[3,16,512]{2,1,0:T(8,128)S(1)}, u32[]{:S(2)}, u32[]{:S(2)}) collective-permute-start(f32[3,16,512]{2,1,0:T(8,128)S(1)} %get-tuple-element.123), channel_id=1, source_target_pairs={{0,7},{1,6},{2,1},{3,0},{4,3},{5,2},{6,5},{7,4},{8,15},{9,14},{10,... | collective-permute-start | bytes 294920 | tf_op jit(solution)/shard_map/ppermute | solution.py:367
  41.7 5.5 %collective-permute-start.22 = (f32[3,56,512]{2,1,0:T(8,128)S(1)}, f32[3,56,512]{2,1,0:T(8,128)S(1)}, u32[]{:S(2)}, u32[]{:S(2)}) collective-permute-start(f32[3,56,512]{2,1,0:T(8,128)S(1)} %get-tuple-element.85), channel_id=1, source_target_pairs={{0,1},{1,0},{2,3},{3,2},{4,5},{5,4},{6,7},{7,6},{8,9},{9,8},{10,11... | collective-permute-start | bytes 1032200 | tf_op jit(solution)/shard_map/ppermute | solution.py:355
  42.6 38.2 %collective-permute-start.46 = (f32[3,128,512]{2,1,0:T(8,128)S(1)}, f32[3,128,512]{2,1,0:T(8,128)S(1)}, u32[]{:S(2)}, u32[]{:S(2)}) collective-permute-start(f32[3,128,512]{2,1,0:T(8,128)S(1)} %stage_lead.1), channel_id=1, source_target_pairs={{0,16},{8,24},{1,17},{9,25},{2,18},{10,26},{3,19},{11,27},{4,20},{... | collective-permute-start | bytes 2359304 | tf_op jit(solution)/shard_map/ppermute | solution.py:350
  46.8 8.5 %collective-permute-start.29 = (f32[3,16,512]{2,1,0:T(8,128)S(1)}, f32[3,16,512]{2,1,0:T(8,128)S(1)}, u32[]{:S(2)}, u32[]{:S(2)}) collective-permute-start(f32[3,16,512]{2,1,0:T(8,128)S(1)} %slice.149), channel_id=1, source_target_pairs={{0,1},{1,0},{2,3},{3,2},{4,5},{5,4},{6,7},{7,6},{8,9},{9,8},{10,11... | collective-permute-start | bytes 294920 | tf_op jit(solution)/shard_map/ppermute | solution.py:355
  47.3 7.1 %collective-permute-start.23 = (f32[3,16,512]{2,1,0:T(8,128)S(1)}, f32[3,16,512]{2,1,0:T(8,128)S(1)}, u32[]{:S(2)}, u32[]{:S(2)}) collective-permute-start(f32[3,16,512]{2,1,0:T(8,128)S(1)} %get-tuple-element.122), channel_id=1, source_target_pairs={{0,3},{1,2},{2,5},{3,4},{4,7},{5,6},{6,1},{7,0},{8,11},{9,10},{10,... | collective-permute-start | bytes 294920 | tf_op jit(solution)/shard_map/ppermute | solution.py:367
  48.6 6.4 %collective-permute-start.27 = (f32[3,16,512]{2,1,0:T(8,128)S(1)}, f32[3,16,512]{2,1,0:T(8,128)S(1)}, u32[]{:S(2)}, u32[]{:S(2)}) collective-permute-start(f32[3,16,512]{2,1,0:T(8,128)S(1)} %get-tuple-element.121), channel_id=1, source_target_pairs={{0,7},{1,6},{2,1},{3,0},{4,3},{5,2},{6,5},{7,4},{8,15},{9,14},{10,... | collective-permute-start | bytes 294920 | tf_op jit(solution)/shard_map/ppermute | solution.py:367
  50.0 4.2 %collective-permute-start.25 = (f32[3,8,512]{2,1,0:T(8,128)S(1)}, f32[3,8,512]{2,1,0:T(8,128)S(1)}, u32[]{:S(2)}, u32[]{:S(2)}) collective-permute-start(f32[3,8,512]{2,1,0:T(8,128)S(1)} %slice.182), channel_id=1, source_target_pairs={{0,5},{1,4},{2,7},{3,6},{4,1},{5,0},{6,3},{7,2},{8,13},{9,12},{10,... | collective-permute-start | bytes 147464 | tf_op jit(solution)/shard_map/ppermute | solution.py:367
  57.5 8.3 %collective-permute-start.37 = (f32[3,16,512]{2,1,0:T(8,128)S(1)}, f32[3,16,512]{2,1,0:T(8,128)S(1)}, u32[]{:S(2)}, u32[]{:S(2)}) collective-permute-start(f32[3,16,512]{2,1,0:T(8,128)S(1)} %slice.155), channel_id=1, source_target_pairs={{0,1},{1,0},{2,3},{3,2},{4,5},{5,4},{6,7},{7,6},{8,9},{9,8},{10,11... | collective-permute-start | bytes 294920 | tf_op jit(solution)/shard_map/ppermute | solution.py:355
  58.0 7.2 %collective-permute-start.31 = (f32[3,16,512]{2,1,0:T(8,128)S(1)}, f32[3,16,512]{2,1,0:T(8,128)S(1)}, u32[]{:S(2)}, u32[]{:S(2)}) collective-permute-start(f32[3,16,512]{2,1,0:T(8,128)S(1)} %get-tuple-element.120), channel_id=1, source_target_pairs={{0,3},{1,2},{2,5},{3,4},{4,7},{5,6},{6,1},{7,0},{8,11},{9,10},{10,... | collective-permute-start | bytes 294920 | tf_op jit(solution)/shard_map/ppermute | solution.py:367
  59.4 6.1 %collective-permute-start.35 = (f32[3,16,512]{2,1,0:T(8,128)S(1)}, f32[3,16,512]{2,1,0:T(8,128)S(1)}, u32[]{:S(2)}, u32[]{:S(2)}) collective-permute-start(f32[3,16,512]{2,1,0:T(8,128)S(1)} %get-tuple-element.119), channel_id=1, source_target_pairs={{0,7},{1,6},{2,1},{3,0},{4,3},{5,2},{6,5},{7,4},{8,15},{9,14},{10,... | collective-permute-start | bytes 294920 | tf_op jit(solution)/shard_map/ppermute | solution.py:367
  60.7 4.3 %collective-permute-start.33 = (f32[3,8,512]{2,1,0:T(8,128)S(1)}, f32[3,8,512]{2,1,0:T(8,128)S(1)}, u32[]{:S(2)}, u32[]{:S(2)}) collective-permute-start(f32[3,8,512]{2,1,0:T(8,128)S(1)} %slice.186), channel_id=1, source_target_pairs={{0,5},{1,4},{2,7},{3,6},{4,1},{5,0},{6,3},{7,2},{8,13},{9,12},{10,... | collective-permute-start | bytes 147464 | tf_op jit(solution)/shard_map/ppermute | solution.py:367
  68.0 8.6 %collective-permute-start.47 = (f32[3,16,512]{2,1,0:T(8,128)S(1)}, f32[3,16,512]{2,1,0:T(8,128)S(1)}, u32[]{:S(2)}, u32[]{:S(2)}) collective-permute-start(f32[3,16,512]{2,1,0:T(8,128)S(1)} %slice.161), channel_id=1, source_target_pairs={{0,1},{1,0},{2,3},{3,2},{4,5},{5,4},{6,7},{7,6},{8,9},{9,8},{10,11... | collective-permute-start | bytes 294920 | tf_op jit(solution)/shard_map/ppermute | solution.py:355
  68.5 7.6 %collective-permute-start.39 = (f32[3,16,512]{2,1,0:T(8,128)S(1)}, f32[3,16,512]{2,1,0:T(8,128)S(1)}, u32[]{:S(2)}, u32[]{:S(2)}) collective-permute-start(f32[3,16,512]{2,1,0:T(8,128)S(1)} %get-tuple-element.118), channel_id=1, source_target_pairs={{0,3},{1,2},{2,5},{3,4},{4,7},{5,6},{6,1},{7,0},{8,11},{9,10},{10,... | collective-permute-start | bytes 294920 | tf_op jit(solution)/shard_map/ppermute | solution.py:367
  70.4 5.9 %collective-permute-start.43 = (f32[3,16,512]{2,1,0:T(8,128)S(1)}, f32[3,16,512]{2,1,0:T(8,128)S(1)}, u32[]{:S(2)}, u32[]{:S(2)}) collective-permute-start(f32[3,16,512]{2,1,0:T(8,128)S(1)} %get-tuple-element.117), channel_id=1, source_target_pairs={{0,7},{1,6},{2,1},{3,0},{4,3},{5,2},{6,5},{7,4},{8,15},{9,14},{10,... | collective-permute-start | bytes 294920 | tf_op jit(solution)/shard_map/ppermute | solution.py:367
  71.6 4.2 %collective-permute-start.41 = (f32[3,8,512]{2,1,0:T(8,128)S(1)}, f32[3,8,512]{2,1,0:T(8,128)S(1)}, u32[]{:S(2)}, u32[]{:S(2)}) collective-permute-start(f32[3,8,512]{2,1,0:T(8,128)S(1)} %slice.190), channel_id=1, source_target_pairs={{0,5},{1,4},{2,7},{3,6},{4,1},{5,0},{6,3},{7,2},{8,13},{9,12},{10,... | collective-permute-start | bytes 147464 | tf_op jit(solution)/shard_map/ppermute | solution.py:367
  78.5 20.7 %collective-permute-start.45 = (f32[3,128,512]{2,1,0:T(8,128)S(1)}, f32[3,128,512]{2,1,0:T(8,128)S(1)}, u32[]{:S(2)}, u32[]{:S(2)}) collective-permute-start(f32[3,128,512]{2,1,0:T(8,128)S(1)} %get-tuple-element.100), channel_id=1, source_target_pairs={{0,8},{8,16},{16,24},{1,9},{9,17},{17,25},{2,10},{10,18},{18,26},{... | collective-permute-start | bytes 2359304 | tf_op jit(solution)/shard_map/ppermute | solution.py:350
  81.2 18.4 %collective-permute-start.48 = (f32[3,56,512]{2,1,0:T(8,128)S(1)}, f32[3,56,512]{2,1,0:T(8,128)S(1)}, u32[]{:S(2)}, u32[]{:S(2)}) collective-permute-start(f32[3,56,512]{2,1,0:T(8,128)S(1)} %get-tuple-element.111), channel_id=1, source_target_pairs={{0,1},{1,0},{2,3},{3,2},{4,5},{5,4},{6,7},{7,6},{8,9},{9,8},{10,11... | collective-permute-start | bytes 1032200 | tf_op jit(solution)/shard_map/ppermute | solution.py:355
  99.7 8.0 %collective-permute-start.49 = (f32[3,16,512]{2,1,0:T(8,128)S(1)}, f32[3,16,512]{2,1,0:T(8,128)S(1)}, u32[]{:S(2)}, u32[]{:S(2)}) collective-permute-start(f32[3,16,512]{2,1,0:T(8,128)S(1)} %get-tuple-element.116), channel_id=1, source_target_pairs={{0,3},{1,2},{2,5},{3,4},{4,7},{5,6},{6,1},{7,0},{8,11},{9,10},{10,... | collective-permute-start | bytes 294920 | tf_op jit(solution)/shard_map/ppermute | solution.py:367
  102.6 5.6 %collective-permute-start.53 = (f32[3,16,512]{2,1,0:T(8,128)S(1)}, f32[3,16,512]{2,1,0:T(8,128)S(1)}, u32[]{:S(2)}, u32[]{:S(2)}) collective-permute-start(f32[3,16,512]{2,1,0:T(8,128)S(1)} %get-tuple-element.115), channel_id=1, source_target_pairs={{0,7},{1,6},{2,1},{3,0},{4,3},{5,2},{6,5},{7,4},{8,15},{9,14},{10,... | collective-permute-start | bytes 294920 | tf_op jit(solution)/shard_map/ppermute | solution.py:367
  104.1 4.2 %collective-permute-start.55 = (f32[3,16,512]{2,1,0:T(8,128)S(1)}, f32[3,16,512]{2,1,0:T(8,128)S(1)}, u32[]{:S(2)}, u32[]{:S(2)}) collective-permute-start(f32[3,16,512]{2,1,0:T(8,128)S(1)} %slice.167), channel_id=1, source_target_pairs={{0,1},{1,0},{2,3},{3,2},{4,5},{5,4},{6,7},{7,6},{8,9},{9,8},{10,11... | collective-permute-start | bytes 294920 | tf_op jit(solution)/shard_map/ppermute | solution.py:355
  (25 other events, 56.9 us)

commit v6 on v5

--- a/solution.py
+++ b/solution.py
@@ -202,27 +202,27 @@
     return rate_h, rate_u, rate_v
 
 
-def enter_call(plan, state, received=None, tables=None, send=None):
+def enter_call(plan, state, received=None, tables=None, send=None, halves=(0, 1)):
     sources = [state] if received is None else [state, received]
-    opening = tables is not None
+    opening, count = tables is not None, len(halves)
     held_in = pltpu.HBM if opening else pltpu.VMEM
     more = [pltpu.with_memory_space_constraint(a, held_in) for a in (tables if opening else [send])]
 
     def body(*refs):
         source_refs, refs = refs[: len(sources)], refs[len(sources) :]
         more_refs, outs = refs[: len(more)], refs[len(more) :]
-        nexts, moments, arrived = outs[0:4:2], outs[1:4:2], outs[-1]
+        nexts, moments, arrived = outs[0 : 2 * count : 2], outs[1 : 2 * count : 2], outs[-1]
 
         def copy(source_ref, at):
-            return pltpu.make_async_copy(source_ref.at[:, :, plan.columns(at == 1)], nexts[at], arrived.at[at])
+            return pltpu.make_async_copy(source_ref.at[:, :, plan.columns(halves[at] == 1)], nexts[at], arrived.at[at])
 
         def start(source_ref):
-            for at in range(2):
+            for at in range(count):
                 copy(source_ref, at).start()
 
         if opening:
             picks = [
-                pltpu.make_async_copy(more_refs[n].at[member_of_pair()], outs[4 + n], arrived.at[2 + n]) for n in range(2)
+                pltpu.make_async_copy(more_refs[n].at[member_of_pair()], outs[2 * count + n], arrived.at[2 + n]) for n in range(2)
             ]
             picks.append(pltpu.make_async_copy(more_refs[2], outs[-2], arrived.at[4]))
             for pick in picks:
@@ -232,17 +232,19 @@
                 pick.wait()
             square = (plan.rows, plan.rows)
             here = lax.broadcasted_iota(jnp.int32, square, 0) == lax.broadcasted_iota(jnp.int32, square, 1)
-            outs[6][...] = jnp.sum(jnp.where(here, outs[-2][...], 0.0), axis=1, keepdims=True)
+            outs[2 * count + 2][...] = jnp.sum(jnp.where(here, outs[-2][...], 0.0), axis=1, keepdims=True)
+        elif received is None:
+            start(source_refs[0])
         else:
             first = lax.axis_index("tm") == 0
             pl.when(first)(lambda: start(source_refs[0]))
             pl.when(jnp.logical_not(first))(lambda: start(source_refs[1]))
-        send_ref = outs[4] if opening else more_refs[0]
-        for at in range(2):
+        send_ref = outs[2 * count] if opening else more_refs[0]
+        for at in range(count):
             copy(source_refs[0], at).wait()
             plan.emit_moments(nexts[at], send_ref, moments[at])
 
-    shapes = [plan.state, *plan.moments] * 2
+    shapes = [plan.state, *plan.moments] * count
     scratch = [pltpu.SemaphoreType.DMA((5,))]
     if opening:
         shapes += [jax.ShapeDtypeStruct(a.shape[1:], a.dtype) for a in tables[:2]]
@@ -388,8 +390,10 @@
 
     before = ahead_in_time(own, 1)
     both_send, both_apply = jnp.asarray(send_tables), jnp.asarray(apply_tables)
-    opened = enter_call(plan, own, tables=(both_send, both_apply, coriolis[None, :]))
-    states, moments, (send, apply, turning) = opened[0:4:2], list(opened[1:4:2]), opened[4:]
+    opened = enter_call(plan, own, tables=(both_send, both_apply, coriolis[None, :]), halves=(0,))
+    send, apply, turning = opened[2:]
+    opened_mine = enter_call(plan, own, send=send, halves=(1,))
+    states, moments = [opened[0], opened_mine[0]], [opened[1], opened_mine[1]]
     states, moments = stage(("move", "move"), states, moments, sends=True)
     states, moments = stage(("move", "move"), states, moments, sends=True)
     (lead,) = stage(("lead",), states, moments, groups=(FAR,))

time: 112 us -> 110 us (0.982)
  waiting for transfers between devices: 37.6 us -> 33.4 us
  local copies, waits for them, and re-layouts: 0.21 us -> 2.38 us
    ppermute x3, waiting for transfers between devices: 22.6 us -> 17.7 us  [ahead_in_time(): return lax.ppermute(array, 'tm', [(i, i + by) for i in range(size - by)])]
    unnamed x2 -> x6, local copies, waits for them, and re-layouts: 0.01 us -> 2.18 us
    pallas_call x2 -> x3, Pallas kernels: 2.83 us -> 2.6 us  [enter_call(): pl.pallas_call(body, in_specs=[HBM] * len(sources) + [HBM if opening else...]
  transfers between devices with their start and end apart: 56 -> 56, of which waited for: 20 -> 20; matrix products, arithmetic and copies ran while one was open for 0% -> 0% of each run, Pallas kernels for 20% -> 22%
where the time goes in v6:
time: 110 us; the launch traced here: 108 us
  starting transfers between devices  45.8 us (42%)
  waiting for transfers between devices  33.4 us (30%)
  Pallas kernels  25.9 us (24%)
  local copies, waits for them, and re-layouts  2.38 us (2%)
    ppermute x21, starting transfers between devices, exchange(): lax.ppermute(part, 'grid', [(i, (i + 2 * d) % size ^ 1) for i in range(si...  27.2 us
    pallas_call x22, Pallas kernels, on_chip_call(): pl.pallas_call(body, in_specs=[VMEM] * len(held), out_specs=[VMEM if keep...  23.3 us
    ppermute x3, waiting for transfers between devices, ahead_in_time(): return lax.ppermute(array, 'tm', [(i, i + by) for i in range(size - by)])  17.7 us
    ppermute x21, waiting for transfers between devices, exchange(): lax.ppermute(part, 'grid', [(i, (i + 2 * d) % size ^ 1) for i in range(si...  13.7 us
    ppermute x32, starting transfers between devices, mate_swap(): return lax.ppermute(array, 'grid', [(i, i ^ 1) for i in range(size)])  9.55 us
    ppermute x3, starting transfers between devices, ahead_in_time(): return lax.ppermute(array, 'tm', [(i, i + by) for i in range(size - by)])  9.15 us
    pallas_call x3, Pallas kernels, enter_call(): pl.pallas_call(body, in_specs=[HBM] * len(sources) + [HBM if opening else...  2.6 us
  transfers between devices with their start and end apart: 56, of which 20 were waited for; matrix products, arithmetic and copies ran while one was open for 0% of the time, Pallas kernels for 22%

profile of v6, /device:TPU:9, one launch (start us, length us, event | category | flops | bytes accessed | tf_op | source)
XLA Modules:
  0.0 108.5 jit_solution(6944140738747580659)
XLA Ops:
  0.0 3.2 %collective-permute-start = (f32[3,128,1024]{2,1,0:T(8,128)}, f32[3,128,1024]{2,1,0:T(8,128)S(1)}, u32[]{:S(2)}, u32[]{:S(2)}) collective-permute-start(f32[3,128,1024]{2,1,0:T(8,128)} %bitcast.30), channel_id=1, source_target_pairs={{0,8},{8,16},{16,24},{1,9},{9,17},{17,25},{2,10},{10,18},{18,26},{... | collective-permute-start | bytes 4718600 | tf_op jit(solution)/shard_map/ppermute | solution.py:352
  3.2 1.4 %copy-done = f32[1,3,128,1024]{3,2,1,0:T(8,128)S(1)} copy-done((f32[1,3,128,1024]{3,2,1,0:T(8,128)S(1)}, f32[1,3,128,1024]{3,2,1,0:T(8,128)}, u32[]{:S(2)}) %copy-start) | copy-done | bytes 1572888
  4.6 1.4 %enter.3 = (f32[3,128,512]{2,1,0:T(8,128)S(1)}, f32[3,56,512]{2,1,0:T(8,128)S(1)}, bf16[128,128]{1,0:T(8,128)(2,1)S(1)}, bf16[256,192]{1,0:T(8,128)(2,1)S(1)}, f32[128,1]{1,0:T(8,128)S(1)}) custom-call(f32[3,128,1024]{2,1,0:T(8,128)S(1)} %bitcast.31, bf16[2,128,128]{2,1,0:T(8,128)(2,1)} %constant.7.clone.refs_1_, ...), custom_call_target="tpu_custom_call" | custom-call | flops 10000000000 | bytes 1048576 | tf_op jit(solution)/shard_map/enter/pallas_call | solution.py:253
  8.4 1.5 %collective-permute-start.2 = (f32[3,16,512]{2,1,0:T(8,128)S(1)}, f32[3,16,512]{2,1,0:T(8,128)S(1)}, u32[]{:S(2)}, u32[]{:S(2)}) collective-permute-start(f32[3,16,512]{2,1,0:T(8,128)S(1)} %get-tuple-element.128), channel_id=1, source_target_pairs={{0,3},{1,2},{2,5},{3,4},{4,7},{5,6},{6,1},{7,0},{8,11},{9,10},{10,... | collective-permute-start | bytes 294920 | tf_op jit(solution)/shard_map/ppermute | solution.py:369
  11.1 1.5 %collective-permute-start.3 = (f32[3,8,512]{2,1,0:T(8,128)S(1)}, f32[3,8,512]{2,1,0:T(8,128)S(1)}, u32[]{:S(2)}, u32[]{:S(2)}) collective-permute-start(f32[3,8,512]{2,1,0:T(8,128)S(1)} %slice.170), channel_id=1, source_target_pairs={{0,5},{1,4},{2,7},{3,6},{4,1},{5,0},{6,3},{7,2},{8,13},{9,12},{10,... | collective-permute-start | bytes 147464 | tf_op jit(solution)/shard_map/ppermute | solution.py:369
  12.6 1.4 %along_x.7 = (f32[384,512]{1,0:T(8,128)S(1)}, f32[384,512]{1,0:T(8,128)S(1)}) custom-call(f32[384,512]{1,0:T(8,128)S(1)} %bitcast.45, f32[384,512]{1,0:T(8,128)S(1)} %bitcast.42, bf16[4,512,512]{2,1,0:T(8,128)(2,1)S(1)} %copy-done.2), custom_call_target="tpu_custom_call" | custom-call | flops 10000000000 | bytes 1048576 | tf_op jit(solution)/shard_map/along_x/pallas_call | solution.py:133
  14.0 1.5 %collective-permute-done.3.rest_1_ = f32[3,8,512]{2,1,0:T(8,128)S(1)} collective-permute-done((f32[3,8,512]{2,1,0:T(8,128)S(1)}, f32[3,8,512]{2,1,0:T(8,128)S(1)}, u32[]{:S(2)}, u32[]{:S(2)}) %collective-permute-start.3) | collective-permute-done | bytes 49184 | tf_op jit(solution)/shard_map/ppermute | solution.py:369
  20.7 1.6 %collective-permute-start.12 = (f32[3,16,512]{2,1,0:T(8,128)S(1)}, f32[3,16,512]{2,1,0:T(8,128)S(1)}, u32[]{:S(2)}, u32[]{:S(2)}) collective-permute-start(f32[3,16,512]{2,1,0:T(8,128)S(1)} %get-tuple-element.125), channel_id=1, source_target_pairs={{0,7},{1,6},{2,1},{3,0},{4,3},{5,2},{6,5},{7,4},{8,15},{9,14},{10,... | collective-permute-start | bytes 294920 | tf_op jit(solution)/shard_map/ppermute | solution.py:369
  23.0 1.4 %along_x.8 = (f32[384,512]{1,0:T(8,128)S(1)}, f32[384,512]{1,0:T(8,128)S(1)}) custom-call(f32[384,512]{1,0:T(8,128)S(1)} %bitcast.40, f32[384,512]{1,0:T(8,128)S(1)} %bitcast.39, bf16[4,512,512]{2,1,0:T(8,128)(2,1)S(1)} %copy-done.2), custom_call_target="tpu_custom_call" | custom-call | flops 10000000000 | bytes 1048576 | tf_op jit(solution)/shard_map/along_x/pallas_call | solution.py:133
  24.4 2.1 %collective-permute-done.11.rest_1_ = f32[3,8,512]{2,1,0:T(8,128)S(1)} collective-permute-done((f32[3,8,512]{2,1,0:T(8,128)S(1)}, f32[3,8,512]{2,1,0:T(8,128)S(1)}, u32[]{:S(2)}, u32[]{:S(2)}) %collective-permute-start.11) | collective-permute-done | bytes 49184 | tf_op jit(solution)/shard_map/ppermute | solution.py:369
  30.0 2.0 %collective-permute-start.18 = (f32[3,16,512]{2,1,0:T(8,128)S(1)}, f32[3,16,512]{2,1,0:T(8,128)S(1)}, u32[]{:S(2)}, u32[]{:S(2)}) collective-permute-start(f32[3,16,512]{2,1,0:T(8,128)S(1)} %get-tuple-element.124), channel_id=1, source_target_pairs={{0,3},{1,2},{2,5},{3,4},{4,7},{5,6},{6,1},{7,0},{8,11},{9,10},{10,... | collective-permute-start | bytes 294920 | tf_op jit(solution)/shard_map/ppermute | solution.py:369
  33.6 2.3 %along_x.9 = (f32[384,512]{1,0:T(8,128)S(1)}, f32[384,512]{1,0:T(8,128)}) custom-call(f32[384,512]{1,0:T(8,128)S(1)} %bitcast.44, f32[384,512]{1,0:T(8,128)S(1)} %bitcast.53, bf16[4,512,512]{2,1,0:T(8,128)(2,1)S(1)} %copy-done.2), custom_call_target="tpu_custom_call" | custom-call | flops 10000000000 | bytes 1048576 | tf_op jit(solution)/shard_map/along_x/pallas_call | solution.py:133
  35.9 1.4 %collective-permute-done.19.rest_1_ = f32[3,8,512]{2,1,0:T(8,128)S(1)} collective-permute-done((f32[3,8,512]{2,1,0:T(8,128)S(1)}, f32[3,8,512]{2,1,0:T(8,128)S(1)}, u32[]{:S(2)}, u32[]{:S(2)}) %collective-permute-start.19) | collective-permute-done | bytes 49184 | tf_op jit(solution)/shard_map/ppermute | solution.py:369
  40.0 4.0 %collective-permute-start.46 = (f32[3,128,512]{2,1,0:T(8,128)S(1)}, f32[3,128,512]{2,1,0:T(8,128)S(1)}, u32[]{:S(2)}, u32[]{:S(2)}) collective-permute-start(f32[3,128,512]{2,1,0:T(8,128)S(1)} %stage_lead.1), channel_id=1, source_target_pairs={{0,16},{8,24},{1,17},{9,25},{2,18},{10,26},{3,19},{11,27},{4,20},{... | collective-permute-start | bytes 2359304 | tf_op jit(solution)/shard_map/ppermute | solution.py:352
  44.5 1.4 %collective-permute-start.23 = (f32[3,16,512]{2,1,0:T(8,128)S(1)}, f32[3,16,512]{2,1,0:T(8,128)S(1)}, u32[]{:S(2)}, u32[]{:S(2)}) collective-permute-start(f32[3,16,512]{2,1,0:T(8,128)S(1)} %get-tuple-element.122), channel_id=1, source_target_pairs={{0,3},{1,2},{2,5},{3,4},{4,7},{5,6},{6,1},{7,0},{8,11},{9,10},{10,... | collective-permute-start | bytes 294920 | tf_op jit(solution)/shard_map/ppermute | solution.py:369
  45.9 1.3 %collective-permute-start.27 = (f32[3,16,512]{2,1,0:T(8,128)S(1)}, f32[3,16,512]{2,1,0:T(8,128)S(1)}, u32[]{:S(2)}, u32[]{:S(2)}) collective-permute-start(f32[3,16,512]{2,1,0:T(8,128)S(1)} %get-tuple-element.121), channel_id=1, source_target_pairs={{0,7},{1,6},{2,1},{3,0},{4,3},{5,2},{6,5},{7,4},{8,15},{9,14},{10,... | collective-permute-start | bytes 294920 | tf_op jit(solution)/shard_map/ppermute | solution.py:369
  47.2 1.3 %collective-permute-start.25 = (f32[3,8,512]{2,1,0:T(8,128)S(1)}, f32[3,8,512]{2,1,0:T(8,128)S(1)}, u32[]{:S(2)}, u32[]{:S(2)}) collective-permute-start(f32[3,8,512]{2,1,0:T(8,128)S(1)} %slice.182), channel_id=1, source_target_pairs={{0,5},{1,4},{2,7},{3,6},{4,1},{5,0},{6,3},{7,2},{8,13},{9,12},{10,... | collective-permute-start | bytes 147464 | tf_op jit(solution)/shard_map/ppermute | solution.py:369
  48.5 1.4 %along_x.10 = (f32[384,512]{1,0:T(8,128)S(1)}, f32[384,512]{1,0:T(8,128)S(1)}) custom-call(f32[384,512]{1,0:T(8,128)S(1)} %bitcast.46, f32[384,512]{1,0:T(8,128)S(1)} %bitcast.36, bf16[4,512,512]{2,1,0:T(8,128)(2,1)S(1)} %copy-done.2), custom_call_target="tpu_custom_call" | custom-call | flops 10000000000 | bytes 1048576 | tf_op jit(solution)/shard_map/along_x/pallas_call | solution.py:133
  49.9 1.5 %collective-permute-done.25.rest_1_ = f32[3,8,512]{2,1,0:T(8,128)S(1)} collective-permute-done((f32[3,8,512]{2,1,0:T(8,128)S(1)}, f32[3,8,512]{2,1,0:T(8,128)S(1)}, u32[]{:S(2)}, u32[]{:S(2)}) %collective-permute-start.25) | collective-permute-done | bytes 49184 | tf_op jit(solution)/shard_map/ppermute | solution.py:369
  55.2 1.4 %collective-permute-start.31 = (f32[3,16,512]{2,1,0:T(8,128)S(1)}, f32[3,16,512]{2,1,0:T(8,128)S(1)}, u32[]{:S(2)}, u32[]{:S(2)}) collective-permute-start(f32[3,16,512]{2,1,0:T(8,128)S(1)} %get-tuple-element.120), channel_id=1, source_target_pairs={{0,3},{1,2},{2,5},{3,4},{4,7},{5,6},{6,1},{7,0},{8,11},{9,10},{10,... | collective-permute-start | bytes 294920 | tf_op jit(solution)/shard_map/ppermute | solution.py:369
  58.8 1.4 %along_x.11 = (f32[384,512]{1,0:T(8,128)S(1)}, f32[384,512]{1,0:T(8,128)S(1)}) custom-call(f32[384,512]{1,0:T(8,128)S(1)} %bitcast.34, f32[384,512]{1,0:T(8,128)S(1)} %bitcast.35, bf16[4,512,512]{2,1,0:T(8,128)(2,1)S(1)} %copy-done.2), custom_call_target="tpu_custom_call" | custom-call | flops 10000000000 | bytes 1048576 | tf_op jit(solution)/shard_map/along_x/pallas_call | solution.py:133
  60.2 2.0 %collective-permute-done.33.rest_1_ = f32[3,8,512]{2,1,0:T(8,128)S(1)} collective-permute-done((f32[3,8,512]{2,1,0:T(8,128)S(1)}, f32[3,8,512]{2,1,0:T(8,128)S(1)}, u32[]{:S(2)}, u32[]{:S(2)}) %collective-permute-start.33) | collective-permute-done | bytes 49184 | tf_op jit(solution)/shard_map/ppermute | solution.py:369
  65.7 2.0 %collective-permute-start.39 = (f32[3,16,512]{2,1,0:T(8,128)S(1)}, f32[3,16,512]{2,1,0:T(8,128)S(1)}, u32[]{:S(2)}, u32[]{:S(2)}) collective-permute-start(f32[3,16,512]{2,1,0:T(8,128)S(1)} %get-tuple-element.118), channel_id=1, source_target_pairs={{0,3},{1,2},{2,5},{3,4},{4,7},{5,6},{6,1},{7,0},{8,11},{9,10},{10,... | collective-permute-start | bytes 294920 | tf_op jit(solution)/shard_map/ppermute | solution.py:369
  69.3 1.4 %along_x.12 = (f32[384,512]{1,0:T(8,128)S(1)}, f32[384,512]{1,0:T(8,128)S(1)}) custom-call(f32[384,512]{1,0:T(8,128)S(1)} %bitcast.38, f32[384,512]{1,0:T(8,128)S(1)} %bitcast.37, bf16[4,512,512]{2,1,0:T(8,128)(2,1)S(1)} %copy-done.2), custom_call_target="tpu_custom_call" | custom-call | flops 10000000000 | bytes 1048576 | tf_op jit(solution)/shard_map/along_x/pallas_call | solution.py:133
  70.7 2.3 %collective-permute-done.41.rest_1_ = f32[3,8,512]{2,1,0:T(8,128)S(1)} collective-permute-done((f32[3,8,512]{2,1,0:T(8,128)S(1)}, f32[3,8,512]{2,1,0:T(8,128)S(1)}, u32[]{:S(2)}, u32[]{:S(2)}) %collective-permute-start.41) | collective-permute-done | bytes 49184 | tf_op jit(solution)/shard_map/ppermute | solution.py:369
  75.7 1.9 %collective-permute-start.45 = (f32[3,128,512]{2,1,0:T(8,128)S(1)}, f32[3,128,512]{2,1,0:T(8,128)S(1)}, u32[]{:S(2)}, u32[]{:S(2)}) collective-permute-start(f32[3,128,512]{2,1,0:T(8,128)S(1)} %get-tuple-element.100), channel_id=1, source_target_pairs={{0,8},{8,16},{16,24},{1,9},{9,17},{17,25},{2,10},{10,18},{18,26},{... | collective-permute-start | bytes 2359304 | tf_op jit(solution)/shard_map/ppermute | solution.py:352
  79.0 17.3 %collective-permute-done.45.refs_0_ = f32[3,128,512]{2,1,0:T(8,128)S(1)} collective-permute-done((f32[3,128,512]{2,1,0:T(8,128)S(1)}, f32[3,128,512]{2,1,0:T(8,128)S(1)}, u32[]{:S(2)}, u32[]{:S(2)}) %collective-permute-start.45) | collective-permute-done | bytes 786464 | tf_op jit(solution)/shard_map/ppermute | solution.py:352
  96.8 3.0 %collective-permute-start.49 = (f32[3,16,512]{2,1,0:T(8,128)S(1)}, f32[3,16,512]{2,1,0:T(8,128)S(1)}, u32[]{:S(2)}, u32[]{:S(2)}) collective-permute-start(f32[3,16,512]{2,1,0:T(8,128)S(1)} %get-tuple-element.116), channel_id=1, source_target_pairs={{0,3},{1,2},{2,5},{3,4},{4,7},{5,6},{6,1},{7,0},{8,11},{9,10},{10,... | collective-permute-start | bytes 294920 | tf_op jit(solution)/shard_map/ppermute | solution.py:369
  99.8 1.5 %collective-permute-start.53 = (f32[3,16,512]{2,1,0:T(8,128)S(1)}, f32[3,16,512]{2,1,0:T(8,128)S(1)}, u32[]{:S(2)}, u32[]{:S(2)}) collective-permute-start(f32[3,16,512]{2,1,0:T(8,128)S(1)} %get-tuple-element.115), channel_id=1, source_target_pairs={{0,7},{1,6},{2,1},{3,0},{4,3},{5,2},{6,5},{7,4},{8,15},{9,14},{10,... | collective-permute-start | bytes 294920 | tf_op jit(solution)/shard_map/ppermute | solution.py:369
  101.7 1.4 %along_x.13 = (f32[384,512]{1,0:T(8,128)S(1)}, f32[384,512]{1,0:T(8,128)S(1)}) custom-call(f32[384,512]{1,0:T(8,128)S(1)} %bitcast.43, f32[384,512]{1,0:T(8,128)S(1)} %bitcast.41, bf16[4,512,512]{2,1,0:T(8,128)(2,1)S(1)} %copy-done.2), custom_call_target="tpu_custom_call" | custom-call | flops 10000000000 | bytes 1048576 | tf_op jit(solution)/shard_map/along_x/pallas_call | solution.py:133
  103.1 1.8 %collective-permute-done.51.rest_1_ = f32[3,8,512]{2,1,0:T(8,128)S(1)} collective-permute-done((f32[3,8,512]{2,1,0:T(8,128)S(1)}, f32[3,8,512]{2,1,0:T(8,128)S(1)}, u32[]{:S(2)}, u32[]{:S(2)}) %collective-permute-start.51) | collective-permute-done | bytes 49184 | tf_op jit(solution)/shard_map/ppermute | solution.py:369
  106.7 1.5 %stage_join.1 = f32[3,128,1024]{2,1,0:T(8,128)} custom-call(f32[3,128,512]{2,1,0:T(8,128)S(1)} %get-tuple-element.102.state_ref, f32[3,128,512]{2,1,0:T(8,128)S(1)} %bitcast.52, f32[128,1]{1,0:T(8,128)S(1)} %get-tuple-element.64.turning_ref, f32[3,16,512]{2,1,0:T(8,128)S(1)} %collective-permute-done.50.rest_0_, ...), custom_call_target="tpu_custom_call" | custom-call | flops 10000000000 | bytes 1048576 | tf_op jit(solution)/shard_map/stage_join/pallas_call | solution.py:133
  (139 shorter events, 35.5 us)
Async XLA Ops:
  0.0 38.3 %collective-permute-start = (f32[3,128,1024]{2,1,0:T(8,128)}, f32[3,128,1024]{2,1,0:T(8,128)S(1)}, u32[]{:S(2)}, u32[]{:S(2)}) collective-permute-start(f32[3,128,1024]{2,1,0:T(8,128)} %bitcast.30), channel_id=1, source_target_pairs={{0,8},{8,16},{16,24},{1,9},{9,17},{17,25},{2,10},{10,18},{18,26},{... | collective-permute-start | bytes 4718600 | tf_op jit(solution)/shard_map/ppermute | solution.py:352
  7.5 9.2 %collective-permute-start.5 = (f32[3,16,512]{2,1,0:T(8,128)S(1)}, f32[3,16,512]{2,1,0:T(8,128)S(1)}, u32[]{:S(2)}, u32[]{:S(2)}) collective-permute-start(f32[3,16,512]{2,1,0:T(8,128)S(1)} %slice.131), channel_id=1, source_target_pairs={{0,1},{1,0},{2,3},{3,2},{4,5},{5,4},{6,7},{7,6},{8,9},{9,8},{10,11... | collective-permute-start | bytes 294920 | tf_op jit(solution)/shard_map/ppermute | solution.py:357
  8.4 7.3 %collective-permute-start.2 = (f32[3,16,512]{2,1,0:T(8,128)S(1)}, f32[3,16,512]{2,1,0:T(8,128)S(1)}, u32[]{:S(2)}, u32[]{:S(2)}) collective-permute-start(f32[3,16,512]{2,1,0:T(8,128)S(1)} %get-tuple-element.128), channel_id=1, source_target_pairs={{0,3},{1,2},{2,5},{3,4},{4,7},{5,6},{6,1},{7,0},{8,11},{9,10},{10,... | collective-permute-start | bytes 294920 | tf_op jit(solution)/shard_map/ppermute | solution.py:369
  9.9 6.7 %collective-permute-start.4 = (f32[3,16,512]{2,1,0:T(8,128)S(1)}, f32[3,16,512]{2,1,0:T(8,128)S(1)}, u32[]{:S(2)}, u32[]{:S(2)}) collective-permute-start(f32[3,16,512]{2,1,0:T(8,128)S(1)} %get-tuple-element.127), channel_id=1, source_target_pairs={{0,7},{1,6},{2,1},{3,0},{4,3},{5,2},{6,5},{7,4},{8,15},{9,14},{10,... | collective-permute-start | bytes 294920 | tf_op jit(solution)/shard_map/ppermute | solution.py:369
  11.1 4.4 %collective-permute-start.3 = (f32[3,8,512]{2,1,0:T(8,128)S(1)}, f32[3,8,512]{2,1,0:T(8,128)S(1)}, u32[]{:S(2)}, u32[]{:S(2)}) collective-permute-start(f32[3,8,512]{2,1,0:T(8,128)S(1)} %slice.170), channel_id=1, source_target_pairs={{0,5},{1,4},{2,7},{3,6},{4,1},{5,0},{6,3},{7,2},{8,13},{9,12},{10,... | collective-permute-start | bytes 147464 | tf_op jit(solution)/shard_map/ppermute | solution.py:369
  19.0 8.2 %collective-permute-start.13 = (f32[3,16,512]{2,1,0:T(8,128)S(1)}, f32[3,16,512]{2,1,0:T(8,128)S(1)}, u32[]{:S(2)}, u32[]{:S(2)}) collective-permute-start(f32[3,16,512]{2,1,0:T(8,128)S(1)} %slice.137), channel_id=1, source_target_pairs={{0,1},{1,0},{2,3},{3,2},{4,5},{5,4},{6,7},{7,6},{8,9},{9,8},{10,11... | collective-permute-start | bytes 294920 | tf_op jit(solution)/shard_map/ppermute | solution.py:357
  19.4 7.3 %collective-permute-start.10 = (f32[3,16,512]{2,1,0:T(8,128)S(1)}, f32[3,16,512]{2,1,0:T(8,128)S(1)}, u32[]{:S(2)}, u32[]{:S(2)}) collective-permute-start(f32[3,16,512]{2,1,0:T(8,128)S(1)} %get-tuple-element.126), channel_id=1, source_target_pairs={{0,3},{1,2},{2,5},{3,4},{4,7},{5,6},{6,1},{7,0},{8,11},{9,10},{10,... | collective-permute-start | bytes 294920 | tf_op jit(solution)/shard_map/ppermute | solution.py:369
  20.7 6.4 %collective-permute-start.12 = (f32[3,16,512]{2,1,0:T(8,128)S(1)}, f32[3,16,512]{2,1,0:T(8,128)S(1)}, u32[]{:S(2)}, u32[]{:S(2)}) collective-permute-start(f32[3,16,512]{2,1,0:T(8,128)S(1)} %get-tuple-element.125), channel_id=1, source_target_pairs={{0,7},{1,6},{2,1},{3,0},{4,3},{5,2},{6,5},{7,4},{8,15},{9,14},{10,... | collective-permute-start | bytes 294920 | tf_op jit(solution)/shard_map/ppermute | solution.py:369
  22.2 4.3 %collective-permute-start.11 = (f32[3,8,512]{2,1,0:T(8,128)S(1)}, f32[3,8,512]{2,1,0:T(8,128)S(1)}, u32[]{:S(2)}, u32[]{:S(2)}) collective-permute-start(f32[3,8,512]{2,1,0:T(8,128)S(1)} %slice.174), channel_id=1, source_target_pairs={{0,5},{1,4},{2,7},{3,6},{4,1},{5,0},{6,3},{7,2},{8,13},{9,12},{10,... | collective-permute-start | bytes 147464 | tf_op jit(solution)/shard_map/ppermute | solution.py:369
  29.5 6.5 %collective-permute-start.21 = (f32[3,16,512]{2,1,0:T(8,128)S(1)}, f32[3,16,512]{2,1,0:T(8,128)S(1)}, u32[]{:S(2)}, u32[]{:S(2)}) collective-permute-start(f32[3,16,512]{2,1,0:T(8,128)S(1)} %slice.143), channel_id=1, source_target_pairs={{0,1},{1,0},{2,3},{3,2},{4,5},{5,4},{6,7},{7,6},{8,9},{9,8},{10,11... | collective-permute-start | bytes 294920 | tf_op jit(solution)/shard_map/ppermute | solution.py:357
  30.0 7.3 %collective-permute-start.18 = (f32[3,16,512]{2,1,0:T(8,128)S(1)}, f32[3,16,512]{2,1,0:T(8,128)S(1)}, u32[]{:S(2)}, u32[]{:S(2)}) collective-permute-start(f32[3,16,512]{2,1,0:T(8,128)S(1)} %get-tuple-element.124), channel_id=1, source_target_pairs={{0,3},{1,2},{2,5},{3,4},{4,7},{5,6},{6,1},{7,0},{8,11},{9,10},{10,... | collective-permute-start | bytes 294920 | tf_op jit(solution)/shard_map/ppermute | solution.py:369
  32.0 5.7 %collective-permute-start.20 = (f32[3,16,512]{2,1,0:T(8,128)S(1)}, f32[3,16,512]{2,1,0:T(8,128)S(1)}, u32[]{:S(2)}, u32[]{:S(2)}) collective-permute-start(f32[3,16,512]{2,1,0:T(8,128)S(1)} %get-tuple-element.123), channel_id=1, source_target_pairs={{0,7},{1,6},{2,1},{3,0},{4,3},{5,2},{6,5},{7,4},{8,15},{9,14},{10,... | collective-permute-start | bytes 294920 | tf_op jit(solution)/shard_map/ppermute | solution.py:369
  33.2 4.1 %collective-permute-start.19 = (f32[3,8,512]{2,1,0:T(8,128)S(1)}, f32[3,8,512]{2,1,0:T(8,128)S(1)}, u32[]{:S(2)}, u32[]{:S(2)}) collective-permute-start(f32[3,8,512]{2,1,0:T(8,128)S(1)} %slice.178), channel_id=1, source_target_pairs={{0,5},{1,4},{2,7},{3,6},{4,1},{5,0},{6,3},{7,2},{8,13},{9,12},{10,... | collective-permute-start | bytes 147464 | tf_op jit(solution)/shard_map/ppermute | solution.py:369
  39.9 4.6 %collective-permute-start.22 = (f32[3,56,512]{2,1,0:T(8,128)S(1)}, f32[3,56,512]{2,1,0:T(8,128)S(1)}, u32[]{:S(2)}, u32[]{:S(2)}) collective-permute-start(f32[3,56,512]{2,1,0:T(8,128)S(1)} %get-tuple-element.85), channel_id=1, source_target_pairs={{0,1},{1,0},{2,3},{3,2},{4,5},{5,4},{6,7},{7,6},{8,9},{9,8},{10,11... | collective-permute-start | bytes 1032200 | tf_op jit(solution)/shard_map/ppermute | solution.py:357
  40.0 38.0 %collective-permute-start.46 = (f32[3,128,512]{2,1,0:T(8,128)S(1)}, f32[3,128,512]{2,1,0:T(8,128)S(1)}, u32[]{:S(2)}, u32[]{:S(2)}) collective-permute-start(f32[3,128,512]{2,1,0:T(8,128)S(1)} %stage_lead.1), channel_id=1, source_target_pairs={{0,16},{8,24},{1,17},{9,25},{2,18},{10,26},{3,19},{11,27},{4,20},{... | collective-permute-start | bytes 2359304 | tf_op jit(solution)/shard_map/ppermute | solution.py:352
  44.1 8.5 %collective-permute-start.29 = (f32[3,16,512]{2,1,0:T(8,128)S(1)}, f32[3,16,512]{2,1,0:T(8,128)S(1)}, u32[]{:S(2)}, u32[]{:S(2)}) collective-permute-start(f32[3,16,512]{2,1,0:T(8,128)S(1)} %slice.149), channel_id=1, source_target_pairs={{0,1},{1,0},{2,3},{3,2},{4,5},{5,4},{6,7},{7,6},{8,9},{9,8},{10,11... | collective-permute-start | bytes 294920 | tf_op jit(solution)/shard_map/ppermute | solution.py:357
  44.5 7.1 %collective-permute-start.23 = (f32[3,16,512]{2,1,0:T(8,128)S(1)}, f32[3,16,512]{2,1,0:T(8,128)S(1)}, u32[]{:S(2)}, u32[]{:S(2)}) collective-permute-start(f32[3,16,512]{2,1,0:T(8,128)S(1)} %get-tuple-element.122), channel_id=1, source_target_pairs={{0,3},{1,2},{2,5},{3,4},{4,7},{5,6},{6,1},{7,0},{8,11},{9,10},{10,... | collective-permute-start | bytes 294920 | tf_op jit(solution)/shard_map/ppermute | solution.py:369
  45.9 6.4 %collective-permute-start.27 = (f32[3,16,512]{2,1,0:T(8,128)S(1)}, f32[3,16,512]{2,1,0:T(8,128)S(1)}, u32[]{:S(2)}, u32[]{:S(2)}) collective-permute-start(f32[3,16,512]{2,1,0:T(8,128)S(1)} %get-tuple-element.121), channel_id=1, source_target_pairs={{0,7},{1,6},{2,1},{3,0},{4,3},{5,2},{6,5},{7,4},{8,15},{9,14},{10,... | collective-permute-start | bytes 294920 | tf_op jit(solution)/shard_map/ppermute | solution.py:369
  47.2 4.2 %collective-permute-start.25 = (f32[3,8,512]{2,1,0:T(8,128)S(1)}, f32[3,8,512]{2,1,0:T(8,128)S(1)}, u32[]{:S(2)}, u32[]{:S(2)}) collective-permute-start(f32[3,8,512]{2,1,0:T(8,128)S(1)} %slice.182), channel_id=1, source_target_pairs={{0,5},{1,4},{2,7},{3,6},{4,1},{5,0},{6,3},{7,2},{8,13},{9,12},{10,... | collective-permute-start | bytes 147464 | tf_op jit(solution)/shard_map/ppermute | solution.py:369
  54.7 8.3 %collective-permute-start.37 = (f32[3,16,512]{2,1,0:T(8,128)S(1)}, f32[3,16,512]{2,1,0:T(8,128)S(1)}, u32[]{:S(2)}, u32[]{:S(2)}) collective-permute-start(f32[3,16,512]{2,1,0:T(8,128)S(1)} %slice.155), channel_id=1, source_target_pairs={{0,1},{1,0},{2,3},{3,2},{4,5},{5,4},{6,7},{7,6},{8,9},{9,8},{10,11... | collective-permute-start | bytes 294920 | tf_op jit(solution)/shard_map/ppermute | solution.py:357
  55.2 7.2 %collective-permute-start.31 = (f32[3,16,512]{2,1,0:T(8,128)S(1)}, f32[3,16,512]{2,1,0:T(8,128)S(1)}, u32[]{:S(2)}, u32[]{:S(2)}) collective-permute-start(f32[3,16,512]{2,1,0:T(8,128)S(1)} %get-tuple-element.120), channel_id=1, source_target_pairs={{0,3},{1,2},{2,5},{3,4},{4,7},{5,6},{6,1},{7,0},{8,11},{9,10},{10,... | collective-permute-start | bytes 294920 | tf_op jit(solution)/shard_map/ppermute | solution.py:369
  56.6 6.1 %collective-permute-start.35 = (f32[3,16,512]{2,1,0:T(8,128)S(1)}, f32[3,16,512]{2,1,0:T(8,128)S(1)}, u32[]{:S(2)}, u32[]{:S(2)}) collective-permute-start(f32[3,16,512]{2,1,0:T(8,128)S(1)} %get-tuple-element.119), channel_id=1, source_target_pairs={{0,7},{1,6},{2,1},{3,0},{4,3},{5,2},{6,5},{7,4},{8,15},{9,14},{10,... | collective-permute-start | bytes 294920 | tf_op jit(solution)/shard_map/ppermute | solution.py:369
  57.9 4.3 %collective-permute-start.33 = (f32[3,8,512]{2,1,0:T(8,128)S(1)}, f32[3,8,512]{2,1,0:T(8,128)S(1)}, u32[]{:S(2)}, u32[]{:S(2)}) collective-permute-start(f32[3,8,512]{2,1,0:T(8,128)S(1)} %slice.186), channel_id=1, source_target_pairs={{0,5},{1,4},{2,7},{3,6},{4,1},{5,0},{6,3},{7,2},{8,13},{9,12},{10,... | collective-permute-start | bytes 147464 | tf_op jit(solution)/shard_map/ppermute | solution.py:369
  65.2 8.6 %collective-permute-start.47 = (f32[3,16,512]{2,1,0:T(8,128)S(1)}, f32[3,16,512]{2,1,0:T(8,128)S(1)}, u32[]{:S(2)}, u32[]{:S(2)}) collective-permute-start(f32[3,16,512]{2,1,0:T(8,128)S(1)} %slice.161), channel_id=1, source_target_pairs={{0,1},{1,0},{2,3},{3,2},{4,5},{5,4},{6,7},{7,6},{8,9},{9,8},{10,11... | collective-permute-start | bytes 294920 | tf_op jit(solution)/shard_map/ppermute | solution.py:357
  65.7 7.6 %collective-permute-start.39 = (f32[3,16,512]{2,1,0:T(8,128)S(1)}, f32[3,16,512]{2,1,0:T(8,128)S(1)}, u32[]{:S(2)}, u32[]{:S(2)}) collective-permute-start(f32[3,16,512]{2,1,0:T(8,128)S(1)} %get-tuple-element.118), channel_id=1, source_target_pairs={{0,3},{1,2},{2,5},{3,4},{4,7},{5,6},{6,1},{7,0},{8,11},{9,10},{10,... | collective-permute-start | bytes 294920 | tf_op jit(solution)/shard_map/ppermute | solution.py:369
  67.7 5.9 %collective-permute-start.43 = (f32[3,16,512]{2,1,0:T(8,128)S(1)}, f32[3,16,512]{2,1,0:T(8,128)S(1)}, u32[]{:S(2)}, u32[]{:S(2)}) collective-permute-start(f32[3,16,512]{2,1,0:T(8,128)S(1)} %get-tuple-element.117), channel_id=1, source_target_pairs={{0,7},{1,6},{2,1},{3,0},{4,3},{5,2},{6,5},{7,4},{8,15},{9,14},{10,... | collective-permute-start | bytes 294920 | tf_op jit(solution)/shard_map/ppermute | solution.py:369
  68.8 4.2 %collective-permute-start.41 = (f32[3,8,512]{2,1,0:T(8,128)S(1)}, f32[3,8,512]{2,1,0:T(8,128)S(1)}, u32[]{:S(2)}, u32[]{:S(2)}) collective-permute-start(f32[3,8,512]{2,1,0:T(8,128)S(1)} %slice.190), channel_id=1, source_target_pairs={{0,5},{1,4},{2,7},{3,6},{4,1},{5,0},{6,3},{7,2},{8,13},{9,12},{10,... | collective-permute-start | bytes 147464 | tf_op jit(solution)/shard_map/ppermute | solution.py:369
  75.7 20.7 %collective-permute-start.45 = (f32[3,128,512]{2,1,0:T(8,128)S(1)}, f32[3,128,512]{2,1,0:T(8,128)S(1)}, u32[]{:S(2)}, u32[]{:S(2)}) collective-permute-start(f32[3,128,512]{2,1,0:T(8,128)S(1)} %get-tuple-element.100), channel_id=1, source_target_pairs={{0,8},{8,16},{16,24},{1,9},{9,17},{17,25},{2,10},{10,18},{18,26},{... | collective-permute-start | bytes 2359304 | tf_op jit(solution)/shard_map/ppermute | solution.py:352
  78.4 18.4 %collective-permute-start.48 = (f32[3,56,512]{2,1,0:T(8,128)S(1)}, f32[3,56,512]{2,1,0:T(8,128)S(1)}, u32[]{:S(2)}, u32[]{:S(2)}) collective-permute-start(f32[3,56,512]{2,1,0:T(8,128)S(1)} %get-tuple-element.111), channel_id=1, source_target_pairs={{0,1},{1,0},{2,3},{3,2},{4,5},{5,4},{6,7},{7,6},{8,9},{9,8},{10,11... | collective-permute-start | bytes 1032200 | tf_op jit(solution)/shard_map/ppermute | solution.py:357
  96.8 8.1 %collective-permute-start.49 = (f32[3,16,512]{2,1,0:T(8,128)S(1)}, f32[3,16,512]{2,1,0:T(8,128)S(1)}, u32[]{:S(2)}, u32[]{:S(2)}) collective-permute-start(f32[3,16,512]{2,1,0:T(8,128)S(1)} %get-tuple-element.116), channel_id=1, source_target_pairs={{0,3},{1,2},{2,5},{3,4},{4,7},{5,6},{6,1},{7,0},{8,11},{9,10},{10,... | collective-permute-start | bytes 294920 | tf_op jit(solution)/shard_map/ppermute | solution.py:369
  99.8 5.6 %collective-permute-start.53 = (f32[3,16,512]{2,1,0:T(8,128)S(1)}, f32[3,16,512]{2,1,0:T(8,128)S(1)}, u32[]{:S(2)}, u32[]{:S(2)}) collective-permute-start(f32[3,16,512]{2,1,0:T(8,128)S(1)} %get-tuple-element.115), channel_id=1, source_target_pairs={{0,7},{1,6},{2,1},{3,0},{4,3},{5,2},{6,5},{7,4},{8,15},{9,14},{10,... | collective-permute-start | bytes 294920 | tf_op jit(solution)/shard_map/ppermute | solution.py:369
  101.3 4.2 %collective-permute-start.55 = (f32[3,16,512]{2,1,0:T(8,128)S(1)}, f32[3,16,512]{2,1,0:T(8,128)S(1)}, u32[]{:S(2)}, u32[]{:S(2)}) collective-permute-start(f32[3,16,512]{2,1,0:T(8,128)S(1)} %slice.167), channel_id=1, source_target_pairs={{0,1},{1,0},{2,3},{3,2},{4,5},{5,4},{6,7},{7,6},{8,9},{9,8},{10,11... | collective-permute-start | bytes 294920 | tf_op jit(solution)/shard_map/ppermute | solution.py:357
  (27 other events, 52.8 us)
